TPU v7x, 32 devices: a whole 2x2x4 slice. The times are simulated.
32 devices in a mesh: ens: 2 (over x), along: 16 (over z, y, core).
Axes of the slice: x: 2, y: 2, z: 4, core: 2. Of those that a mesh axis runs over, the one named last changes fastest.
Arguments:
- basic_state: float32 [40, 512, 1024], P(None, ('ens', 'along')), parts along dimension 1, may hold values from -4 to 4
- land_sea: int32 [512, 1024], P(('ens', 'along')), parts along dimension 0, may hold values 0 or 1
- obs_cells: int32 [32, 3, 512], P(('ens', 'along')), parts along dimension 0, may hold values from 0 to 655359
- obs_count: int32 [32, 3], P(('ens', 'along')), parts along dimension 0, may hold values from 1 to 512, as said below
- obs_value: float32 [32, 3, 512], P(('ens', 'along')), parts along dimension 0, may hold values from -12 to 12
Outputs:
- gradient: float32 [40, 512, 1024], P(None, ('ens', 'along')), parts along dimension 1
- misfit: float32 [2], P('ens'), parts along dimension 0
There are 2 independent parts, one for each index of `ens`. A program takes and returns all parts, laid end to end along the dimension named above; each array names one. Nothing has to cross between parts.
Inputs may be any that keep to these rules, and one draw needn't show every extreme that they name: `obs_cells`: each entry is a cell of the tile's own block, flattened as (level * 16 + row) * 1024 + column; cells may repeat; slots from obs_count on are unused. Slots 0 .. obs_count - 1 of a tile's list at a time are live; in every draw some tile is full at some time.
All inputs are finite; a program needn't handle non-finite values. No bound on the sum of `land_sea` on one device may be relied on, other than what follows from the above.
Results may differ from a plain program's by a relative error of at most 0.0001.
Values sent between devices are 32-bit elements; how exact they have to be, the bound alone decides.
No kernel may reach another device: no remote copies, remote signals or barrier semaphores. Data moves between devices by JAX's collectives and lax.ppermute only.
A program may use at most 128 MiB of HBM per device.

v0:
```python
import functools

import jax
import jax.numpy as jnp
from jax import lax
from jax.experimental import pallas as pl
from jax.experimental.pallas import tpu as pltpu
from jax.sharding import PartitionSpec as P

F32 = jnp.float32
I32 = jnp.int32
ROWS, CT, LV, LN = 16, 8, 40, 128
H = 3
RX = ROWS + 2 * H
COL = CT * LV
EDGE = H * COL + H * CT + 16
CAP = 512
NT = 3
PAY = 16

VM = pl.BlockSpec(memory_space=pltpu.VMEM)
SM = pl.BlockSpec(memory_space=pltpu.SMEM)
HBM = pl.BlockSpec(memory_space=pltpu.MemorySpace.HBM)
ANY = pl.BlockSpec(memory_space=pl.ANY)
FIELD = jax.ShapeDtypeStruct((RX * COL, LN), F32)
MASK = jax.ShapeDtypeStruct((RX * CT, LN), F32)


def params(mib):
    return pltpu.CompilerParams(vmem_limit_bytes=mib << 20)


def cost(us):
    return pl.CostEstimate(flops=0, bytes_accessed=int(us * 3.0e6), transcendentals=0)


def lanes():
    return lax.broadcasted_iota(I32, (8, LN), 1)


def sublanes():
    return lax.broadcasted_iota(I32, (8, LN), 0)


def stencil_row(src, at, emit):
    lane, sub = lanes(), sublanes()
    first, last = lane == 0, lane == LN - 1
    low, high = sub == 0, sub == 7
    base = pl.multiple_of(at * COL, COL)
    for k in range(LV // 8):
        offs = [base + c * LV + k * 8 for c in range(CT)]
        mids = [src[pl.ds(pl.multiple_of(o, 8), 8), :] for o in offs]
        fwd = [pltpu.roll(v, 1, 1) for v in mids]
        bwd = [pltpu.roll(v, LN - 1, 1) for v in mids]
        for c in range(CT):
            v, o = mids[c], offs[c]
            west = jnp.where(first, fwd[c - 1] if c > 0 else 0.0, fwd[c])
            east = jnp.where(last, bwd[c + 1] if c < CT - 1 else 0.0, bwd[c])
            north = src[pl.ds(pl.multiple_of(o - COL, 8), 8), :]
            south = src[pl.ds(pl.multiple_of(o + COL, 8), 8), :]
            if k > 0:
                down = src[pl.ds(o - 1, 8), :]
            else:
                down = jnp.where(low, v, pltpu.roll(v, 1, 0))
            if k < LV // 8 - 1:
                up = src[pl.ds(o + 1, 8), :]
            else:
                up = jnp.where(high, v, pltpu.roll(v, 7, 0))
            s = ((north + south) + (west + east)) + 0.2 * (down + up)
            emit(c, k, v, s, o)


def mask_row(mask, at, c):
    return mask[pl.ds(at * CT + c, 8, stride=0), :]


def forward_row(src, dst, mask, at):
    ms = [mask_row(mask, at, c) for c in range(CT)]

    def emit(c, k, v, s, o):
        dst[pl.ds(pl.multiple_of(o, 8), 8), :] = ms[c] * (s + v * (0.6 - v * v))

    stencil_row(src, at, emit)


def adjoint_row(src, state, forcing, mask, at):
    ms = [mask_row(mask, at, c) for c in range(CT)]

    def emit(c, k, g, s, o):
        spot = pl.ds(pl.multiple_of(o, 8), 8)
        y = state[spot, :]
        forcing[spot, :] = ms[c] * (s + g * (0.6 - 3.0 * (y * y)) + forcing[spot, :])

    stencil_row(src, at, emit)


def gradient_row(src, state, out, at):
    def emit(c, k, g, s, o):
        y = state[pl.ds(pl.multiple_of(o, 8), 8), :]
        out[pl.ds(pl.multiple_of(o - H * COL, 8), 8), :] = 0.2 * (s + g * (0.6 - 3.0 * (y * y)))

    stencil_row(src, at, emit)


def loop(first, last, body):
    lax.fori_loop(first + H, last + H + 1, lambda at, _: (body(at), 0)[1], 0)


def column(ref, out, at):
    col = ref[at] & (CT * LN - 1)
    sub = lax.broadcasted_iota(I32, (16, CAP), 0)

    def part(i, _):
        out[pl.ds(pl.multiple_of(i * 16, 16), 16), :] = jnp.where(col == sub + i * 16, 1.0, 0.0).astype(jnp.bfloat16)
        return 0

    lax.fori_loop(0, CT * LN // 16, part, 0, unroll=2)


def split(d):
    high = d.astype(jnp.bfloat16).astype(F32)
    return high, d - high


def spread(line, terms, left, first, count):
    high, low = split(terms)
    sub = lax.broadcasted_iota(I32, (16, CAP), 0)
    for i in range(count // 16):
        hit = line == sub + i * 16
        where = pl.ds(first + i * 16, 16)
        left[where, pl.ds(0, CAP)] = jnp.where(hit, high, 0.0).astype(jnp.bfloat16)
        left[where, pl.ds(CAP, CAP)] = jnp.where(hit, low, 0.0).astype(jnp.bfloat16)


def product(left, rows, cols):
    dims = (((1,), (1,)), ((), ()))
    return lax.dot_general(left[pl.ds(0, rows), pl.ds(0, CAP)], cols, dims, preferred_element_type=F32) + lax.dot_general(
        left[pl.ds(0, rows), pl.ds(CAP, CAP)], cols, dims, preferred_element_type=F32
    )


def edges_kernel(basic, land, cells, staged, up, down, mask, sems):
    def copy(c):
        return pltpu.make_async_copy(basic.at[:, :, pl.ds(c * LN, LN)], staged.at[c], sems.at[c])

    for c in range(CT):
        copy(c).start()
    for c in range(CT):
        mask[pl.ds(H * CT + c, ROWS, stride=CT), :] = 0.2 * land[:, pl.ds(c * LN, LN)].astype(F32)
    for t in range(NT):
        for q in range(CAP // LN):
            row = cells[t, :, pl.ds(q * LN, LN)].astype(F32)
            for out in (up, down):
                out[pl.ds(H * COL + H * CT + t * 4 + q, 1), :] = row
    for c in range(CT):
        copy(c).wait()
        flat = staged.at[c].reshape(LV * ROWS, LN)
        for out, first in ((up, 0), (down, ROWS - H)):
            for j in range(H):
                r = first + j
                half = 2.5 * mask_row(mask, r + H, c)
                for k in range(LV // 8):
                    v = flat[pl.ds(k * 8 * ROWS + r, 8, stride=ROWS), :]
                    out[pl.ds((j * CT + c) * LV + k * 8, 8), :] = half * v
                out[pl.ds(H * COL + j * CT + c, 1), :] = mask[pl.ds((r + H) * CT + c, 1), :]


def edges(basic, land, cells):
    return pl.pallas_call(
        edges_kernel,
        out_shape=[
            jax.ShapeDtypeStruct((CT, LV, ROWS, LN), F32),
            jax.ShapeDtypeStruct((EDGE, LN), F32),
            jax.ShapeDtypeStruct((EDGE, LN), F32),
            MASK,
        ],
        in_specs=[HBM, VM, VM],
        out_specs=[VM] * 4,
        scratch_shapes=[pltpu.SemaphoreType.DMA((CT,))],
        compiler_params=params(4),
        cost_estimate=cost(2),
        name="edges",
    )(basic, land, cells)


def interior_kernel(staged, mask, cells, y0, y1, y2, y3, cols):
    for c in range(CT):
        flat = staged.at[c].reshape(LV * ROWS, LN)

        def turn(r, _):
            half = 2.5 * mask_row(mask, r + H, c)
            for k in range(LV // 8):
                v = flat[pl.ds(k * 8 * ROWS + r, 8, stride=ROWS), :]
                y0[pl.ds(pl.multiple_of((r + H) * COL + c * LV + k * 8, 8), 8), :] = half * v
            return 0

        lax.fori_loop(0, ROWS, turn, 0)

    zero = jnp.zeros((8, LN), F32)
    for at in (H - 2, ROWS + H + 1):
        for j in range(COL // 8):
            y2[pl.ds(at * COL + j * 8, 8), :] = zero
    loop(1, 14, lambda at: forward_row(y0, y1, mask, at))
    loop(2, 13, lambda at: forward_row(y1, y2, mask, at))
    loop(3, 12, lambda at: forward_row(y2, y3, mask, at))
    for t in range(NT):
        column(cells, cols.at[t], t)


def interior(staged, mask, cells):
    return pl.pallas_call(
        interior_kernel,
        out_shape=[FIELD] * 4 + [jax.ShapeDtypeStruct((NT, CT * LN, CAP), jnp.bfloat16)],
        in_specs=[VM] * 3,
        out_specs=[VM] * 5,
        compiler_params=params(8),
        cost_estimate=cost(9),
        name="interior",
    )(staged, mask, cells)


def bands_kernel(y0i, y1i, y2i, y3i, maski, cells, count, value, spots, above, below,
                 y0, y1, y2, mask, total, pay, terms, g1, g2, g3, g4, at_ref, sem):
    fetch = pltpu.make_async_copy(spots, at_ref, sem)
    fetch.start()
    y3 = y3i
    for halo, first in ((above, 0), (below, ROWS + H)):
        for j in range(H):
            base = (first + j) * COL
            for q in range(COL // 8):
                y0[pl.ds(base + q * 8, 8), :] = halo[pl.ds(j * COL + q * 8, 8), :]
            mask[pl.ds((first + j) * CT, CT), :] = halo[pl.ds(H * COL + j * CT, CT), :]
    for src, dst, reach in ((y0, y1, 2), (y1, y2, 1), (y2, y3, 0)):
        loop(-reach, 2 - reach, lambda at: forward_row(src, dst, mask, at))
        loop(ROWS - 3 + reach, ROWS - 1 + reach, lambda at: forward_row(src, dst, mask, at))
    fetch.wait()
    many = 8

    def group(i, _):
        for u in range(many):
            s = i * many + u
            third = at_ref[2 * CAP + s]
            g1[pl.ds(s, 1), :] = y1[pl.ds(at_ref[s], 1), :]
            g2[pl.ds(s, 1), :] = y2[pl.ds(at_ref[CAP + s], 1), :]
            g3[pl.ds(s, 1), :] = y3[pl.ds(third, 1), :]
            g4[pl.ds(s, 1), :] = y2[pl.ds(third, 1), :]
        return 0

    lax.fori_loop(0, CAP // many, group, 0)
    sub = lax.broadcasted_iota(I32, (LN, LN), 0)
    slot = lax.broadcasted_iota(I32, (1, LN), 1)
    acc = jnp.zeros((1, LN), F32)
    for t, g in enumerate((g1, g2, g3)):
        for q in range(CAP // LN):
            part = pl.ds(q * LN, LN)
            hit = (cells[t, :, part] & (LN - 1)) == sub
            x = jnp.sum(jnp.where(hit, g[part, :].T, 0.0), axis=0, keepdims=True)
            live = slot + q * LN < count[0, t]
            d = jnp.where(live, 2.0 * x - value[t, :, part], 0.0)
            acc = acc + d * d
            pay[pl.ds(4 * t + q, 1), :] = d
            terms[pl.ds(t, 1), part] = d
            if t == NT - 1:
                z = jnp.sum(jnp.where(hit, g4[part, :].T, 0.0), axis=0, keepdims=True)
                pay[pl.ds(12 + q, 1), :] = -3.0 * (z * z) * d
    total[...] = jnp.where(sublanes() == 0, jnp.broadcast_to(acc, (8, LN)), 0.0)


def bands(y0, y1, y2, y3, mask, cells, count, value, spots, above, below):
    rows = pltpu.VMEM((CAP, LN), F32)
    return pl.pallas_call(
        bands_kernel,
        out_shape=[FIELD] * 3
        + [MASK, jax.ShapeDtypeStruct((8, LN), F32), jax.ShapeDtypeStruct((PAY, LN), F32), jax.ShapeDtypeStruct((8, CAP), F32)],
        in_specs=[VM] * 6 + [SM, VM, ANY] + [VM] * 2,
        out_specs=[VM] * 7,
        input_output_aliases={0: 0, 1: 1, 2: 2, 4: 3},
        scratch_shapes=[rows, rows, rows, rows, pltpu.SMEM((NT * CAP,), I32), pltpu.SemaphoreType.DMA],
        compiler_params=params(8),
        cost_estimate=cost(5),
        name="bands",
    )(y0, y1, y2, y3, mask, cells, count, value, spots, above, below)


def inner_adjoint_kernel(y0, y1, y2, mask, cells, terms, cols, above, below, f1, f2, f3, grad, far, left):
    for t, (f, scale) in enumerate(((f1, 25.0), (f2, 25.0), (f3, 5.0))):
        cell = cells[t]
        line = ((cell >> 10) & (ROWS - 1)) * LV + (cell >> 14)
        spread(line, terms[pl.ds(t, 1), :], left, 0, ROWS * LV)

        def block(p, _):
            out = product(left, ROWS * LV, cols[t, pl.ds(pl.multiple_of(p * 2 * LN, 2 * LN), 2 * LN), :])
            for r in range(ROWS):
                for j in range(2):
                    c = 2 * p + j
                    m = scale * mask_row(mask, r + H, c)
                    for k in range(LV // 8):
                        spot = pl.ds(pl.multiple_of((r + H) * COL + c * LV + k * 8, 8), 8)
                        f[spot, :] = m * out[r * LV + k * 8 : r * LV + k * 8 + 8, j * LN : (j + 1) * LN]
            return 0

        lax.fori_loop(0, CT // 2, block, 0)
    loop(1, 14, lambda at: adjoint_row(f3, y2, f2, mask, at))
    loop(2, 13, lambda at: adjoint_row(f2, y1, f1, mask, at))
    loop(3, 12, lambda at: gradient_row(f1, y0, grad, at))
    for side, halo in enumerate((above, below)):
        for t in range(NT):
            for q in range(CAP // LN):
                far[NT * side + t, :, pl.ds(q * LN, LN)] = halo[pl.ds(H * COL + H * CT + 4 * t + q, 1), :].astype(I32)


def inner_adjoint(y0, y1, y2, mask, cells, terms, cols, above, below):
    return pl.pallas_call(
        inner_adjoint_kernel,
        out_shape=[FIELD] * 3 + [jax.ShapeDtypeStruct((ROWS * COL, LN), F32), jax.ShapeDtypeStruct((2 * NT, 1, CAP), I32)],
        in_specs=[VM] * 9,
        out_specs=[VM] * 5,
        scratch_shapes=[pltpu.VMEM((ROWS * LV, 2 * CAP), jnp.bfloat16)],
        compiler_params=params(12),
        cost_estimate=cost(9),
        name="inner_adjoint",
    )(y0, y1, y2, mask, cells, terms, cols, above, below)


def finish_kernel(y0, y1, y2, f1i, f2i, f3i, mask, gradi, far, above, below, f1, f2, f3, grad, out, staged, cols, left, line_ref, sems):
    for side, pay in enumerate((above, below)):
        for t, (f, scale) in enumerate(((f1, 25.0), (f2, 25.0), (f3, 5.0))):
            near = t + 1
            cell = far[NT * side + t]
            column(far, cols, NT * side + t)
            row, level = (cell >> 10) & (ROWS - 1), cell >> 14
            line = (row - (ROWS - near if side == 0 else 0)) * LV + level
            for q in range(CAP // LN):
                line_ref[pl.ds(0, 1), pl.ds(q * LN, LN)] = pay[pl.ds(4 * t + q, 1), :]
                if t == NT - 1:
                    line_ref[pl.ds(1, 1), pl.ds(q * LN, LN)] = pay[pl.ds(12 + q, 1), :]
            deep = (near * LV + 15) // 16 * 16
            spread(line, line_ref[pl.ds(0, 1), :], left, 0, deep)
            if t == NT - 1:
                deep = 128
                second = jnp.where(row == (ROWS - 2 if side == 0 else 1), level, -1)
                spread(second, line_ref[pl.ds(1, 1), :], left, deep, 48)
                deep = 176
            base = H - near if side == 0 else ROWS + H

            def block(p, _):
                res = product(left, deep, cols[pl.ds(pl.multiple_of(p * 2 * LN, 2 * LN), 2 * LN), :])
                for j in range(2):
                    c = 2 * p + j
                    for r in range(near):
                        m = scale * mask_row(mask, base + r, c)
                        for k in range(LV // 8):
                            spot = pl.ds(pl.multiple_of((base + r) * COL + c * LV + k * 8, 8), 8)
                            f[spot, :] = m * res[r * LV + k * 8 : r * LV + k * 8 + 8, j * LN : (j + 1) * LN]
                    if t == NT - 1:
                        m = 5.0 * mask_row(mask, base + 1, c)
                        for k in range(LV // 8):
                            spot = pl.ds(pl.multiple_of((base + 1) * COL + c * LV + k * 8, 8), 8)
                            f2[spot, :] = f2[spot, :] + m * res[128 + k * 8 : 136 + k * 8, j * LN : (j + 1) * LN]
                return 0

            lax.fori_loop(0, CT // 2, block, 0)
    for src, state, dst, reach in ((f3, y2, f2, 2), (f2, y1, f1, 1)):
        loop(-reach, 2 - reach, lambda at: adjoint_row(src, state, dst, mask, at))
        loop(ROWS - 3 + reach, ROWS - 1 + reach, lambda at: adjoint_row(src, state, dst, mask, at))
    loop(0, 2, lambda at: gradient_row(f1, y0, grad, at))
    loop(ROWS - 3, ROWS - 1, lambda at: gradient_row(f1, y0, grad, at))

    def copy(c):
        return pltpu.make_async_copy(staged.at[c], out.at[:, :, pl.ds(c * LN, LN)], sems.at[c])

    for c in range(CT):
        def turn(k, _):
            for half in range(2):
                v = grad[pl.ds(half * 8 * COL + c * LV + k, 8, stride=COL), :]
                staged[c, k, pl.ds(half * 8, 8), :] = v
            return 0

        lax.fori_loop(0, LV, turn, 0, unroll=8)
        copy(c).start()
    for c in range(CT):
        copy(c).wait()


def finish(y0, y1, y2, f1, f2, f3, mask, grad, far, above, below):
    return pl.pallas_call(
        finish_kernel,
        out_shape=[FIELD] * 3 + [jax.ShapeDtypeStruct((ROWS * COL, LN), F32), jax.ShapeDtypeStruct((LV, ROWS, CT * LN), F32)],
        in_specs=[VM] * 11,
        out_specs=[VM] * 4 + [ANY],
        input_output_aliases={3: 0, 4: 1, 5: 2, 7: 3},
        scratch_shapes=[
            pltpu.VMEM((CT, LV, ROWS, LN), F32),
            pltpu.VMEM((CT * LN, CAP), jnp.bfloat16),
            pltpu.VMEM((176, 2 * CAP), jnp.bfloat16),
            pltpu.VMEM((8, CAP), F32),
            pltpu.SemaphoreType.DMA((CT,)),
        ],
        compiler_params=params(12),
        cost_estimate=cost(4),
        name="finish",
    )(y0, y1, y2, f1, f2, f3, mask, grad, far, above, below)[4]


def add_kernel(a, b, out):
    out[...] = a[...] + b[...]


def reduce_kernel(scale, a, b, out):
    out[...] = jnp.sum(a[...] + b[...], keepdims=True) * scale


def small(kernel, shape, a, b, name):
    return pl.pallas_call(
        kernel,
        out_shape=jax.ShapeDtypeStruct(shape, F32),
        in_specs=[VM, VM],
        out_specs=VM,
        compiler_params=params(1),
        cost_estimate=cost(0.1),
        name=name,
    )(a, b)


def sum_along(x, scale):
    size = lax.axis_size("along")
    if size & (size - 1):
        other, x = jnp.zeros_like(x), lax.psum(x, "along")
    else:
        step, other = 1, None
        while step < size:
            if other is not None:
                x = small(add_kernel, x.shape, x, other, "add")
            other = lax.ppermute(x, "along", [(i, i ^ step) for i in range(size)])
            step *= 2
    return small(functools.partial(reduce_kernel, scale), (1, 1), x, other, "reduce").reshape(1)


def local(basic_state, land_sea, obs_cells, obs_count, obs_value):
    size = lax.axis_size("along")
    later = [(i, i + 1) for i in range(size - 1)]
    earlier = [(i + 1, i) for i in range(size - 1)]
    cells = obs_cells.transpose(1, 0, 2)
    value = obs_value.transpose(1, 0, 2)
    spots = (((cells >> 7) & (ROWS * CT - 1)) + H * CT) * LV + (cells >> 14)
    staged, up, down, mask = edges(basic_state, land_sea, cells)
    above = lax.ppermute(down, "along", later)
    below = lax.ppermute(up, "along", earlier)
    y0, y1, y2, y3, cols = interior(staged, mask, cells)
    y0, y1, y2, mask, total, pay, terms = bands(
        y0, y1, y2, y3, mask, cells, obs_count, value, spots.reshape(-1), above, below
    )
    above2 = lax.ppermute(pay, "along", later)
    below2 = lax.ppermute(pay, "along", earlier)
    misfit = sum_along(total, 1.0 / (2.0 * size * obs_cells.shape[1] * obs_cells.shape[2]))
    f1, f2, f3, grad, far = inner_adjoint(y0, y1, y2, mask, cells, terms, cols, above, below)
    gradient = finish(y0, y1, y2, f1, f2, f3, mask, grad, far, above2, below2)
    return gradient, misfit


def solution(mesh):
    in_specs = (
        P(None, ("ens", "along"), None),
        P(("ens", "along"), None),
        P(("ens", "along"), None, None),
        P(("ens", "along"), None),
        P(("ens", "along"), None, None),
    )
    out_specs = (P(None, ("ens", "along"), None), P("ens"))
    return jax.shard_map(local, mesh=mesh, in_specs=in_specs, out_specs=out_specs, check_vma=False)
```

profile of v0, /device:TPU:0, one launch (start us, length us, event | category | flops | bytes accessed | tf_op | source)
XLA Modules:
  0.0 72.1 jit_solution(18310804077216623456)
XLA Ops:
  0.6 0.0 copy-start.6
  0.6 0.0 copy-start
  0.7 1.7 %copy-done = f32[40,16,1024]{2,1,0:T(8,128)S(1)} copy-done((f32[40,16,1024]{2,1,0:T(8,128)S(1)}, f32[40,16,1024]{2,1,0:T(8,128)}, u32[]{:S(2)}) %copy-start) | copy-done | bytes 2621464
  2.4 0.7 copy-done.1
  3.1 0.8 %copy-done.4 = s32[16,1024]{1,0:T(8,128)S(1)} copy-done((s32[16,1024]{1,0:T(8,128)S(1)}, s32[16,1024]{1,0:T(8,128)}, u32[]{:S(2)}) %copy-start.4) | copy-done | bytes 65560
  3.9 1.8 %edges.1 = (f32[8,40,16,128]{3,2,1,0:T(8,128)S(1)}, f32[1000,128]{1,0:T(8,128)}, f32[1000,128]{1,0:T(8,128)}, f32[176,128]{1,0:T(8,128)S(1)}) custom-call(f32[40,16,1024]{2,1,0:T(8,128)S(1)} %copy-done, s32[16,1024]{1,0:T(8,128)S(1)} %copy-done.4, s32[3,1,512]{2,1,0:T(1,128)S(1)} %bitcast.3), custom_call_target="tpu_custom_call" | custom-call | bytes 6000000 | tf_op jit(solution)/shard_map/edges/pallas_call | solution.py:169
  5.7 2.4 %collective-permute-start = (f32[1000,128]{1,0:T(8,128)}, f32[1000,128]{1,0:T(8,128)S(1)}, u32[]{:S(2)}, u32[]{:S(2)}) collective-permute-start(f32[1000,128]{1,0:T(8,128)} %get-tuple-element.30), channel_id=1, source_target_pairs={{0,1},{1,2},{2,3},{3,4},{4,5},{5,6},{6,7},{7,8},{8,9},{9,10},{10,1... | collective-permute-start | bytes 1536008 | tf_op jit(solution)/shard_map/ppermute | solution.py:447
  8.1 1.3 %collective-permute-start.1 = (f32[1000,128]{1,0:T(8,128)}, f32[1000,128]{1,0:T(8,128)}, u32[]{:S(2)}, u32[]{:S(2)}) collective-permute-start(f32[1000,128]{1,0:T(8,128)} %get-tuple-element.31), channel_id=1, source_target_pairs={{1,0},{2,1},{3,2},{4,3},{5,4},{6,5},{7,6},{8,7},{9,8},{10,9},{11,1... | collective-permute-start | bytes 1536008 | tf_op jit(solution)/shard_map/ppermute | solution.py:448
  9.4 0.7 %add_reduce_fusion = s32[3,512]{1,0:T(4,128)S(1)} fusion(s32[1,3,512]{2,0,1:T(1,128)} %param.7), kind=kLoop, calls=%fused_computation | loop fusion | flops 9216 | bytes 12288 | tf_op jit(solution)/shard_map/add | solution.py:445
  10.2 0.0 copy-start.2
  10.2 0.7 copy-done.2
  10.9 8.6 %interior.1 = (f32[7040,128]{1,0:T(8,128)S(1)}, f32[7040,128]{1,0:T(8,128)S(1)}, f32[7040,128]{1,0:T(8,128)S(1)}, f32[7040,128]{1,0:T(8,128)S(1)}, bf16[3,1024,512]{2,1,0:T(8,128)(2,1)S(1)}) custom-call(f32[8,40,16,128]{3,2,1,0:T(8,128)S(1)} %get-tuple-element.24.staged, f32[176,128]{1,0:T(8,128)S(1)} %get-tuple-element.25.mask.maski, s32[3,1,512]{2,1,0:T(1,128)S(1)} %bitcast.4), custom_call_target="tpu_custom_call" | custom-call | bytes 27000000 | tf_op jit(solution)/shard_map/interior/pallas_call | solution.py:211
  19.5 0.0 collective-permute-done.above
  19.5 0.0 collective-permute-done.1.below
  19.5 0.0 copy-done.6
  19.5 0.0 copy-start.3
  19.5 6.0 %bands.1 = (f32[7040,128]{1,0:T(8,128)S(1)}, f32[7040,128]{1,0:T(8,128)S(1)}, f32[7040,128]{1,0:T(8,128)S(1)}, f32[176,128]{1,0:T(8,128)S(1)}, f32[8,128]{1,0:T(...) custom-call(f32[7040,128]{1,0:T(8,128)S(1)} %get-tuple-element.26.y0, ...), custom_call_target="tpu_custom_call", output_to_operand_aliasing={{0}: (0, {}), {1}: (1, {}), {2}: (2, {}), {3}: (4, {})} | custom-call | bytes 15000000 | tf_op jit(solution)/shard_map/bands/pallas_call | solution.py:271
  25.5 3.3 %collective-permute-start.4 = (f32[8,128]{1,0:T(8,128)S(1)}, f32[8,128]{1,0:T(8,128)S(1)}, u32[]{:S(2)}, u32[]{:S(2)}) collective-permute-start(f32[8,128]{1,0:T(8,128)S(1)} %get-tuple-element.45.a), channel_id=1, source_target_pairs={{0,1},{1,0},{2,3},{3,2},{4,5},{5,4},{6,7},{7,6},{8,9},{9,8},{10,11... | collective-permute-start | bytes 12296 | tf_op jit(solution)/shard_map/ppermute | solution.py:434
  28.8 0.8 %collective-permute-done.4.b = f32[8,128]{1,0:T(8,128)S(1)} collective-permute-done((f32[8,128]{1,0:T(8,128)S(1)}, f32[8,128]{1,0:T(8,128)S(1)}, u32[]{:S(2)}, u32[]{:S(2)}) %collective-permute-start.4) | collective-permute-done | bytes 4128 | tf_op jit(solution)/shard_map/ppermute | solution.py:434
  29.6 2.4 %collective-permute-start.5 = (f32[8,128]{1,0:T(8,128)S(1)}, f32[8,128]{1,0:T(8,128)S(1)}, u32[]{:S(2)}, u32[]{:S(2)}) collective-permute-start(f32[8,128]{1,0:T(8,128)S(1)} %add.27.a), channel_id=1, source_target_pairs={{0,2},{1,3},{2,0},{3,1},{4,6},{5,7},{6,4},{7,5},{8,10},{9,11},{10,... | collective-permute-start | bytes 12296 | tf_op jit(solution)/shard_map/ppermute | solution.py:434
  32.0 1.3 %collective-permute-start.3 = (f32[16,128]{1,0:T(8,128)S(1)}, f32[16,128]{1,0:T(8,128)S(1)}, u32[]{:S(2)}, u32[]{:S(2)}) collective-permute-start(f32[16,128]{1,0:T(8,128)S(1)} %get-tuple-element.43), channel_id=1, source_target_pairs={{1,0},{2,1},{3,2},{4,3},{5,4},{6,5},{7,6},{8,7},{9,8},{10,9},{11,1... | collective-permute-start | bytes 24584 | tf_op jit(solution)/shard_map/ppermute | solution.py:454
  33.3 3.0 %collective-permute-start.2 = (f32[16,128]{1,0:T(8,128)S(1)}, f32[16,128]{1,0:T(8,128)S(1)}, u32[]{:S(2)}, u32[]{:S(2)}) collective-permute-start(f32[16,128]{1,0:T(8,128)S(1)} %get-tuple-element.43), channel_id=1, source_target_pairs={{0,1},{1,2},{2,3},{3,4},{4,5},{5,6},{6,7},{7,8},{8,9},{9,10},{10,1... | collective-permute-start | bytes 24584 | tf_op jit(solution)/shard_map/ppermute | solution.py:453
  36.4 0.0 collective-permute-done.5.b
  36.4 1.6 %collective-permute-start.6 = (f32[8,128]{1,0:T(8,128)S(1)}, f32[8,128]{1,0:T(8,128)S(1)}, u32[]{:S(2)}, u32[]{:S(2)}) collective-permute-start(f32[8,128]{1,0:T(8,128)S(1)} %add.28.a), channel_id=1, source_target_pairs={{0,4},{1,5},{2,6},{3,7},{4,0},{5,1},{6,2},{7,3},{8,12},{9,13},{10,... | collective-permute-start | bytes 12296 | tf_op jit(solution)/shard_map/ppermute | solution.py:434
  38.0 2.0 %collective-permute-done.6.b = f32[8,128]{1,0:T(8,128)S(1)} collective-permute-done((f32[8,128]{1,0:T(8,128)S(1)}, f32[8,128]{1,0:T(8,128)S(1)}, u32[]{:S(2)}, u32[]{:S(2)}) %collective-permute-start.6) | collective-permute-done | bytes 4128 | tf_op jit(solution)/shard_map/ppermute | solution.py:434
  40.1 2.6 %collective-permute-start.7 = (f32[8,128]{1,0:T(8,128)S(1)}, f32[8,128]{1,0:T(8,128)S(1)}, u32[]{:S(2)}, u32[]{:S(2)}) collective-permute-start(f32[8,128]{1,0:T(8,128)S(1)} %add.29.a), channel_id=1, source_target_pairs={{0,8},{1,9},{2,10},{3,11},{4,12},{5,13},{6,14},{7,15},{8,0},{9,1},... | collective-permute-start | bytes 12296 | tf_op jit(solution)/shard_map/ppermute | solution.py:434
  42.7 14.1 %inner_adjoint.1 = (f32[7040,128]{1,0:T(8,128)S(1)}, f32[7040,128]{1,0:T(8,128)S(1)}, f32[7040,128]{1,0:T(8,128)S(1)}, f32[5120,128]{1,0:T(8,128)S(1)}, s32[6,1,512]{2,1,0:T(1,128)S(1)}) custom-call(f32[7040,128]{1,0:T(8,128)S(1)} %get-tuple-element.32.y0, f32[7040,128]{1,0:T(8,128)S(1)} %get-tuple-element.33.y1, f32[7040,128]{1,0:T(8,128)S(1)} %get-tuple-element.34.y2, ...), custom_call_target="tpu_custom_call" | custom-call | bytes 27000000 | tf_op jit(solution)/shard_map/inner_adjoint/pallas_call | solution.py:313
  56.8 0.0 collective-permute-done.3.below
  56.8 0.0 collective-permute-done.2.above
  56.8 14.6 %finish.1 = (f32[7040,128]{1,0:T(8,128)S(1)}, f32[7040,128]{1,0:T(8,128)S(1)}, f32[7040,128]{1,0:T(8,128)S(1)}, f32[5120,128]{1,0:T(8,128)S(1)}, f32[40,16,1024]{2,1,0:T(8,128)}) custom-call(f32[7040,128]{1,0:T(8,128)S(1)} %get-tuple-element.32.y0, ...), custom_call_target="tpu_custom_call", output_to_operand_aliasing={{0}: (3, {}), {1}: (4, {}), {2}: (5, {}), {3}: (7, {})} | custom-call | bytes 12000000 | tf_op jit(solution)/shard_map/finish/pallas_call | solution.py:386
  71.5 0.0 collective-permute-done.7.b
  71.5 0.6 reduce.3
  (9 shorter events, 0.0 us)
Async XLA Ops:
  0.6 18.9 %copy-start.6 = (s32[1,3]{1,0:T(1,128)S(1)}, s32[1,3]{1,0:T(1,128)}, u32[]{:S(2)}) copy-start(s32[1,3]{1,0:T(1,128)} %count.1) | copy-start | bytes 40
  0.6 1.7 %copy-start = (f32[40,16,1024]{2,1,0:T(8,128)S(1)}, f32[40,16,1024]{2,1,0:T(8,128)}, u32[]{:S(2)}) copy-start(f32[40,16,1024]{2,1,0:T(8,128)} %basic.1) | copy-start | bytes 7864324
  2.4 0.7 copy-start.1
  3.1 0.8 %copy-start.4 = (s32[16,1024]{1,0:T(8,128)S(1)}, s32[16,1024]{1,0:T(8,128)}, u32[]{:S(2)}) copy-start(s32[16,1024]{1,0:T(8,128)} %land.1) | copy-start | bytes 196612
  3.9 15.6 %copy-start.5 = (f32[1,3,512]{2,0,1:T(1,128)S(1)}, f32[1,3,512]{2,0,1:T(1,128)}, u32[]{:S(2)}) copy-start(f32[1,3,512]{2,0,1:T(1,128)} %param.9) | copy-start | bytes 18436
  5.7 13.7 %collective-permute-start = (f32[1000,128]{1,0:T(8,128)}, f32[1000,128]{1,0:T(8,128)S(1)}, u32[]{:S(2)}, u32[]{:S(2)}) collective-permute-start(f32[1000,128]{1,0:T(8,128)} %get-tuple-element.30), channel_id=1, source_target_pairs={{0,1},{1,2},{2,3},{3,4},{4,5},{5,6},{6,7},{7,8},{8,9},{9,10},{10,1... | collective-permute-start | bytes 1536008 | tf_op jit(solution)/shard_map/ppermute | solution.py:447
  8.1 11.4 %collective-permute-start.1 = (f32[1000,128]{1,0:T(8,128)}, f32[1000,128]{1,0:T(8,128)}, u32[]{:S(2)}, u32[]{:S(2)}) collective-permute-start(f32[1000,128]{1,0:T(8,128)} %get-tuple-element.31), channel_id=1, source_target_pairs={{1,0},{2,1},{3,2},{4,3},{5,4},{6,5},{7,6},{8,7},{9,8},{10,9},{11,1... | collective-permute-start | bytes 1536008 | tf_op jit(solution)/shard_map/ppermute | solution.py:448
  10.2 0.7 copy-start.2
  19.5 23.2 %copy-start.3 = (s32[1,3,512]{2,0,1:T(1,128)S(1)}, s32[1,3,512]{2,0,1:T(1,128)}, u32[]{:S(2)}) copy-start(s32[1,3,512]{2,0,1:T(1,128)} %param.7) | copy-start | bytes 18436
  25.5 4.1 %collective-permute-start.4 = (f32[8,128]{1,0:T(8,128)S(1)}, f32[8,128]{1,0:T(8,128)S(1)}, u32[]{:S(2)}, u32[]{:S(2)}) collective-permute-start(f32[8,128]{1,0:T(8,128)S(1)} %get-tuple-element.45.a), channel_id=1, source_target_pairs={{0,1},{1,0},{2,3},{3,2},{4,5},{5,4},{6,7},{7,6},{8,9},{9,8},{10,11... | collective-permute-start | bytes 12296 | tf_op jit(solution)/shard_map/ppermute | solution.py:434
  29.6 6.7 %collective-permute-start.5 = (f32[8,128]{1,0:T(8,128)S(1)}, f32[8,128]{1,0:T(8,128)S(1)}, u32[]{:S(2)}, u32[]{:S(2)}) collective-permute-start(f32[8,128]{1,0:T(8,128)S(1)} %add.27.a), channel_id=1, source_target_pairs={{0,2},{1,3},{2,0},{3,1},{4,6},{5,7},{6,4},{7,5},{8,10},{9,11},{10,... | collective-permute-start | bytes 12296 | tf_op jit(solution)/shard_map/ppermute | solution.py:434
  32.0 24.8 %collective-permute-start.3 = (f32[16,128]{1,0:T(8,128)S(1)}, f32[16,128]{1,0:T(8,128)S(1)}, u32[]{:S(2)}, u32[]{:S(2)}) collective-permute-start(f32[16,128]{1,0:T(8,128)S(1)} %get-tuple-element.43), channel_id=1, source_target_pairs={{1,0},{2,1},{3,2},{4,3},{5,4},{6,5},{7,6},{8,7},{9,8},{10,9},{11,1... | collective-permute-start | bytes 24584 | tf_op jit(solution)/shard_map/ppermute | solution.py:454
  33.3 23.5 %collective-permute-start.2 = (f32[16,128]{1,0:T(8,128)S(1)}, f32[16,128]{1,0:T(8,128)S(1)}, u32[]{:S(2)}, u32[]{:S(2)}) collective-permute-start(f32[16,128]{1,0:T(8,128)S(1)} %get-tuple-element.43), channel_id=1, source_target_pairs={{0,1},{1,2},{2,3},{3,4},{4,5},{5,6},{6,7},{7,8},{8,9},{9,10},{10,1... | collective-permute-start | bytes 24584 | tf_op jit(solution)/shard_map/ppermute | solution.py:453
  36.4 3.7 %collective-permute-start.6 = (f32[8,128]{1,0:T(8,128)S(1)}, f32[8,128]{1,0:T(8,128)S(1)}, u32[]{:S(2)}, u32[]{:S(2)}) collective-permute-start(f32[8,128]{1,0:T(8,128)S(1)} %add.28.a), channel_id=1, source_target_pairs={{0,4},{1,5},{2,6},{3,7},{4,0},{5,1},{6,2},{7,3},{8,12},{9,13},{10,... | collective-permute-start | bytes 12296 | tf_op jit(solution)/shard_map/ppermute | solution.py:434
  40.1 31.4 %collective-permute-start.7 = (f32[8,128]{1,0:T(8,128)S(1)}, f32[8,128]{1,0:T(8,128)S(1)}, u32[]{:S(2)}, u32[]{:S(2)}) collective-permute-start(f32[8,128]{1,0:T(8,128)S(1)} %add.29.a), channel_id=1, source_target_pairs={{0,8},{1,9},{2,10},{3,11},{4,12},{5,13},{6,14},{7,15},{8,0},{9,1},... | collective-permute-start | bytes 12296 | tf_op jit(solution)/shard_map/ppermute | solution.py:434
where the time goes:
time: 72.6 us; the launch traced here: 72.1 us
  Pallas kernels  45.8 us (63%)
  starting transfers between devices  17.9 us (25%)
  local copies, waits for them, and re-layouts  3.98 us (5%)
  waiting for transfers between devices  2.87 us (4%)
  between operations  0.81 us (1%)
  other arithmetic  0.73 us (1%)
    pallas_call x1, Pallas kernels, finish(): pl.pallas_call(finish_kernel, out_shape=[FIELD] * 3 + [jax.ShapeDtypeStru...  14.6 us
    pallas_call x1, Pallas kernels, inner_adjoint(): pl.pallas_call(inner_adjoint_kernel, out_shape=[FIELD] * 3 + [jax.ShapeDt...  14.1 us
    ppermute x4, starting transfers between devices, sum_along(): other = lax.ppermute(x, 'along', [(i, i ^ step) for i in range(size)])  9.95 us
    pallas_call x1, Pallas kernels, interior(): pl.pallas_call(interior_kernel, out_shape=[FIELD] * 4 + [jax.ShapeDtypeSt...  8.6 us
    pallas_call x1, Pallas kernels, bands(): pl.pallas_call(bands_kernel, out_shape=[FIELD] * 3 + [MASK, jax.ShapeDtyp...  6 us
    unnamed x14, local copies, waits for them, and re-layouts  3.97 us
    ppermute x1, starting transfers between devices, local(): above2 = lax.ppermute(pay, 'along', later)  3.03 us
    ppermute x4, waiting for transfers between devices, sum_along(): other = lax.ppermute(x, 'along', [(i, i ^ step) for i in range(size)])  2.85 us
  transfers between devices with their start and end apart: 8, of which 2 were waited for; matrix products, arithmetic and copies ran while one was open for 1% of the time, Pallas kernels for 52%

commit v1 on v0

v1 whole, which is shorter than its diff:
```python
import functools

import jax
import jax.numpy as jnp
from jax import lax
from jax.experimental import pallas as pl
from jax.experimental.pallas import tpu as pltpu
from jax.sharding import PartitionSpec as P

F32 = jnp.float32
I32 = jnp.int32
ROWS, CT, LV, LN = 16, 8, 40, 128
H = 3
RX = ROWS + 2 * H
COL = CT * LV
EDGE = H * COL + H * CT
CAP = 512
NT = 3
PAY = 32
CODE = 16

VM = pl.BlockSpec(memory_space=pltpu.VMEM)
SM = pl.BlockSpec(memory_space=pltpu.SMEM)
HBM = pl.BlockSpec(memory_space=pltpu.MemorySpace.HBM)
ANY = pl.BlockSpec(memory_space=pl.ANY)
FIELD = jax.ShapeDtypeStruct((RX * COL, LN), F32)
MASK = jax.ShapeDtypeStruct((RX * CT, LN), F32)


def params(mib):
    return pltpu.CompilerParams(vmem_limit_bytes=mib << 20)


def cost(us):
    return pl.CostEstimate(flops=0, bytes_accessed=int(us * 3.0e6), transcendentals=0)


def lanes():
    return lax.broadcasted_iota(I32, (8, LN), 1)


def sublanes():
    return lax.broadcasted_iota(I32, (8, LN), 0)


def stencil_row(src, at, emit):
    lane, sub = lanes(), sublanes()
    first, last = lane == 0, lane == LN - 1
    low, high = sub == 0, sub == 7
    base = pl.multiple_of(at * COL, COL)
    for k in range(LV // 8):
        offs = [base + c * LV + k * 8 for c in range(CT)]
        mids = [src[pl.ds(pl.multiple_of(o, 8), 8), :] for o in offs]
        fwd = [pltpu.roll(v, 1, 1) for v in mids]
        bwd = [pltpu.roll(v, LN - 1, 1) for v in mids]
        for c in range(CT):
            v, o = mids[c], offs[c]
            west = jnp.where(first, fwd[c - 1] if c > 0 else 0.0, fwd[c])
            east = jnp.where(last, bwd[c + 1] if c < CT - 1 else 0.0, bwd[c])
            north = src[pl.ds(pl.multiple_of(o - COL, 8), 8), :]
            south = src[pl.ds(pl.multiple_of(o + COL, 8), 8), :]
            if k > 0:
                down = src[pl.ds(o - 1, 8), :]
            else:
                down = jnp.where(low, v, pltpu.roll(v, 1, 0))
            if k < LV // 8 - 1:
                up = src[pl.ds(o + 1, 8), :]
            else:
                up = jnp.where(high, v, pltpu.roll(v, 7, 0))
            s = ((north + south) + (west + east)) + 0.2 * (down + up)
            emit(c, k, v, s, o)


class Fetch:
    def __init__(self, src, dst, sems):
        self.parts = [pltpu.make_async_copy(src.at[t, 0], dst.at[pl.ds(t * CAP, CAP)], sems.at[t]) for t in range(NT)]

    def start(self):
        for part in self.parts:
            part.start()

    def wait(self):
        for part in self.parts:
            part.wait()


def mask_row(mask, at, c):
    return mask[pl.ds(at * CT + c, 8, stride=0), :]


def forward_row(src, dst, mask, at):
    ms = [mask_row(mask, at, c) for c in range(CT)]

    def emit(c, k, v, s, o):
        dst[pl.ds(pl.multiple_of(o, 8), 8), :] = ms[c] * (s + v * (0.6 - v * v))

    stencil_row(src, at, emit)


def adjoint_row(src, state, forcing, mask, at):
    ms = [mask_row(mask, at, c) for c in range(CT)]

    def emit(c, k, g, s, o):
        spot = pl.ds(pl.multiple_of(o, 8), 8)
        y = state[spot, :]
        forcing[spot, :] = ms[c] * ((s + g * (0.6 - 3.0 * (y * y))) + forcing[spot, :])

    stencil_row(src, at, emit)


def gradient_row(src, state, out, at):
    def emit(c, k, g, s, o):
        y = state[pl.ds(pl.multiple_of(o, 8), 8), :]
        out[pl.ds(pl.multiple_of(o - H * COL, 8), 8), :] = 0.2 * (s + g * (0.6 - 3.0 * (y * y)))

    stencil_row(src, at, emit)


def loop(first, last, body):
    lax.fori_loop(first + H, last + H + 1, lambda at, _: (body(at), 0)[1], 0)


def edges_kernel(basic, land_at, staged, up, down, mask, land, sems):
    def copy(c):
        return pltpu.make_async_copy(basic.at[:, :, pl.ds(c * LN, LN)], staged.at[c], sems.at[c])

    sea = pltpu.make_async_copy(land_at, land, sems.at[CT])
    sea.start()
    for c in range(CT):
        copy(c).start()
    sea.wait()
    for c in range(CT):
        mask[pl.ds(H * CT + c, ROWS, stride=CT), :] = 0.2 * land[:, pl.ds(c * LN, LN)].astype(F32)
    for c in range(CT):
        copy(c).wait()
        flat = staged.at[c].reshape(LV * ROWS, LN)
        for out, first in ((up, 0), (down, ROWS - H)):
            for j in range(H):
                r = first + j
                half = 2.5 * mask_row(mask, r + H, c)
                for k in range(LV // 8):
                    v = flat[pl.ds(k * 8 * ROWS + r, 8, stride=ROWS), :]
                    out[pl.ds((j * CT + c) * LV + k * 8, 8), :] = half * v
                out[pl.ds(H * COL + j * CT + c, 1), :] = mask[pl.ds((r + H) * CT + c, 1), :]


def edges(basic, land):
    return pl.pallas_call(
        edges_kernel,
        out_shape=[
            jax.ShapeDtypeStruct((CT, LV, ROWS, LN), F32),
            jax.ShapeDtypeStruct((EDGE, LN), F32),
            jax.ShapeDtypeStruct((EDGE, LN), F32),
            MASK,
        ],
        in_specs=[HBM, HBM],
        out_specs=[VM] * 4,
        scratch_shapes=[pltpu.VMEM((ROWS, CT * LN), I32), pltpu.SemaphoreType.DMA((CT + 1,))],
        compiler_params=params(4),
        cost_estimate=cost(2),
        name="edges",
    )(pltpu.with_memory_space_constraint(basic, pltpu.HBM), pltpu.with_memory_space_constraint(land, pltpu.HBM))


def order_kernel(cells, count, value, addr, live, sval, lane, spot, second, codes):
    slot = lax.broadcasted_iota(I32, (1, CAP), 1)
    ups, downs = [], []
    for t in range(NT):
        row = (cells[t] >> 10) & (ROWS - 1)
        alive = slot < count[0, t]
        ups.append(jnp.logical_and(alive, row <= t))
        downs.append(jnp.logical_and(alive, row >= ROWS - 1 - t))
    one = [jnp.where(f, 1.0, 0.0) for f in ups + downs]
    flags = jnp.concatenate(one + [jnp.zeros((10, CAP), F32)], axis=0).astype(jnp.bfloat16)
    tri = jnp.where(
        lax.broadcasted_iota(I32, (CAP, CAP), 0) < lax.broadcasted_iota(I32, (CAP, CAP), 1), 1.0, 0.0
    ).astype(jnp.bfloat16)
    before = jnp.dot(flags, tri, preferred_element_type=F32)
    codes[...] = jnp.zeros((CODE, LN), F32)
    sub = lax.broadcasted_iota(I32, (CAP, CAP), 0)
    first = lax.broadcasted_iota(I32, (1, LN), 1)
    tally = jnp.zeros((1, LN), F32)
    for t in range(NT):
        up, down = ups[t], downs[t]
        pu, pd = before[t : t + 1], before[NT + t : NT + t + 1]
        nu = jnp.sum(one[t], axis=1, keepdims=True)
        nd = jnp.sum(one[NT + t], axis=1, keepdims=True)
        tally = tally + jnp.where(first == t, nu, 0.0) + jnp.where(first == NT + t, nd, 0.0)
        rank = jnp.where(up, pu, jnp.where(down, CAP - nd + pd, nu + slot.astype(F32) - pu - pd)).astype(I32)
        place = jnp.where(sub == rank, 1.0, 0.0).astype(jnp.bfloat16)
        cell, v = cells[t], value[t]
        v1 = v.astype(jnp.bfloat16).astype(F32)
        v2 = (v - v1).astype(jnp.bfloat16).astype(F32)
        parts = [
            (cell >> 16).astype(F32),
            ((cell >> 8) & 255).astype(F32),
            (cell & 255).astype(F32),
            v1,
            v2,
            v - v1 - v2,
            jnp.where(slot < count[0, t], 1.0, 0.0),
        ]
        left = jnp.concatenate(parts + [jnp.zeros((9, CAP), F32)], axis=0).astype(jnp.bfloat16)
        out = lax.dot_general(left, place, (((1,), (1,)), ((), ())), preferred_element_type=F32)
        cell = (out[0:1] * 65536.0 + out[1:2] * 256.0 + out[2:3]).astype(I32)
        row, level, where = (cell >> 10) & (ROWS - 1), cell >> 14, (cell >> 7) & (ROWS * CT - 1)
        alive = out[6:7] > 0.5
        own = (where + H * CT) * LV + level
        addr[t] = own
        spot[t] = where + H * CT
        sval[t] = out[3:4] + out[4:5] + out[5:6]
        lane[t] = jnp.where(alive, (cell & (LN - 1)).astype(F32), -1.0)
        live[t] = out[6:7]
        if t == NT - 1:
            second[0] = jnp.where(jnp.logical_or(row == 1, row == ROWS - 2), -3.0, 0.0)
        far = jnp.where(row < ROWS // 2, own + ROWS * COL, own - ROWS * COL)
        near = jnp.logical_or(row <= t, row >= ROWS - 1 - t)
        code = jnp.where(near, far * LN + (cell & (LN - 1)), 0).astype(F32)
        for q in range(CAP // LN):
            codes[pl.ds(4 * t + q, 1), :] = code[:, q * LN : (q + 1) * LN]
    codes[pl.ds(12, 1), :] = tally


def order(cells, count, value):
    ints, floats = jax.ShapeDtypeStruct((NT, 1, CAP), I32), jax.ShapeDtypeStruct((NT, 1, CAP), F32)
    return pl.pallas_call(
        order_kernel,
        out_shape=[ints, floats, floats, floats, ints, jax.ShapeDtypeStruct((1, 1, CAP), F32), jax.ShapeDtypeStruct((CODE, LN), F32)],
        in_specs=[VM, SM, VM],
        out_specs=[VM] * 7,
        compiler_params=params(6),
        cost_estimate=cost(2),
        name="order",
    )(cells, count, value)


def upright(line):
    return jnp.broadcast_to(line, (LN, LN)).T


def interior_kernel(staged, mask, lane, sval, spots, y0, y1, y2, y3, f1, f2, f3, twice, known, sea, at_ref, sem):
    fetch = Fetch(spots, at_ref, sem)
    fetch.start()
    for c in range(CT):
        flat = staged.at[c].reshape(LV * ROWS, LN)

        def turn(r, _):
            half = 2.5 * mask_row(mask, r + H, c)
            for k in range(LV // 8):
                v = flat[pl.ds(k * 8 * ROWS + r, 8, stride=ROWS), :]
                y0[pl.ds(pl.multiple_of((r + H) * COL + c * LV + k * 8, 8), 8), :] = half * v
            return 0

        lax.fori_loop(0, ROWS, turn, 0, unroll=2)

    zero = jnp.zeros((8, LN), F32)
    for at in (H - 2, ROWS + H + 1):
        for j in range(COL // 8):
            y2[pl.ds(at * COL + j * 8, 8), :] = zero

    def clear(at, _):
        for f in (f1, f2, f3):
            for j in range(COL // 8):
                f[pl.ds(pl.multiple_of(at * COL, 8) + j * 8, 8), :] = zero
        return 0

    lax.fori_loop(0, RX, clear, 0)
    loop(1, 14, lambda at: forward_row(y0, y1, mask, at))
    loop(2, 13, lambda at: forward_row(y1, y2, mask, at))
    loop(3, 12, lambda at: forward_row(y2, y3, mask, at))
    ids = lax.broadcasted_iota(I32, (LN, LN), 1).astype(F32)
    for t in range(NT):
        for q in range(CAP // LN):
            part = pl.ds(q * LN, LN)
            hit = upright(lane[t, :, part]) == ids
            rows = pl.ds(t * CAP + q * LN, LN)
            twice[rows, :] = jnp.where(hit, 2.0, 0.0)
            known[rows, :] = jnp.where(hit, upright(sval[t, :, part]), 0.0)
    fetch.wait()

    def group(i, _):
        for u in range(8):
            s = i * 8 + u
            sea[pl.ds(s, 1), :] = mask[pl.ds(at_ref[2 * CAP + s], 1), :]
        return 0

    lax.fori_loop(0, CAP // 8, group, 0)


def interior(staged, mask, lane, sval, spots):
    rows = jax.ShapeDtypeStruct((NT * CAP, LN), F32)
    return pl.pallas_call(
        interior_kernel,
        out_shape=[FIELD] * 7 + [rows, rows, jax.ShapeDtypeStruct((CAP, LN), F32)],
        in_specs=[VM] * 4 + [ANY],
        out_specs=[VM] * 10,
        scratch_shapes=[pltpu.SMEM((NT * CAP,), I32), pltpu.SemaphoreType.DMA((NT,))],
        compiler_params=params(6),
        cost_estimate=cost(9),
        name="interior",
    )(staged, mask, lane, sval, spots)


def bands_kernel(y0i, y1i, y2i, y3, maski, twice, known, sea, second, codes, addrs, above, below,
                 y0, y1, y2, mask, total, pay, terms, g1, g2, g3, g4, at_ref, sem):
    fetch = Fetch(addrs, at_ref, sem)
    fetch.start()
    for halo, first in ((above, 0), (below, ROWS + H)):
        for j in range(H):
            base = (first + j) * COL
            for q in range(COL // 8):
                y0[pl.ds(base + q * 8, 8), :] = halo[pl.ds(j * COL + q * 8, 8), :]
            mask[pl.ds((first + j) * CT, CT), :] = halo[pl.ds(H * COL + j * CT, CT), :]
    for src, dst, reach in ((y0, y1, 2), (y1, y2, 1), (y2, y3, 0)):
        loop(-reach, 2 - reach, lambda at: forward_row(src, dst, mask, at))
        loop(ROWS - 3 + reach, ROWS - 1 + reach, lambda at: forward_row(src, dst, mask, at))
    fetch.wait()
    many = 8

    def group(i, _):
        for u in range(many):
            s = i * many + u
            third = at_ref[2 * CAP + s]
            g1[pl.ds(s, 1), :] = y1[pl.ds(at_ref[s], 1), :]
            g2[pl.ds(s, 1), :] = y2[pl.ds(at_ref[CAP + s], 1), :]
            g3[pl.ds(s, 1), :] = y3[pl.ds(third, 1), :]
            g4[pl.ds(s, 1), :] = y2[pl.ds(third, 1), :]
        return 0

    lax.fori_loop(0, CAP // many, group, 0)
    acc = jnp.zeros((8, LN), F32)
    for t, g in enumerate((g1, g2, g3)):
        for q in range(CAP // LN):
            part, rows = pl.ds(q * LN, LN), pl.ds(t * CAP + q * LN, LN)
            d = g[part, :] * twice[rows, :] - known[rows, :]
            acc = acc + jnp.sum((d * d).reshape(LN // 8, 8, LN), axis=0)
            if t == NT - 1:
                d = d * (5.0 * sea[part, :])
                z = g4[part, :]
                e = jnp.sum(((z * z) * d).T, axis=0, keepdims=True)
                pay[pl.ds(12 + q, 1), :] = e * second[0, :, part]
            else:
                d = 5.0 * d
            terms[rows, :] = d
            pay[pl.ds(4 * t + q, 1), :] = jnp.sum(d.T, axis=0, keepdims=True)
    pay[pl.ds(CODE, CODE), :] = codes[...]
    total[...] = acc


def bands(y0, y1, y2, y3, mask, twice, known, sea, second, codes, addrs, above, below):
    rows = pltpu.VMEM((CAP, LN), F32)
    return pl.pallas_call(
        bands_kernel,
        out_shape=[FIELD] * 3
        + [
            MASK,
            jax.ShapeDtypeStruct((8, LN), F32),
            jax.ShapeDtypeStruct((PAY, LN), F32),
            jax.ShapeDtypeStruct((NT * CAP, LN), F32),
        ],
        in_specs=[VM] * 10 + [ANY] + [VM] * 2,
        out_specs=[VM] * 7,
        input_output_aliases={0: 0, 1: 1, 2: 2, 4: 3},
        scratch_shapes=[rows, rows, rows, rows, pltpu.SMEM((NT * CAP,), I32), pltpu.SemaphoreType.DMA((NT,))],
        compiler_params=params(4),
        cost_estimate=cost(5),
        name="bands",
    )(y0, y1, y2, y3, mask, twice, known, sea, second, codes, addrs, above, below)


def scatter_kernel(f1i, f2i, f3i, terms, addrs, f1, f2, f3, at_ref, sem):
    fetch = Fetch(addrs, at_ref, sem)
    fetch.start()
    fetch.wait()

    def group(i, _):
        for u in range(8):
            s = i * 8 + u
            for t, f in enumerate((f1, f2, f3)):
                spot = pl.ds(at_ref[t * CAP + s], 1)
                f[spot, :] = f[spot, :] + terms[pl.ds(t * CAP + s, 1), :]
        return 0

    lax.fori_loop(0, CAP // 8, group, 0)


def scatter(f1, f2, f3, terms, addrs):
    return pl.pallas_call(
        scatter_kernel,
        out_shape=[FIELD] * 3,
        in_specs=[VM] * 4 + [ANY],
        out_specs=[VM] * 3,
        input_output_aliases={0: 0, 1: 1, 2: 2},
        scratch_shapes=[pltpu.SMEM((NT * CAP,), I32), pltpu.SemaphoreType.DMA((NT,))],
        compiler_params=params(2),
        cost_estimate=cost(3),
        name="scatter",
    )(f1, f2, f3, terms, addrs)


def adjoint_kernel(first, last, src, state, forcing, mask, out):
    loop(first, last, lambda at: adjoint_row(src, state, out, mask, at))


def adjoint(first, last, src, state, forcing, mask):
    return pl.pallas_call(
        functools.partial(adjoint_kernel, first, last),
        out_shape=FIELD,
        in_specs=[VM] * 4,
        out_specs=VM,
        input_output_aliases={2: 0},
        compiler_params=params(2),
        cost_estimate=cost(2),
        name="adjoint",
    )(src, state, forcing, mask)


def middle_kernel(f1, y0, grad):
    loop(3, 12, lambda at: gradient_row(f1, y0, grad, at))


def middle(f1, y0):
    return pl.pallas_call(
        middle_kernel,
        out_shape=jax.ShapeDtypeStruct((ROWS * COL, LN), F32),
        in_specs=[VM] * 2,
        out_specs=VM,
        compiler_params=params(2),
        cost_estimate=cost(2),
        name="middle",
    )(f1, y0)


def finish_kernel(y0, y1, y2, f1i, f2i, f3i, mask, gradi, above, below, f1, f2, f3, grad, out, staged, a_ref, b_ref, sems):
    fetches = [pltpu.make_async_copy(src, dst, sems.at[CT + i]) for i, (src, dst) in enumerate(((above, a_ref), (below, b_ref)))]
    for f in fetches:
        f.start()
    for f in fetches:
        f.wait()
    counts = 2 * CODE * LN - (CODE - 12) * LN
    lane = lax.broadcasted_iota(I32, (1, LN), 1)
    na = [a_ref[counts + NT + t].astype(I32) for t in range(NT)]
    nb = [b_ref[counts + t].astype(I32) for t in range(NT)]
    most = na[0]
    for n in na[1:] + nb:
        most = jnp.maximum(most, n)

    def item(j, _):
        for t, f in ((2, f3), (1, f2), (0, f1)):
            for ref, n, slot in ((a_ref, na[t], CAP - 1 - j), (b_ref, nb[t], j)):
                code = ref[CODE * LN + t * CAP + slot].astype(I32)
                hit = lane == jnp.where(j < n, code & (LN - 1), -1)
                spot = pl.ds(code >> 7, 1)
                f[spot, :] = f[spot, :] + jnp.where(hit, ref[t * CAP + slot], 0.0)
                if t == NT - 1:
                    f2[spot, :] = f2[spot, :] + jnp.where(hit, ref[12 * LN + slot], 0.0)
        return 0

    lax.fori_loop(0, most, item, 0)
    for src, state, dst, reach in ((f3, y2, f2, 2), (f2, y1, f1, 1)):
        loop(-reach, 2 - reach, lambda at: adjoint_row(src, state, dst, mask, at))
        loop(ROWS - 3 + reach, ROWS - 1 + reach, lambda at: adjoint_row(src, state, dst, mask, at))
    loop(0, 2, lambda at: gradient_row(f1, y0, grad, at))
    loop(ROWS - 3, ROWS - 1, lambda at: gradient_row(f1, y0, grad, at))

    def copy(c):
        return pltpu.make_async_copy(staged.at[c], out.at[:, :, pl.ds(c * LN, LN)], sems.at[c])

    for c in range(CT):
        def turn(k, _):
            for half in range(2):
                v = grad[pl.ds(half * 8 * COL + c * LV + k, 8, stride=COL), :]
                staged[c, k, pl.ds(half * 8, 8), :] = v
            return 0

        lax.fori_loop(0, LV, turn, 0, unroll=8)
        copy(c).start()
    for c in range(CT):
        copy(c).wait()


def finish(y0, y1, y2, f1, f2, f3, mask, grad, above, below):
    return pl.pallas_call(
        finish_kernel,
        out_shape=[FIELD] * 3 + [jax.ShapeDtypeStruct((ROWS * COL, LN), F32), jax.ShapeDtypeStruct((LV, ROWS, CT * LN), F32)],
        in_specs=[VM] * 8 + [ANY] * 2,
        out_specs=[VM] * 4 + [ANY],
        input_output_aliases={3: 0, 4: 1, 5: 2, 7: 3},
        scratch_shapes=[
            pltpu.VMEM((CT, LV, ROWS, LN), F32),
            pltpu.SMEM((PAY * LN,), F32),
            pltpu.SMEM((PAY * LN,), F32),
            pltpu.SemaphoreType.DMA((CT + 2,)),
        ],
        compiler_params=params(6),
        cost_estimate=cost(6),
        name="finish",
    )(y0, y1, y2, f1, f2, f3, mask, grad, above, below)[4]


def add_kernel(a, b, out):
    out[...] = a[...] + b[...]


def reduce_kernel(scale, a, b, out):
    out[...] = jnp.sum(a[...] + b[...], keepdims=True) * scale


def small(kernel, shape, a, b, name):
    return pl.pallas_call(
        kernel,
        out_shape=jax.ShapeDtypeStruct(shape, F32),
        in_specs=[VM, VM],
        out_specs=VM,
        compiler_params=params(1),
        cost_estimate=cost(0.1),
        name=name,
    )(a, b)


def sum_along(x, stages, scale):
    size = lax.axis_size("along")
    steps = [1 << i for i in range(size.bit_length() - 1)]
    held = ()
    if size & (size - 1):
        x, steps = lax.psum(x, "along"), []
    other = jnp.zeros_like(x)
    for i in range(max(len(steps), len(stages))):
        if i < len(steps):
            if i > 0:
                x = small(add_kernel, x.shape, x, other, "add")
                x, held = lax.optimization_barrier((x, held))
            other = lax.ppermute(x, "along", [(p, p ^ steps[i]) for p in range(size)])
        if i < len(stages):
            held = stages[i](*held)
    return small(functools.partial(reduce_kernel, scale), (1, 1), x, other, "reduce").reshape(1), held


def local(basic_state, land_sea, obs_cells, obs_count, obs_value):
    size = lax.axis_size("along")
    later = [(i, i + 1) for i in range(size - 1)]
    earlier = [(i + 1, i) for i in range(size - 1)]
    cells = obs_cells.transpose(1, 0, 2)
    value = obs_value.transpose(1, 0, 2)
    staged, up, down, mask = edges(basic_state, land_sea)
    above = lax.ppermute(down, "along", later)
    below = lax.ppermute(up, "along", earlier)
    addrs, _, sval, lane, spots, second, codes = order(cells, obs_count, value)
    y0, y1, y2, y3, f1, f2, f3, twice, known, sea = interior(staged, mask, lane, sval, spots)
    y0, y1, y2, mask, total, pay, terms = bands(
        y0, y1, y2, y3, mask, twice, known, sea, second, codes, addrs, above, below
    )
    above = lax.ppermute(pay, "along", later).reshape(-1)
    below = lax.ppermute(pay, "along", earlier).reshape(-1)
    stages = (
        lambda: scatter(f1, f2, f3, terms, addrs),
        lambda a, b, c: (a, adjoint(1, 14, c, y2, b, mask), c),
        lambda a, b, c: (adjoint(2, 13, b, y1, a, mask), b, c),
        lambda a, b, c: (a, b, c, middle(a, y0)),
    )
    misfit, held = sum_along(total, stages, 1.0 / (2.0 * size * obs_cells.shape[1] * obs_cells.shape[2]))
    gradient = finish(y0, y1, y2, *held[:3], mask, held[3], above, below)
    return gradient, misfit


def solution(mesh):
    in_specs = (
        P(None, ("ens", "along"), None),
        P(("ens", "along"), None),
        P(("ens", "along"), None, None),
        P(("ens", "along"), None),
        P(("ens", "along"), None, None),
    )
    out_specs = (P(None, ("ens", "along"), None), P("ens"))
    return jax.shard_map(local, mesh=mesh, in_specs=in_specs, out_specs=out_specs, check_vma=False)
```

time: 72.6 us -> 57.2 us (0.79)
  Pallas kernels: 45.8 us -> 35.2 us
  waiting for transfers between devices: 2.87 us -> 0.02 us
  local copies, waits for them, and re-layouts: 3.98 us -> 2.03 us
  other arithmetic: 0.73 us -> 0 us
    pallas_call x1, Pallas kernels: 14.6 us -> 7.91 us  [finish(): pl.pallas_call(finish_kernel, out_shape=[FIELD] * 3 + [jax.ShapeDtypeStru...]
    pallas_call x2 -> x6, Pallas kernels: 22.7 us -> 19.7 us  [the longest x1 8.76 us: interior(): pl.pallas_call(interior_kernel, out_shape=[FIELD] * 7 + [rows, rows, jax....]
    ppermute x6, waiting for transfers between devices: 2.86 us -> 0.02 us  [the longest x4 0.01 us: sum_along(): other = lax.ppermute(x, 'along', [(p, p ^ steps[i]) for p in range(size)])]
    unnamed x14 -> x6, local copies, waits for them, and re-layouts: 3.97 us -> 2.03 us
    pallas_call x1, Pallas kernels: 6 us -> 5.03 us  [bands(): pl.pallas_call(bands_kernel, out_shape=[FIELD] * 3 + [MASK, jax.ShapeDtyp...]
  transfers between devices with their start and end apart: 8 -> 8, of which waited for: 2 -> 0; matrix products, arithmetic and copies ran while one was open for 1% -> 0% of each run, Pallas kernels for 52% -> 49%
where the time goes in v1:
time: 57.2 us; the launch traced here: 56.3 us
  Pallas kernels  35.2 us (62%)
  starting transfers between devices  18.3 us (32%)
  local copies, waits for them, and re-layouts  2.03 us (4%)
  between operations  0.82 us (1%)
    ppermute x4, starting transfers between devices, sum_along(): other = lax.ppermute(x, 'along', [(p, p ^ steps[i]) for p in range(size)])  10.3 us
    pallas_call x1, Pallas kernels, interior(): pl.pallas_call(interior_kernel, out_shape=[FIELD] * 7 + [rows, rows, jax....  8.76 us
    pallas_call x1, Pallas kernels, finish(): pl.pallas_call(finish_kernel, out_shape=[FIELD] * 3 + [jax.ShapeDtypeStru...  7.91 us
    pallas_call x1, Pallas kernels, bands(): pl.pallas_call(bands_kernel, out_shape=[FIELD] * 3 + [MASK, jax.ShapeDtyp...  5.03 us
    pallas_call x2, Pallas kernels, adjoint(): pl.pallas_call(functools.partial(adjoint_kernel, first, last), out_shape=...  4.18 us
    pallas_call x1, Pallas kernels, scatter(): pl.pallas_call(scatter_kernel, out_shape=[FIELD] * 3, in_specs=[VM] * 4 +...  3.32 us
    ppermute x1, starting transfers between devices, local(): above = lax.ppermute(pay, 'along', later).reshape(-1)  3.03 us
    ppermute x1, starting transfers between devices, local(): above = lax.ppermute(down, 'along', later)  2.39 us
  transfers between devices with their start and end apart: 8, of which 0 were waited for; matrix products, arithmetic and copies ran while one was open for 0% of the time, Pallas kernels for 49%

profile of v1, /device:TPU:0, one launch (start us, length us, event | category | flops | bytes accessed | tf_op | source)
XLA Modules:
  0.0 56.3 jit_solution(1846176888266449581)
XLA Ops:
  0.6 1.9 %edges.1 = (f32[8,40,16,128]{3,2,1,0:T(8,128)S(1)}, f32[984,128]{1,0:T(8,128)S(1)}, f32[984,128]{1,0:T(8,128)S(1)}, f32[176,128]{1,0:T(8,128)S(1)}) custom-call(f32[40,16,1024]{2,1,0:T(8,128)} %basic.1, s32[16,1024]{1,0:T(8,128)} %land_at.1), custom_call_target="tpu_custom_call" | custom-call | bytes 6000000 | tf_op jit(solution)/shard_map/edges/pallas_call | solution.py:148
  2.5 2.4 %collective-permute-start = (f32[984,128]{1,0:T(8,128)S(1)}, f32[984,128]{1,0:T(8,128)S(1)}, u32[]{:S(2)}, u32[]{:S(2)}) collective-permute-start(f32[984,128]{1,0:T(8,128)S(1)} %get-tuple-element.60), channel_id=1, source_target_pairs={{0,1},{1,2},{2,3},{3,4},{4,5},{5,6},{6,7},{7,8},{8,9},{9,10},{10,1... | collective-permute-start | bytes 1511432 | tf_op jit(solution)/shard_map/ppermute | solution.py:546
  4.9 1.3 %collective-permute-start.1 = (f32[984,128]{1,0:T(8,128)S(1)}, f32[984,128]{1,0:T(8,128)S(1)}, u32[]{:S(2)}, u32[]{:S(2)}) collective-permute-start(f32[984,128]{1,0:T(8,128)S(1)} %get-tuple-element.61), channel_id=1, source_target_pairs={{1,0},{2,1},{3,2},{4,3},{5,4},{6,5},{7,6},{8,7},{9,8},{10,9},{11,1... | collective-permute-start | bytes 1511432 | tf_op jit(solution)/shard_map/ppermute | solution.py:547
  6.2 0.0 copy-start
  6.2 0.7 %copy-done = s32[1,3,512]{2,0,1:T(1,128)S(1)} copy-done((s32[1,3,512]{2,0,1:T(1,128)S(1)}, s32[1,3,512]{2,0,1:T(1,128)}, u32[]{:S(2)}) %copy-start) | copy-done | bytes 6168
  6.9 0.0 copy-start.1
  6.9 0.7 %copy-done.1 = f32[1,3,512]{2,0,1:T(1,128)S(1)} copy-done((f32[1,3,512]{2,0,1:T(1,128)S(1)}, f32[1,3,512]{2,0,1:T(1,128)}, u32[]{:S(2)}) %copy-start.1) | copy-done | bytes 6168
  7.6 0.0 copy-start.2
  7.6 0.7 %copy-done.2 = s32[1,3]{1,0:T(1,128)S(1)} copy-done((s32[1,3]{1,0:T(1,128)S(1)}, s32[1,3]{1,0:T(1,128)}, u32[]{:S(2)}) %copy-start.2) | copy-done | bytes 36
  8.2 1.9 %order.1 = (s32[3,1,512]{2,1,0:T(1,128)S(1)}, f32[3,1,512]{2,1,0:T(1,128)}, f32[3,1,512]{2,1,0:T(1,128)S(1)}, f32[3,1,512]{2,1,0:T(1,128)S(1)}, s32[3,1,512]{2,1...) custom-call(s32[3,1,512]{2,1,0:T(1,128)S(1)} %bitcast.7, s32[1,3]{1,0:T(1,128)S(1)} %copy-done.2, ...), custom_call_target="tpu_custom_call" | custom-call | bytes 6000000 | tf_op jit(solution)/shard_map/order/pallas_call | solution.py:226
  10.1 8.8 %interior.1 = (f32[7040,128]{1,0:T(8,128)S(1)}, f32[7040,128]{1,0:T(8,128)S(1)}, f32[7040,128]{1,0:T(8,128)S(1)}, f32[7040,128]{1,0:T(8,128)S(1)}, f32[7040,128]...) custom-call(f32[8,40,16,128]{3,2,1,0:T(8,128)S(1)} %get-tuple-elemen, ...), custom_call_target="tpu_custom_call" | custom-call | bytes 27000000 | tf_op jit(solution)/shard_map/interior/pallas_call | solution.py:292
  18.9 0.0 collective-permute-done.above
  18.9 0.0 collective-permute-done.1.below
  18.9 5.0 %bands.1 = (f32[7040,128]{1,0:T(8,128)S(1)}, f32[7040,128]{1,0:T(8,128)S(1)}, f32[7040,128]{1,0:T(8,128)S(1)}, f32[176,128]{1,0:T(8,128)S(1)}, f32[8,128]{1,0:T(...) custom-call(f32[7040,128]{1,0:T(8,128)S(1)} %get-tuple-element.50.y0, ...), custom_call_target="tpu_custom_call", output_to_operand_aliasing={{0}: (0, {}), {1}: (1, {}), {2}: (2, {}), {3}: (4, {})} | custom-call | bytes 15000000 | tf_op jit(solution)/shard_map/bands/pallas_call | solution.py:352
  23.9 3.3 %collective-permute-start.2 = (f32[8,128]{1,0:T(8,128)S(1)}, f32[8,128]{1,0:T(8,128)S(1)}, u32[]{:S(2)}, u32[]{:S(2)}) collective-permute-start(f32[8,128]{1,0:T(8,128)S(1)} %get-tuple-element.65.a), channel_id=1, source_target_pairs={{0,1},{1,0},{2,3},{3,2},{4,5},{5,4},{6,7},{7,6},{8,9},{9,8},{10,11... | collective-permute-start | bytes 12296 | tf_op jit(solution)/shard_map/ppermute | solution.py:533
  27.2 1.3 %collective-permute-start.6 = (f32[32,128]{1,0:T(8,128)S(1)}, f32[32,128]{1,0:T(8,128)S(1)}, u32[]{:S(2)}, u32[]{:S(2)}) collective-permute-start(f32[32,128]{1,0:T(8,128)S(1)} %get-tuple-element.85), channel_id=1, source_target_pairs={{1,0},{2,1},{3,2},{4,3},{5,4},{6,5},{7,6},{8,7},{9,8},{10,9},{11,1... | collective-permute-start | bytes 49160 | tf_op jit(solution)/shard_map/ppermute | solution.py:554
  28.5 3.0 %collective-permute-start.5 = (f32[32,128]{1,0:T(8,128)S(1)}, f32[32,128]{1,0:T(8,128)S(1)}, u32[]{:S(2)}, u32[]{:S(2)}) collective-permute-start(f32[32,128]{1,0:T(8,128)S(1)} %get-tuple-element.85), channel_id=1, source_target_pairs={{0,1},{1,2},{2,3},{3,4},{4,5},{5,6},{6,7},{7,8},{8,9},{9,10},{10,1... | collective-permute-start | bytes 49160 | tf_op jit(solution)/shard_map/ppermute | solution.py:553
  31.6 3.3 %scatter.1 = (f32[7040,128]{1,0:T(8,128)S(1)}, f32[7040,128]{1,0:T(8,128)S(1)}, f32[7040,128]{1,0:T(8,128)S(1)}) custom-call(f32[7040,128]{1,0:T(8,128)S(1)} %get-tuple-element.66.f1i, f32[7040,128]{1,0:T(8,128)S(1)} %get-tuple-element.67.f2i, f32[7040,128]{1,0:T(8,128)S(1)} %get-tuple-element.68.f3i, ...), custom_call_target="tpu_custom_call", output_to_operand_aliasing={{0}: (0, {}), {1}: (1, {}), {2}: (2, {})} | custom-call | bytes 9000000 | tf_op jit(solution)/shard_map/scatter/pallas_call | solution.py:388
  34.9 0.0 collective-permute-done.2.b
  34.9 1.7 %collective-permute-start.3 = (f32[8,128]{1,0:T(8,128)S(1)}, f32[8,128]{1,0:T(8,128)S(1)}, u32[]{:S(2)}, u32[]{:S(2)}) collective-permute-start(f32[8,128]{1,0:T(8,128)S(1)} %add.3.a), channel_id=1, source_target_pairs={{0,2},{1,3},{2,0},{3,1},{4,6},{5,7},{6,4},{7,5},{8,10},{9,11},{10,... | collective-permute-start | bytes 12296 | tf_op jit(solution)/shard_map/ppermute | solution.py:533
  36.6 2.3 %adjoint.2.src.f2i = f32[7040,128]{1,0:T(8,128)S(1)} custom-call(f32[7040,128]{1,0:T(8,128)S(1)} %get-tuple-element.84.src.f3i, f32[7040,128]{1,0:T(8,128)S(1)} %get-tuple-element.64.state.y2, f32[7040,128]{1,0:T(8,128)S(1)} %get-tuple-element.76.forcing, f32[176,128]{1,0:T(8,128)S(1)} %get-tuple-element.77.mask), custom_call_target="tpu_custom_call", output_to_operand_aliasing={{}: (2, {})} | custom-call | bytes 6000000 | tf_op jit(solution)/shard_map/adjoint/pallas_call | solution.py:406
  38.9 0.0 collective-permute-done.3.b
  38.9 2.6 %collective-permute-start.4 = (f32[8,128]{1,0:T(8,128)S(1)}, f32[8,128]{1,0:T(8,128)S(1)}, u32[]{:S(2)}, u32[]{:S(2)}) collective-permute-start(f32[8,128]{1,0:T(8,128)S(1)} %add.4.a), channel_id=1, source_target_pairs={{0,4},{1,5},{2,6},{3,7},{4,0},{5,1},{6,2},{7,3},{8,12},{9,13},{10,... | collective-permute-start | bytes 12296 | tf_op jit(solution)/shard_map/ppermute | solution.py:533
  41.6 1.9 %adjoint.3.f1.f1i = f32[7040,128]{1,0:T(8,128)S(1)} custom-call(f32[7040,128]{1,0:T(8,128)S(1)} %adjoint.2.src.f2i, f32[7040,128]{1,0:T(8,128)S(1)} %get-tuple-element.63.state.y1, f32[7040,128]{1,0:T(8,128)S(1)} %get-tuple-element.80.forcing, f32[176,128]{1,0:T(8,128)S(1)} %get-tuple-element.77.mask), custom_call_target="tpu_custom_call", output_to_operand_aliasing={{}: (2, {})} | custom-call | bytes 6000000 | tf_op jit(solution)/shard_map/adjoint/pallas_call | solution.py:406
  43.5 0.0 collective-permute-done.4.b
  43.5 2.7 %collective-permute-start.7 = (f32[8,128]{1,0:T(8,128)S(1)}, f32[8,128]{1,0:T(8,128)S(1)}, u32[]{:S(2)}, u32[]{:S(2)}) collective-permute-start(f32[8,128]{1,0:T(8,128)S(1)} %add.5.a), channel_id=1, source_target_pairs={{0,8},{1,9},{2,10},{3,11},{4,12},{5,13},{6,14},{7,15},{8,0},{9,1},... | collective-permute-start | bytes 12296 | tf_op jit(solution)/shard_map/ppermute | solution.py:533
  46.2 1.6 %middle.1.gradi = f32[5120,128]{1,0:T(8,128)S(1)} custom-call(f32[7040,128]{1,0:T(8,128)S(1)} %adjoint.3.f1.f1i, f32[7040,128]{1,0:T(8,128)S(1)} %get-tuple-element.62.y0), custom_call_target="tpu_custom_call" | custom-call | bytes 6000000 | tf_op jit(solution)/shard_map/middle/pallas_call | solution.py:423
  47.8 0.0 collective-permute-done.6
  47.8 0.0 collective-permute-done.5
  47.8 7.9 %finish.1 = (f32[7040,128]{1,0:T(8,128)S(1)}, f32[7040,128]{1,0:T(8,128)S(1)}, f32[7040,128]{1,0:T(8,128)S(1)}, f32[5120,128]{1,0:T(8,128)S(1)}, f32[40,16,1024]{2,1,0:T(8,128)}) custom-call(f32[7040,128]{1,0:T(8,128)S(1)} %get-tuple-element.62.y0, ...), custom_call_target="tpu_custom_call", output_to_operand_aliasing={{0}: (3, {}), {1}: (4, {}), {2}: (5, {}), {3}: (7, {})} | custom-call | bytes 18000000 | tf_op jit(solution)/shard_map/finish/pallas_call | solution.py:483
  55.7 0.0 collective-permute-done.7.b
  55.7 0.6 %reduce.1 = f32[1,1]{1,0:T(1,128)} custom-call(f32[8,128]{1,0:T(8,128)S(1)} %add.5.a, f32[8,128]{1,0:T(8,128)S(1)} %collective-permute-done.7.b), custom_call_target="tpu_custom_call" | custom-call | bytes 300000 | tf_op jit(solution)/shard_map/reduce/pallas_call | solution.py:510
  (3 shorter events, 0.0 us)
Async XLA Ops:
  2.5 16.4 %collective-permute-start = (f32[984,128]{1,0:T(8,128)S(1)}, f32[984,128]{1,0:T(8,128)S(1)}, u32[]{:S(2)}, u32[]{:S(2)}) collective-permute-start(f32[984,128]{1,0:T(8,128)S(1)} %get-tuple-element.60), channel_id=1, source_target_pairs={{0,1},{1,2},{2,3},{3,4},{4,5},{5,6},{6,7},{7,8},{8,9},{9,10},{10,1... | collective-permute-start | bytes 1511432 | tf_op jit(solution)/shard_map/ppermute | solution.py:546
  4.9 14.0 %collective-permute-start.1 = (f32[984,128]{1,0:T(8,128)S(1)}, f32[984,128]{1,0:T(8,128)S(1)}, u32[]{:S(2)}, u32[]{:S(2)}) collective-permute-start(f32[984,128]{1,0:T(8,128)S(1)} %get-tuple-element.61), channel_id=1, source_target_pairs={{1,0},{2,1},{3,2},{4,3},{5,4},{6,5},{7,6},{8,7},{9,8},{10,9},{11,1... | collective-permute-start | bytes 1511432 | tf_op jit(solution)/shard_map/ppermute | solution.py:547
  6.2 0.7 %copy-start = (s32[1,3,512]{2,0,1:T(1,128)S(1)}, s32[1,3,512]{2,0,1:T(1,128)}, u32[]{:S(2)}) copy-start(s32[1,3,512]{2,0,1:T(1,128)} %param.7) | copy-start | bytes 18436
  6.9 0.7 %copy-start.1 = (f32[1,3,512]{2,0,1:T(1,128)S(1)}, f32[1,3,512]{2,0,1:T(1,128)}, u32[]{:S(2)}) copy-start(f32[1,3,512]{2,0,1:T(1,128)} %param.9) | copy-start | bytes 18436
  7.6 0.7 %copy-start.2 = (s32[1,3]{1,0:T(1,128)S(1)}, s32[1,3]{1,0:T(1,128)}, u32[]{:S(2)}) copy-start(s32[1,3]{1,0:T(1,128)} %count.1) | copy-start | bytes 40
  23.9 11.0 %collective-permute-start.2 = (f32[8,128]{1,0:T(8,128)S(1)}, f32[8,128]{1,0:T(8,128)S(1)}, u32[]{:S(2)}, u32[]{:S(2)}) collective-permute-start(f32[8,128]{1,0:T(8,128)S(1)} %get-tuple-element.65.a), channel_id=1, source_target_pairs={{0,1},{1,0},{2,3},{3,2},{4,5},{5,4},{6,7},{7,6},{8,9},{9,8},{10,11... | collective-permute-start | bytes 12296 | tf_op jit(solution)/shard_map/ppermute | solution.py:533
  27.2 20.5 %collective-permute-start.6 = (f32[32,128]{1,0:T(8,128)S(1)}, f32[32,128]{1,0:T(8,128)S(1)}, u32[]{:S(2)}, u32[]{:S(2)}) collective-permute-start(f32[32,128]{1,0:T(8,128)S(1)} %get-tuple-element.85), channel_id=1, source_target_pairs={{1,0},{2,1},{3,2},{4,3},{5,4},{6,5},{7,6},{8,7},{9,8},{10,9},{11,1... | collective-permute-start | bytes 49160 | tf_op jit(solution)/shard_map/ppermute | solution.py:554
  28.5 19.2 %collective-permute-start.5 = (f32[32,128]{1,0:T(8,128)S(1)}, f32[32,128]{1,0:T(8,128)S(1)}, u32[]{:S(2)}, u32[]{:S(2)}) collective-permute-start(f32[32,128]{1,0:T(8,128)S(1)} %get-tuple-element.85), channel_id=1, source_target_pairs={{0,1},{1,2},{2,3},{3,4},{4,5},{5,6},{6,7},{7,8},{8,9},{9,10},{10,1... | collective-permute-start | bytes 49160 | tf_op jit(solution)/shard_map/ppermute | solution.py:553
  34.9 4.0 %collective-permute-start.3 = (f32[8,128]{1,0:T(8,128)S(1)}, f32[8,128]{1,0:T(8,128)S(1)}, u32[]{:S(2)}, u32[]{:S(2)}) collective-permute-start(f32[8,128]{1,0:T(8,128)S(1)} %add.3.a), channel_id=1, source_target_pairs={{0,2},{1,3},{2,0},{3,1},{4,6},{5,7},{6,4},{7,5},{8,10},{9,11},{10,... | collective-permute-start | bytes 12296 | tf_op jit(solution)/shard_map/ppermute | solution.py:533
  38.9 4.6 %collective-permute-start.4 = (f32[8,128]{1,0:T(8,128)S(1)}, f32[8,128]{1,0:T(8,128)S(1)}, u32[]{:S(2)}, u32[]{:S(2)}) collective-permute-start(f32[8,128]{1,0:T(8,128)S(1)} %add.4.a), channel_id=1, source_target_pairs={{0,4},{1,5},{2,6},{3,7},{4,0},{5,1},{6,2},{7,3},{8,12},{9,13},{10,... | collective-permute-start | bytes 12296 | tf_op jit(solution)/shard_map/ppermute | solution.py:533
  43.5 12.2 %collective-permute-start.7 = (f32[8,128]{1,0:T(8,128)S(1)}, f32[8,128]{1,0:T(8,128)S(1)}, u32[]{:S(2)}, u32[]{:S(2)}) collective-permute-start(f32[8,128]{1,0:T(8,128)S(1)} %add.5.a), channel_id=1, source_target_pairs={{0,8},{1,9},{2,10},{3,11},{4,12},{5,13},{6,14},{7,15},{8,0},{9,1},... | collective-permute-start | bytes 12296 | tf_op jit(solution)/shard_map/ppermute | solution.py:533

commit v2 on v1

--- a/solution.py
+++ b/solution.py
@@ -16,7 +16,7 @@
 EDGE = H * COL + H * CT
 CAP = 512
 NT = 3
-PAY = 32
+PAY = 40
 CODE = 16
 
 VM = pl.BlockSpec(memory_space=pltpu.VMEM)
@@ -88,11 +88,13 @@
     return mask[pl.ds(at * CT + c, 8, stride=0), :]
 
 
-def forward_row(src, dst, mask, at):
+def forward_row(src, dst, mask, at, blank=None):
     ms = [mask_row(mask, at, c) for c in range(CT)]
 
     def emit(c, k, v, s, o):
         dst[pl.ds(pl.multiple_of(o, 8), 8), :] = ms[c] * (s + v * (0.6 - v * v))
+        if blank is not None:
+            blank[pl.ds(pl.multiple_of(o, 8), 8), :] = jnp.zeros((8, LN), F32)
 
     stencil_row(src, at, emit)
 
@@ -120,7 +122,11 @@
     lax.fori_loop(first + H, last + H + 1, lambda at, _: (body(at), 0)[1], 0)
 
 
-def edges_kernel(basic, land_at, staged, up, down, mask, land, sems):
+def even():
+    return lax.rem(lax.axis_index("along"), 2) == 0
+
+
+def edges_kernel(basic, land_at, staged, twin, other, mask, land, sems):
     def copy(c):
         return pltpu.make_async_copy(basic.at[:, :, pl.ds(c * LN, LN)], staged.at[c], sems.at[c])
 
@@ -131,10 +137,11 @@
     sea.wait()
     for c in range(CT):
         mask[pl.ds(H * CT + c, ROWS, stride=CT), :] = 0.2 * land[:, pl.ds(c * LN, LN)].astype(F32)
+    lower = jnp.where(even(), ROWS - H, 0)
     for c in range(CT):
         copy(c).wait()
         flat = staged.at[c].reshape(LV * ROWS, LN)
-        for out, first in ((up, 0), (down, ROWS - H)):
+        for out, first in ((twin, lower), (other, ROWS - H - lower)):
             for j in range(H):
                 r = first + j
                 half = 2.5 * mask_row(mask, r + H, c)
@@ -162,7 +169,15 @@
     )(pltpu.with_memory_space_constraint(basic, pltpu.HBM), pltpu.with_memory_space_constraint(land, pltpu.HBM))
 
 
-def order_kernel(cells, count, value, addr, live, sval, lane, spot, second, codes):
+def order_kernel(cells_at, count_at, value_at, addr, sval, lane, spot, second, codes, cells, count, value, sems):
+    fetches = [
+        pltpu.make_async_copy(src, dst, sems.at[i])
+        for i, (src, dst) in enumerate(((cells_at, cells), (count_at, count), (value_at, value)))
+    ]
+    for f in fetches:
+        f.start()
+    for f in fetches:
+        f.wait()
     slot = lax.broadcasted_iota(I32, (1, CAP), 1)
     ups, downs = [], []
     for t in range(NT):
@@ -210,7 +225,6 @@
         spot[t] = where + H * CT
         sval[t] = out[3:4] + out[4:5] + out[5:6]
         lane[t] = jnp.where(alive, (cell & (LN - 1)).astype(F32), -1.0)
-        live[t] = out[6:7]
         if t == NT - 1:
             second[0] = jnp.where(jnp.logical_or(row == 1, row == ROWS - 2), -3.0, 0.0)
         far = jnp.where(row < ROWS // 2, own + ROWS * COL, own - ROWS * COL)
@@ -225,13 +239,19 @@
     ints, floats = jax.ShapeDtypeStruct((NT, 1, CAP), I32), jax.ShapeDtypeStruct((NT, 1, CAP), F32)
     return pl.pallas_call(
         order_kernel,
-        out_shape=[ints, floats, floats, floats, ints, jax.ShapeDtypeStruct((1, 1, CAP), F32), jax.ShapeDtypeStruct((CODE, LN), F32)],
-        in_specs=[VM, SM, VM],
-        out_specs=[VM] * 7,
+        out_shape=[ints, floats, floats, ints, jax.ShapeDtypeStruct((1, 1, CAP), F32), jax.ShapeDtypeStruct((CODE, LN), F32)],
+        in_specs=[HBM] * 3,
+        out_specs=[VM] * 6,
+        scratch_shapes=[
+            pltpu.VMEM((NT, 1, CAP), I32),
+            pltpu.SMEM((1, NT), I32),
+            pltpu.VMEM((NT, 1, CAP), F32),
+            pltpu.SemaphoreType.DMA((3,)),
+        ],
         compiler_params=params(6),
         cost_estimate=cost(2),
         name="order",
-    )(cells, count, value)
+    )(*(pltpu.with_memory_space_constraint(x, pltpu.HBM) for x in (cells, count, value)))
 
 
 def upright(line):
@@ -258,16 +278,13 @@
         for j in range(COL // 8):
             y2[pl.ds(at * COL + j * 8, 8), :] = zero
 
-    def clear(at, _):
-        for f in (f1, f2, f3):
+    for t, f in enumerate((f1, f2, f3)):
+        for at in [*range(H + t + 1), *range(ROWS + H - t - 1, RX)]:
             for j in range(COL // 8):
-                f[pl.ds(pl.multiple_of(at * COL, 8) + j * 8, 8), :] = zero
-        return 0
-
-    lax.fori_loop(0, RX, clear, 0)
-    loop(1, 14, lambda at: forward_row(y0, y1, mask, at))
-    loop(2, 13, lambda at: forward_row(y1, y2, mask, at))
-    loop(3, 12, lambda at: forward_row(y2, y3, mask, at))
+                f[pl.ds(at * COL + j * 8, 8), :] = zero
+    loop(1, 14, lambda at: forward_row(y0, y1, mask, at, f1))
+    loop(2, 13, lambda at: forward_row(y1, y2, mask, at, f2))
+    loop(3, 12, lambda at: forward_row(y2, y3, mask, at, f3))
     ids = lax.broadcasted_iota(I32, (LN, LN), 1).astype(F32)
     for t in range(NT):
         for q in range(CAP // LN):
@@ -301,16 +318,18 @@
     )(staged, mask, lane, sval, spots)
 
 
-def bands_kernel(y0i, y1i, y2i, y3, maski, twice, known, sea, second, codes, addrs, above, below,
-                 y0, y1, y2, mask, total, pay, terms, g1, g2, g3, g4, at_ref, sem):
+def bands_kernel(y0i, y1i, y2i, y3, maski, twice, known, sea, second, codes, addrs, twin, other,
+                 y0, y1, y2, mask, pay, terms, g1, g2, g3, g4, at_ref, sem):
     fetch = Fetch(addrs, at_ref, sem)
     fetch.start()
-    for halo, first in ((above, 0), (below, ROWS + H)):
+    lower = jnp.where(even(), ROWS + H, 0)
+    for halo, first in ((twin, lower), (other, ROWS + H - lower)):
+        base = pl.multiple_of(first * COL, 8)
+        for q in range(H * COL // 8):
+            y0[pl.ds(base + q * 8, 8), :] = halo[pl.ds(q * 8, 8), :]
+        base = pl.multiple_of(first * CT, 8)
         for j in range(H):
-            base = (first + j) * COL
-            for q in range(COL // 8):
-                y0[pl.ds(base + q * 8, 8), :] = halo[pl.ds(j * COL + q * 8, 8), :]
-            mask[pl.ds((first + j) * CT, CT), :] = halo[pl.ds(H * COL + j * CT, CT), :]
+            mask[pl.ds(base + j * CT, CT), :] = halo[pl.ds(H * COL + j * CT, CT), :]
     for src, dst, reach in ((y0, y1, 2), (y1, y2, 1), (y2, y3, 0)):
         loop(-reach, 2 - reach, lambda at: forward_row(src, dst, mask, at))
         loop(ROWS - 3 + reach, ROWS - 1 + reach, lambda at: forward_row(src, dst, mask, at))
@@ -344,7 +363,7 @@
             terms[rows, :] = d
             pay[pl.ds(4 * t + q, 1), :] = jnp.sum(d.T, axis=0, keepdims=True)
     pay[pl.ds(CODE, CODE), :] = codes[...]
-    total[...] = acc
+    pay[pl.ds(2 * CODE, 8), :] = acc
 
 
 def bands(y0, y1, y2, y3, mask, twice, known, sea, second, codes, addrs, above, below):
@@ -354,12 +373,11 @@
         out_shape=[FIELD] * 3
         + [
             MASK,
-            jax.ShapeDtypeStruct((8, LN), F32),
             jax.ShapeDtypeStruct((PAY, LN), F32),
             jax.ShapeDtypeStruct((NT * CAP, LN), F32),
         ],
         in_specs=[VM] * 10 + [ANY] + [VM] * 2,
-        out_specs=[VM] * 7,
+        out_specs=[VM] * 6,
         input_output_aliases={0: 0, 1: 1, 2: 2, 4: 3},
         scratch_shapes=[rows, rows, rows, rows, pltpu.SMEM((NT * CAP,), I32), pltpu.SemaphoreType.DMA((NT,))],
         compiler_params=params(4),
@@ -431,32 +449,60 @@
     )(f1, y0)
 
 
-def finish_kernel(y0, y1, y2, f1i, f2i, f3i, mask, gradi, above, below, f1, f2, f3, grad, out, staged, a_ref, b_ref, sems):
-    fetches = [pltpu.make_async_copy(src, dst, sems.at[CT + i]) for i, (src, dst) in enumerate(((above, a_ref), (below, b_ref)))]
-    for f in fetches:
-        f.start()
-    for f in fetches:
+def finish_kernel(scale, y0, y1, y2, f1i, f2i, f3i, mask, gradi, twin, other, x, y, f1, f2, f3, grad, out, misfit,
+                  staged, a_ref, b_ref, ca, cb, sems):
+    misfit[...] = jnp.sum(x[...] + y[...], keepdims=True) * scale
+
+    def fetches(above, below):
+        return [pltpu.make_async_copy(src, dst, sems.at[CT + i]) for i, (src, dst) in enumerate(((above, a_ref), (below, b_ref)))]
+
+    @pl.when(even())
+    def _():
+        for f in fetches(other, twin):
+            f.start()
+
+    @pl.when(jnp.logical_not(even()))
+    def _():
+        for f in fetches(twin, other):
+            f.start()
+
+    for q in range(COL // 8):
+        for buf in (ca, cb):
+            buf[pl.ds(q * 8, 8), :] = jnp.zeros((8, LN), F32)
+    for f in fetches(twin, other):
         f.wait()
-    counts = 2 * CODE * LN - (CODE - 12) * LN
+    counts = CODE * LN + 12 * LN
     lane = lax.broadcasted_iota(I32, (1, LN), 1)
     na = [a_ref[counts + NT + t].astype(I32) for t in range(NT)]
     nb = [b_ref[counts + t].astype(I32) for t in range(NT)]
-    most = na[0]
-    for n in na[1:] + nb:
-        most = jnp.maximum(most, n)
-
-    def item(j, _):
+    most = 0
+    for t in range(NT):
+        most = jnp.maximum(most, (jnp.maximum(na[t], nb[t]) + t) // (t + 1))
+
+    def item(i, _):
         for t, f in ((2, f3), (1, f2), (0, f1)):
-            for ref, n, slot in ((a_ref, na[t], CAP - 1 - j), (b_ref, nb[t], j)):
-                code = ref[CODE * LN + t * CAP + slot].astype(I32)
-                hit = lane == jnp.where(j < n, code & (LN - 1), -1)
-                spot = pl.ds(code >> 7, 1)
-                f[spot, :] = f[spot, :] + jnp.where(hit, ref[t * CAP + slot], 0.0)
-                if t == NT - 1:
-                    f2[spot, :] = f2[spot, :] + jnp.where(hit, ref[12 * LN + slot], 0.0)
+            for u in range(t + 1):
+                j = i * (t + 1) + u
+                slot_of = jnp.minimum(j, CAP - 1)
+                for ref, n, slot, side in ((a_ref, na[t], CAP - 1 - slot_of, ca), (b_ref, nb[t], slot_of, cb)):
+                    code = ref[CODE * LN + t * CAP + slot].astype(I32)
+                    hit = lane == jnp.where(j < n, code & (LN - 1), -1)
+                    addr = code >> 7
+                    spot = pl.ds(addr, 1)
+                    f[spot, :] = f[spot, :] + jnp.where(hit, ref[t * CAP + slot], 0.0)
+                    if t == NT - 1:
+                        start = (1 if side is ca else ROWS + H + 1) * COL
+                        far = addr - start
+                        inside = jnp.logical_and(far >= 0, far < COL)
+                        spot = pl.ds(jnp.where(inside, far, 0), 1)
+                        side[spot, :] = side[spot, :] + jnp.where(hit, ref[12 * LN + slot], 0.0)
         return 0
 
     lax.fori_loop(0, most, item, 0)
+    for side, at in ((ca, 1), (cb, ROWS + H + 1)):
+        for q in range(COL // 8):
+            spot = pl.ds(at * COL + q * 8, 8)
+            f2[spot, :] = f2[spot, :] + side[pl.ds(q * 8, 8), :]
     for src, state, dst, reach in ((f3, y2, f2, 2), (f2, y1, f1, 1)):
         loop(-reach, 2 - reach, lambda at: adjoint_row(src, state, dst, mask, at))
         loop(ROWS - 3 + reach, ROWS - 1 + reach, lambda at: adjoint_row(src, state, dst, mask, at))
@@ -479,87 +525,91 @@
         copy(c).wait()
 
 
-def finish(y0, y1, y2, f1, f2, f3, mask, grad, above, below):
-    return pl.pallas_call(
-        finish_kernel,
-        out_shape=[FIELD] * 3 + [jax.ShapeDtypeStruct((ROWS * COL, LN), F32), jax.ShapeDtypeStruct((LV, ROWS, CT * LN), F32)],
-        in_specs=[VM] * 8 + [ANY] * 2,
-        out_specs=[VM] * 4 + [ANY],
+def finish(y0, y1, y2, f1, f2, f3, mask, grad, twin, other, x, y, scale):
+    return pl.pallas_call(
+        functools.partial(finish_kernel, scale),
+        out_shape=[FIELD] * 3
+        + [
+            jax.ShapeDtypeStruct((ROWS * COL, LN), F32),
+            jax.ShapeDtypeStruct((LV, ROWS, CT * LN), F32),
+            jax.ShapeDtypeStruct((1, 1), F32),
+        ],
+        in_specs=[VM] * 8 + [ANY] * 2 + [VM] * 2,
+        out_specs=[VM] * 4 + [ANY, VM],
         input_output_aliases={3: 0, 4: 1, 5: 2, 7: 3},
         scratch_shapes=[
             pltpu.VMEM((CT, LV, ROWS, LN), F32),
             pltpu.SMEM((PAY * LN,), F32),
             pltpu.SMEM((PAY * LN,), F32),
+            pltpu.VMEM((COL, LN), F32),
+            pltpu.VMEM((COL, LN), F32),
             pltpu.SemaphoreType.DMA((CT + 2,)),
         ],
         compiler_params=params(6),
         cost_estimate=cost(6),
         name="finish",
-    )(y0, y1, y2, f1, f2, f3, mask, grad, above, below)[4]
-
-
-def add_kernel(a, b, out):
-    out[...] = a[...] + b[...]
-
-
-def reduce_kernel(scale, a, b, out):
-    out[...] = jnp.sum(a[...] + b[...], keepdims=True) * scale
-
-
-def small(kernel, shape, a, b, name):
-    return pl.pallas_call(
-        kernel,
-        out_shape=jax.ShapeDtypeStruct(shape, F32),
+    )(y0, y1, y2, f1, f2, f3, mask, grad, twin, other, x, y)[4:]
+
+
+def add_kernel(first, pay, twin, out):
+    out[...] = pay[pl.ds(first, 8), :] + twin[pl.ds(first, 8), :]
+
+
+def add(first, a, b):
+    return pl.pallas_call(
+        functools.partial(add_kernel, first),
+        out_shape=jax.ShapeDtypeStruct((8, LN), F32),
         in_specs=[VM, VM],
         out_specs=VM,
         compiler_params=params(1),
         cost_estimate=cost(0.1),
-        name=name,
+        name="add",
     )(a, b)
 
 
-def sum_along(x, stages, scale):
+def sum_along(pay, twin, stages):
     size = lax.axis_size("along")
-    steps = [1 << i for i in range(size.bit_length() - 1)]
-    held = ()
+    steps = [1 << i for i in range(1, size.bit_length() - 1)]
+    held = stages[0]()
+    x = add(2 * CODE, pay, twin)
+    other = jnp.zeros_like(x)
     if size & (size - 1):
-        x, steps = lax.psum(x, "along"), []
-    other = jnp.zeros_like(x)
-    for i in range(max(len(steps), len(stages))):
+        x, steps = lax.psum(0.5 * x, "along"), []
+    for i in range(max(len(steps), len(stages) - 1)):
         if i < len(steps):
             if i > 0:
-                x = small(add_kernel, x.shape, x, other, "add")
-                x, held = lax.optimization_barrier((x, held))
+                x = add(0, x, other)
+            x, held = lax.optimization_barrier((x, held))
             other = lax.ppermute(x, "along", [(p, p ^ steps[i]) for p in range(size)])
-        if i < len(stages):
-            held = stages[i](*held)
-    return small(functools.partial(reduce_kernel, scale), (1, 1), x, other, "reduce").reshape(1), held
+        if i + 1 < len(stages):
+            held = stages[i + 1](*held)
+    return x, other, held
 
 
 def local(basic_state, land_sea, obs_cells, obs_count, obs_value):
     size = lax.axis_size("along")
-    later = [(i, i + 1) for i in range(size - 1)]
-    earlier = [(i + 1, i) for i in range(size - 1)]
+    twins = [(i, i ^ 1) for i in range(size)]
+    others = [(i, i - 1 if i % 2 == 0 else i + 1) for i in range(1, size - 1)]
     cells = obs_cells.transpose(1, 0, 2)
     value = obs_value.transpose(1, 0, 2)
-    staged, up, down, mask = edges(basic_state, land_sea)
-    above = lax.ppermute(down, "along", later)
-    below = lax.ppermute(up, "along", earlier)
-    addrs, _, sval, lane, spots, second, codes = order(cells, obs_count, value)
+    staged, twin, other, mask = edges(basic_state, land_sea)
+    other = lax.ppermute(other, "along", others)
+    twin = lax.ppermute(twin, "along", twins)
+    addrs, sval, lane, spots, second, codes = order(cells, obs_count, value)
     y0, y1, y2, y3, f1, f2, f3, twice, known, sea = interior(staged, mask, lane, sval, spots)
-    y0, y1, y2, mask, total, pay, terms = bands(
-        y0, y1, y2, y3, mask, twice, known, sea, second, codes, addrs, above, below
-    )
-    above = lax.ppermute(pay, "along", later).reshape(-1)
-    below = lax.ppermute(pay, "along", earlier).reshape(-1)
+    y0, y1, y2, mask, pay, terms = bands(y0, y1, y2, y3, mask, twice, known, sea, second, codes, addrs, twin, other)
+    other = lax.ppermute(pay, "along", others)
+    twin = lax.ppermute(pay, "along", twins)
     stages = (
         lambda: scatter(f1, f2, f3, terms, addrs),
         lambda a, b, c: (a, adjoint(1, 14, c, y2, b, mask), c),
         lambda a, b, c: (adjoint(2, 13, b, y1, a, mask), b, c),
         lambda a, b, c: (a, b, c, middle(a, y0)),
     )
-    misfit, held = sum_along(total, stages, 1.0 / (2.0 * size * obs_cells.shape[1] * obs_cells.shape[2]))
-    gradient = finish(y0, y1, y2, *held[:3], mask, held[3], above, below)
+    x, y, held = sum_along(pay, twin, stages)
+    scale = 1.0 / (2.0 * size * obs_cells.shape[1] * obs_cells.shape[2])
+    gradient, misfit = finish(y0, y1, y2, *held[:3], mask, held[3], twin.reshape(-1), other.reshape(-1), x, y, scale)
+    misfit = misfit.reshape(1)
     return gradient, misfit
 
 

time: 57.2 us -> 53 us (0.927); the launches traced: 56.3 us -> 52.8 us
  local copies, waits for them, and re-layouts: 2.03 us -> 0 us
  starting transfers between devices: 18.3 us -> 16.3 us
    unnamed x6 -> x0, local copies, waits for them, and re-layouts: 2.03 us -> none
    ppermute x4 -> x3, starting transfers between devices: 10.3 us -> 9.25 us  [sum_along(): other = lax.ppermute(x, 'along', [(p, p ^ steps[i]) for p in range(size)])]
    ppermute x4, starting transfers between devices: 7.99 us -> 7.04 us  [the longest x1 5.19 us: local(): twin = lax.ppermute(pay, 'along', twins)]
    pallas_call x6 -> x5, Pallas kernels: 10.4 us -> 11.1 us  [the longest x1 9.49 us: finish(): pl.pallas_call(functools.partial(finish_kernel, scale), out_shape=[FIELD]...]
  transfers between devices with their start and end apart: 8 -> 7, of which waited for: 0 -> 1; matrix products, arithmetic and copies ran while one was open for 0% -> 0% of each run, Pallas kernels for 49% -> 36%
where the time goes in v2:
time: 53 us; the launch traced here: 52.8 us
  Pallas kernels  35.5 us (67%)
  starting transfers between devices  16.3 us (31%)
  between operations  0.78 us (1%)
    pallas_call x1, Pallas kernels, finish(): pl.pallas_call(functools.partial(finish_kernel, scale), out_shape=[FIELD]...  9.49 us
    ppermute x3, starting transfers between devices, sum_along(): other = lax.ppermute(x, 'along', [(p, p ^ steps[i]) for p in range(size)])  9.25 us
    pallas_call x1, Pallas kernels, interior(): pl.pallas_call(interior_kernel, out_shape=[FIELD] * 7 + [rows, rows, jax....  8.41 us
    ppermute x1, starting transfers between devices, local(): twin = lax.ppermute(pay, 'along', twins)  5.19 us
    pallas_call x1, Pallas kernels, bands(): pl.pallas_call(bands_kernel, out_shape=[FIELD] * 3 + [MASK, jax.ShapeDtyp...  5.01 us
    pallas_call x2, Pallas kernels, adjoint(): pl.pallas_call(functools.partial(adjoint_kernel, first, last), out_shape=...  4.18 us
    pallas_call x1, Pallas kernels, scatter(): pl.pallas_call(scatter_kernel, out_shape=[FIELD] * 3, in_specs=[VM] * 4 +...  3.32 us
    pallas_call x1, Pallas kernels, edges(): pl.pallas_call(edges_kernel, out_shape=[jax.ShapeDtypeStruct((CT, LV, ROW...  1.87 us
  transfers between devices with their start and end apart: 7, of which 1 were waited for; matrix products, arithmetic and copies ran while one was open for 0% of the time, Pallas kernels for 36%

profile of v2, /device:TPU:0, one launch (start us, length us, event | category | flops | bytes accessed | tf_op | source)
XLA Modules:
  0.0 52.8 jit_solution(3000193116926978693)
XLA Ops:
  0.6 1.9 %edges.1 = (f32[8,40,16,128]{3,2,1,0:T(8,128)S(1)}, f32[984,128]{1,0:T(8,128)S(1)}, f32[984,128]{1,0:T(8,128)S(1)}, f32[176,128]{1,0:T(8,128)S(1)}) custom-call(f32[40,16,1024]{2,1,0:T(8,128)} %basic.1, s32[16,1024]{1,0:T(8,128)} %land_at.1), custom_call_target="tpu_custom_call" | custom-call | bytes 6000000 | tf_op jit(solution)/shard_map/edges/pallas_call | solution.py:155
  2.5 0.5 collective-permute-start
  3.0 0.7 %collective-permute-start.1 = (f32[984,128]{1,0:T(8,128)S(1)}, f32[984,128]{1,0:T(8,128)S(1)}, u32[]{:S(2)}, u32[]{:S(2)}) collective-permute-start(f32[984,128]{1,0:T(8,128)S(1)} %get-tuple-element.61), channel_id=1, source_target_pairs={{1,2},{2,1},{3,4},{4,3},{5,6},{6,5},{7,8},{8,7},{9,10},{10,9},{11,... | collective-permute-start | bytes 1511432 | tf_op jit(solution)/shard_map/ppermute | solution.py:596
  3.7 1.6 %order.1 = (s32[3,1,512]{2,1,0:T(1,128)S(1)}, f32[3,1,512]{2,1,0:T(1,128)S(1)}, f32[3,1,512]{2,1,0:T(1,128)S(1)}, s32[3,1,512]{2,1,0:T(1,128)S(1)}, f32[1,1,512]{2,1,0:T(1,128)S(1)}, /*index=5*/f32[16,128]{1,0:T(8,128)S(1)}) custom-call(s32[3,1,512]{2,1,0:T(1,128)} %bitcast.7, s32[1,3]{1,0:T(1,128)} %count_at.1, f32[3,1,512]{2,1,0:T(1,128)} %bitcast.8), custom_call_target="tpu_custom_call" | custom-call | bytes 6000000 | tf_op jit(solution)/shard_map/order/pallas_call | solution.py:240
  5.3 8.4 %interior.1 = (f32[7040,128]{1,0:T(8,128)S(1)}, f32[7040,128]{1,0:T(8,128)S(1)}, f32[7040,128]{1,0:T(8,128)S(1)}, f32[7040,128]{1,0:T(8,128)S(1)}, f32[7040,128]...) custom-call(f32[8,40,16,128]{3,2,1,0:T(8,128)S(1)} %get-tuple-elemen, ...), custom_call_target="tpu_custom_call" | custom-call | bytes 27000000 | tf_op jit(solution)/shard_map/interior/pallas_call | solution.py:309
  13.7 0.0 collective-permute-done.twin
  13.7 0.0 collective-permute-done.1.other
  13.7 5.0 %bands.1 = (f32[7040,128]{1,0:T(8,128)S(1)}, f32[7040,128]{1,0:T(8,128)S(1)}, f32[7040,128]{1,0:T(8,128)S(1)}, f32[176,128]{1,0:T(8,128)S(1)}, f32[40,128]{1,0:T(8,128)S(1)}, /*index=5*/f32[1536,128]{1,0:T(8,128)S(1)}) custom-call(f32[7040,128]{1,0:T(8,128)S(1)} %get-tuple-element.50.y0i, ...), custom_call_target="tpu_custom_call", output_to_operand_aliasing={{0}: (0, {}), {1}: (1, {}), {2}: (2, {}), {3}: (4, {})} | custom-call | bytes 15000000 | tf_op jit(solution)/shard_map/bands/pallas_call | solution.py:371
  18.8 5.2 %collective-permute-start.2 = (f32[40,128]{1,0:T(8,128)S(1)}, f32[40,128]{1,0:T(8,128)S(1)}, u32[]{:S(2)}, u32[]{:S(2)}) collective-permute-start(f32[40,128]{1,0:T(8,128)S(1)} %get-tuple-element.65.pay), channel_id=1, source_target_pairs={{0,1},{1,0},{2,3},{3,2},{4,5},{5,4},{6,7},{7,6},{8,9},{9,8},{10,11... | collective-permute-start | bytes 61448 | tf_op jit(solution)/shard_map/ppermute | solution.py:602
  23.9 0.7 %collective-permute-start.5 = (f32[40,128]{1,0:T(8,128)S(1)}, f32[40,128]{1,0:T(8,128)S(1)}, u32[]{:S(2)}, u32[]{:S(2)}) collective-permute-start(f32[40,128]{1,0:T(8,128)S(1)} %get-tuple-element.65.pay), channel_id=1, source_target_pairs={{1,2},{2,1},{3,4},{4,3},{5,6},{6,5},{7,8},{8,7},{9,10},{10,9},{11,... | collective-permute-start | bytes 61448 | tf_op jit(solution)/shard_map/ppermute | solution.py:601
  24.6 3.3 %scatter.1 = (f32[7040,128]{1,0:T(8,128)S(1)}, f32[7040,128]{1,0:T(8,128)S(1)}, f32[7040,128]{1,0:T(8,128)S(1)}) custom-call(f32[7040,128]{1,0:T(8,128)S(1)} %get-tuple-element.66.f1i, f32[7040,128]{1,0:T(8,128)S(1)} %get-tuple-element.67.f2i, f32[7040,128]{1,0:T(8,128)S(1)} %get-tuple-element.68.f3i, ...), custom_call_target="tpu_custom_call", output_to_operand_aliasing={{0}: (0, {}), {1}: (1, {}), {2}: (2, {})} | custom-call | bytes 9000000 | tf_op jit(solution)/shard_map/scatter/pallas_call | solution.py:406
  27.9 0.0 collective-permute-done.2.twin
  28.0 3.7 %collective-permute-start.3 = (f32[8,128]{1,0:T(8,128)S(1)}, f32[8,128]{1,0:T(8,128)S(1)}, u32[]{:S(2)}, u32[]{:S(2)}) collective-permute-start(f32[8,128]{1,0:T(8,128)S(1)} %add.3.pay), channel_id=1, source_target_pairs={{0,2},{1,3},{2,0},{3,1},{4,6},{5,7},{6,4},{7,5},{8,10},{9,11},{10,... | collective-permute-start | bytes 12296 | tf_op jit(solution)/shard_map/ppermute | solution.py:583
  31.7 2.3 %adjoint.2.src.f2i = f32[7040,128]{1,0:T(8,128)S(1)} custom-call(f32[7040,128]{1,0:T(8,128)S(1)} %get-tuple-element.84.src.f3i, f32[7040,128]{1,0:T(8,128)S(1)} %get-tuple-element.64.state.y2, f32[7040,128]{1,0:T(8,128)S(1)} %get-tuple-element.76.forcing, f32[176,128]{1,0:T(8,128)S(1)} %get-tuple-element.77.mask), custom_call_target="tpu_custom_call", output_to_operand_aliasing={{}: (2, {})} | custom-call | bytes 6000000 | tf_op jit(solution)/shard_map/adjoint/pallas_call | solution.py:424
  33.9 0.0 collective-permute-done.3.twin
  34.0 2.9 %collective-permute-start.4 = (f32[8,128]{1,0:T(8,128)S(1)}, f32[8,128]{1,0:T(8,128)S(1)}, u32[]{:S(2)}, u32[]{:S(2)}) collective-permute-start(f32[8,128]{1,0:T(8,128)S(1)} %add.4.pay), channel_id=1, source_target_pairs={{0,4},{1,5},{2,6},{3,7},{4,0},{5,1},{6,2},{7,3},{8,12},{9,13},{10,... | collective-permute-start | bytes 12296 | tf_op jit(solution)/shard_map/ppermute | solution.py:583
  36.8 1.9 %adjoint.3.f1.f1i = f32[7040,128]{1,0:T(8,128)S(1)} custom-call(f32[7040,128]{1,0:T(8,128)S(1)} %adjoint.2.src.f2i, f32[7040,128]{1,0:T(8,128)S(1)} %get-tuple-element.63.state.y1, f32[7040,128]{1,0:T(8,128)S(1)} %get-tuple-element.80.forcing, f32[176,128]{1,0:T(8,128)S(1)} %get-tuple-element.77.mask), custom_call_target="tpu_custom_call", output_to_operand_aliasing={{}: (2, {})} | custom-call | bytes 6000000 | tf_op jit(solution)/shard_map/adjoint/pallas_call | solution.py:424
  38.8 0.0 collective-permute-done.4.twin
  38.8 2.7 %collective-permute-start.6 = (f32[8,128]{1,0:T(8,128)S(1)}, f32[8,128]{1,0:T(8,128)S(1)}, u32[]{:S(2)}, u32[]{:S(2)}) collective-permute-start(f32[8,128]{1,0:T(8,128)S(1)} %add.5.x), channel_id=1, source_target_pairs={{0,8},{1,9},{2,10},{3,11},{4,12},{5,13},{6,14},{7,15},{8,0},{9,1},... | collective-permute-start | bytes 12296 | tf_op jit(solution)/shard_map/ppermute | solution.py:583
  41.4 1.6 %middle.1.gradi = f32[5120,128]{1,0:T(8,128)S(1)} custom-call(f32[7040,128]{1,0:T(8,128)S(1)} %adjoint.3.f1.f1i, f32[7040,128]{1,0:T(8,128)S(1)} %get-tuple-element.62.y0), custom_call_target="tpu_custom_call" | custom-call | bytes 6000000 | tf_op jit(solution)/shard_map/middle/pallas_call | solution.py:441
  43.0 0.0 collective-permute-done.5
  43.0 0.3 collective-permute-done.6.y
  43.4 9.5 %finish.1 = (f32[7040,128]{1,0:T(8,128)S(1)}, f32[7040,128]{1,0:T(8,128)S(1)}, f32[7040,128]{1,0:T(8,128)S(1)}, f32[5120,128]{1,0:T(8,128)S(1)}, f32[40,16,1024]{2,1,0:T(8,128)}, /*index=5*/f32[1,1]{1,0:T(1,128)}) custom-call(f32[7040,128]{1,0:T(8,128)S(1)} %get-tuple-element.62.y0, ...), custom_call_target="tpu_custom_call", output_to_operand_aliasing={{0}: (3, {}), {1}: (4, {}), {2}: (5, {}), {3}: (7, {})} | custom-call | bytes 18000000 | tf_op jit(solution)/shard_map/finish/pallas_call | solution.py:529
  (3 shorter events, 0.0 us)
Async XLA Ops:
  2.5 11.2 %collective-permute-start = (f32[984,128]{1,0:T(8,128)S(1)}, f32[984,128]{1,0:T(8,128)S(1)}, u32[]{:S(2)}, u32[]{:S(2)}) collective-permute-start(f32[984,128]{1,0:T(8,128)S(1)} %get-tuple-element.60), channel_id=1, source_target_pairs={{0,1},{1,0},{2,3},{3,2},{4,5},{5,4},{6,7},{7,6},{8,9},{9,8},{10,11... | collective-permute-start | bytes 1511432 | tf_op jit(solution)/shard_map/ppermute | solution.py:597
  3.0 10.7 %collective-permute-start.1 = (f32[984,128]{1,0:T(8,128)S(1)}, f32[984,128]{1,0:T(8,128)S(1)}, u32[]{:S(2)}, u32[]{:S(2)}) collective-permute-start(f32[984,128]{1,0:T(8,128)S(1)} %get-tuple-element.61), channel_id=1, source_target_pairs={{1,2},{2,1},{3,4},{4,3},{5,6},{6,5},{7,8},{8,7},{9,10},{10,9},{11,... | collective-permute-start | bytes 1511432 | tf_op jit(solution)/shard_map/ppermute | solution.py:596
  18.8 9.2 %collective-permute-start.2 = (f32[40,128]{1,0:T(8,128)S(1)}, f32[40,128]{1,0:T(8,128)S(1)}, u32[]{:S(2)}, u32[]{:S(2)}) collective-permute-start(f32[40,128]{1,0:T(8,128)S(1)} %get-tuple-element.65.pay), channel_id=1, source_target_pairs={{0,1},{1,0},{2,3},{3,2},{4,5},{5,4},{6,7},{7,6},{8,9},{9,8},{10,11... | collective-permute-start | bytes 61448 | tf_op jit(solution)/shard_map/ppermute | solution.py:602
  23.9 19.1 %collective-permute-start.5 = (f32[40,128]{1,0:T(8,128)S(1)}, f32[40,128]{1,0:T(8,128)S(1)}, u32[]{:S(2)}, u32[]{:S(2)}) collective-permute-start(f32[40,128]{1,0:T(8,128)S(1)} %get-tuple-element.65.pay), channel_id=1, source_target_pairs={{1,2},{2,1},{3,4},{4,3},{5,6},{6,5},{7,8},{8,7},{9,10},{10,9},{11,... | collective-permute-start | bytes 61448 | tf_op jit(solution)/shard_map/ppermute | solution.py:601
  28.0 6.0 %collective-permute-start.3 = (f32[8,128]{1,0:T(8,128)S(1)}, f32[8,128]{1,0:T(8,128)S(1)}, u32[]{:S(2)}, u32[]{:S(2)}) collective-permute-start(f32[8,128]{1,0:T(8,128)S(1)} %add.3.pay), channel_id=1, source_target_pairs={{0,2},{1,3},{2,0},{3,1},{4,6},{5,7},{6,4},{7,5},{8,10},{9,11},{10,... | collective-permute-start | bytes 12296 | tf_op jit(solution)/shard_map/ppermute | solution.py:583
  34.0 4.8 %collective-permute-start.4 = (f32[8,128]{1,0:T(8,128)S(1)}, f32[8,128]{1,0:T(8,128)S(1)}, u32[]{:S(2)}, u32[]{:S(2)}) collective-permute-start(f32[8,128]{1,0:T(8,128)S(1)} %add.4.pay), channel_id=1, source_target_pairs={{0,4},{1,5},{2,6},{3,7},{4,0},{5,1},{6,2},{7,3},{8,12},{9,13},{10,... | collective-permute-start | bytes 12296 | tf_op jit(solution)/shard_map/ppermute | solution.py:583
  38.8 4.6 %collective-permute-start.6 = (f32[8,128]{1,0:T(8,128)S(1)}, f32[8,128]{1,0:T(8,128)S(1)}, u32[]{:S(2)}, u32[]{:S(2)}) collective-permute-start(f32[8,128]{1,0:T(8,128)S(1)} %add.5.x), channel_id=1, source_target_pairs={{0,8},{1,9},{2,10},{3,11},{4,12},{5,13},{6,14},{7,15},{8,0},{9,1},... | collective-permute-start | bytes 12296 | tf_op jit(solution)/shard_map/ppermute | solution.py:583

commit v3 on v2

--- a/solution.py
+++ b/solution.py
@@ -73,7 +73,8 @@
 
 class Fetch:
     def __init__(self, src, dst, sems):
-        self.parts = [pltpu.make_async_copy(src.at[t, 0], dst.at[pl.ds(t * CAP, CAP)], sems.at[t]) for t in range(NT)]
+        count, size = src.shape[0], src.shape[2]
+        self.parts = [pltpu.make_async_copy(src.at[t, 0], dst.at[pl.ds(t * size, size)], sems.at[t]) for t in range(count)]
 
     def start(self):
         for part in self.parts:
@@ -82,6 +83,10 @@
     def wait(self):
         for part in self.parts:
             part.wait()
+
+
+def tally_of(ref):
+    return [[ref[side * NT + t].astype(I32) for t in range(NT)] for side in range(2)]
 
 
 def mask_row(mask, at, c):
@@ -118,8 +123,18 @@
     stencil_row(src, at, emit)
 
 
-def loop(first, last, body):
-    lax.fori_loop(first + H, last + H + 1, lambda at, _: (body(at), 0)[1], 0)
+def loop(first, last, body, unroll):
+    def some(i, _):
+        for u in range(unroll):
+            body(first + H + i * unroll + u)
+        return 0
+
+    lax.fori_loop(0, (last + 1 - first) // unroll, some, 0)
+
+
+def rims(reach, body):
+    for at in [*range(-reach, 3 - reach), *range(ROWS - 3 + reach, ROWS + reach)]:
+        body(at + H)
 
 
 def even():
@@ -169,7 +184,7 @@
     )(pltpu.with_memory_space_constraint(basic, pltpu.HBM), pltpu.with_memory_space_constraint(land, pltpu.HBM))
 
 
-def order_kernel(cells_at, count_at, value_at, addr, sval, lane, spot, second, codes, cells, count, value, sems):
+def order_kernel(cells_at, count_at, value_at, addr, sval, lane, spot, second, tallies, codes, cells, count, value, sems):
     fetches = [
         pltpu.make_async_copy(src, dst, sems.at[i])
         for i, (src, dst) in enumerate(((cells_at, cells), (count_at, count), (value_at, value)))
@@ -222,10 +237,10 @@
         alive = out[6:7] > 0.5
         own = (where + H * CT) * LV + level
         addr[t] = own
-        spot[t] = where + H * CT
         sval[t] = out[3:4] + out[4:5] + out[5:6]
         lane[t] = jnp.where(alive, (cell & (LN - 1)).astype(F32), -1.0)
         if t == NT - 1:
+            spot[0] = where + H * CT
             second[0] = jnp.where(jnp.logical_or(row == 1, row == ROWS - 2), -3.0, 0.0)
         far = jnp.where(row < ROWS // 2, own + ROWS * COL, own - ROWS * COL)
         near = jnp.logical_or(row <= t, row >= ROWS - 1 - t)
@@ -233,15 +248,16 @@
         for q in range(CAP // LN):
             codes[pl.ds(4 * t + q, 1), :] = code[:, q * LN : (q + 1) * LN]
     codes[pl.ds(12, 1), :] = tally
+    tallies[0] = tally
 
 
 def order(cells, count, value):
     ints, floats = jax.ShapeDtypeStruct((NT, 1, CAP), I32), jax.ShapeDtypeStruct((NT, 1, CAP), F32)
     return pl.pallas_call(
         order_kernel,
-        out_shape=[ints, floats, floats, ints, jax.ShapeDtypeStruct((1, 1, CAP), F32), jax.ShapeDtypeStruct((CODE, LN), F32)],
+        out_shape=[ints, floats, floats, jax.ShapeDtypeStruct((1, 1, CAP), I32), jax.ShapeDtypeStruct((1, 1, CAP), F32), jax.ShapeDtypeStruct((1, 1, LN), F32), jax.ShapeDtypeStruct((CODE, LN), F32)],
         in_specs=[HBM] * 3,
-        out_specs=[VM] * 6,
+        out_specs=[VM] * 7,
         scratch_shapes=[
             pltpu.VMEM((NT, 1, CAP), I32),
             pltpu.SMEM((1, NT), I32),
@@ -258,70 +274,108 @@
     return jnp.broadcast_to(line, (LN, LN)).T
 
 
-def interior_kernel(staged, mask, lane, sval, spots, y0, y1, y2, y3, f1, f2, f3, twice, known, sea, at_ref, sem):
-    fetch = Fetch(spots, at_ref, sem)
-    fetch.start()
+def interior_kernel(staged, mask, lane, sval, addrs, spots, tallies, y0, y1, y2, y3, f1, f2, f3, twice, known, sea, total,
+                    g1, g2, g3, terms, at_ref, spot_ref, n_ref, sems):
+    fetches = [Fetch(addrs, at_ref, sems), Fetch(spots, spot_ref, sems.at[pl.ds(NT, 1)]), Fetch(tallies, n_ref, sems.at[pl.ds(NT + 1, 1)])]
+    for fetch in fetches:
+        fetch.start()
     for c in range(CT):
         flat = staged.at[c].reshape(LV * ROWS, LN)
 
-        def turn(r, _):
-            half = 2.5 * mask_row(mask, r + H, c)
-            for k in range(LV // 8):
-                v = flat[pl.ds(k * 8 * ROWS + r, 8, stride=ROWS), :]
-                y0[pl.ds(pl.multiple_of((r + H) * COL + c * LV + k * 8, 8), 8), :] = half * v
+        def turn(i, _):
+            for u in range(4):
+                r = i * 4 + u
+                half = 2.5 * mask_row(mask, r + H, c)
+                for k in range(LV // 8):
+                    v = flat[pl.ds(k * 8 * ROWS + r, 8, stride=ROWS), :]
+                    y0[pl.ds(pl.multiple_of((r + H) * COL + c * LV + k * 8, 8), 8), :] = half * v
             return 0
 
-        lax.fori_loop(0, ROWS, turn, 0, unroll=2)
+        lax.fori_loop(0, ROWS // 4, turn, 0)
 
     zero = jnp.zeros((8, LN), F32)
     for at in (H - 2, ROWS + H + 1):
         for j in range(COL // 8):
             y2[pl.ds(at * COL + j * 8, 8), :] = zero
-
     for t, f in enumerate((f1, f2, f3)):
         for at in [*range(H + t + 1), *range(ROWS + H - t - 1, RX)]:
             for j in range(COL // 8):
                 f[pl.ds(at * COL + j * 8, 8), :] = zero
-    loop(1, 14, lambda at: forward_row(y0, y1, mask, at, f1))
-    loop(2, 13, lambda at: forward_row(y1, y2, mask, at, f2))
-    loop(3, 12, lambda at: forward_row(y2, y3, mask, at, f3))
+    loop(1, 14, lambda at: forward_row(y0, y1, mask, at, f1), 7)
+    loop(2, 13, lambda at: forward_row(y1, y2, mask, at, f2), 6)
+    loop(3, 12, lambda at: forward_row(y2, y3, mask, at, f3), 5)
+    for fetch in fetches:
+        fetch.wait()
+
+    def gather(i, _):
+        for u in range(8):
+            s = i * 8 + u
+            here = pl.ds(s, 1)
+            g1[here, :] = y1[pl.ds(at_ref[s], 1), :]
+            g2[here, :] = y2[pl.ds(at_ref[CAP + s], 1), :]
+            g3[here, :] = y3[pl.ds(at_ref[2 * CAP + s], 1), :]
+            sea[here, :] = mask[pl.ds(spot_ref[s], 1), :]
+        return 0
+
+    lax.fori_loop(0, CAP // 8, gather, 0)
+    ups, downs = tally_of(n_ref)
     ids = lax.broadcasted_iota(I32, (LN, LN), 1).astype(F32)
-    for t in range(NT):
+    slot = lax.broadcasted_iota(I32, (LN, LN), 0)
+    acc = zero
+    for t, g in enumerate((g1, g2, g3)):
         for q in range(CAP // LN):
             part = pl.ds(q * LN, LN)
             hit = upright(lane[t, :, part]) == ids
             rows = pl.ds(t * CAP + q * LN, LN)
-            twice[rows, :] = jnp.where(hit, 2.0, 0.0)
-            known[rows, :] = jnp.where(hit, upright(sval[t, :, part]), 0.0)
-    fetch.wait()
-
-    def group(i, _):
+            two, have = jnp.where(hit, 2.0, 0.0), jnp.where(hit, upright(sval[t, :, part]), 0.0)
+            twice[rows, :] = two
+            known[rows, :] = have
+            early = jnp.logical_and(slot + q * LN >= ups[t], slot + q * LN < CAP - downs[t])
+            d = jnp.where(early, g[part, :] * two - have, 0.0)
+            acc = acc + jnp.sum((d * d).reshape(LN // 8, 8, LN), axis=0)
+            terms[rows, :] = d * (5.0 * sea[part, :]) if t == NT - 1 else 5.0 * d
+    total[...] = acc
+
+    def scatter(i, _):
         for u in range(8):
             s = i * 8 + u
-            sea[pl.ds(s, 1), :] = mask[pl.ds(at_ref[2 * CAP + s], 1), :]
+            for t, f in enumerate((f1, f2, f3)):
+                spot = pl.ds(at_ref[t * CAP + s], 1)
+                f[spot, :] = f[spot, :] + terms[pl.ds(t * CAP + s, 1), :]
         return 0
 
-    lax.fori_loop(0, CAP // 8, group, 0)
-
-
-def interior(staged, mask, lane, sval, spots):
+    lax.fori_loop(0, CAP // 8, scatter, 0)
+
+
+def interior(staged, mask, lane, sval, addrs, spots, tallies):
     rows = jax.ShapeDtypeStruct((NT * CAP, LN), F32)
+    few = pltpu.VMEM((CAP, LN), F32)
     return pl.pallas_call(
         interior_kernel,
-        out_shape=[FIELD] * 7 + [rows, rows, jax.ShapeDtypeStruct((CAP, LN), F32)],
-        in_specs=[VM] * 4 + [ANY],
-        out_specs=[VM] * 10,
-        scratch_shapes=[pltpu.SMEM((NT * CAP,), I32), pltpu.SemaphoreType.DMA((NT,))],
+        out_shape=[FIELD] * 7 + [rows, rows, jax.ShapeDtypeStruct((CAP, LN), F32), jax.ShapeDtypeStruct((8, LN), F32)],
+        in_specs=[VM] * 4 + [ANY] * 3,
+        out_specs=[VM] * 11,
+        scratch_shapes=[
+            few,
+            few,
+            few,
+            pltpu.VMEM((NT * CAP, LN), F32),
+            pltpu.SMEM((NT * CAP,), I32),
+            pltpu.SMEM((CAP,), I32),
+            pltpu.SMEM((LN,), F32),
+            pltpu.SemaphoreType.DMA((NT + 2,)),
+        ],
         compiler_params=params(6),
-        cost_estimate=cost(9),
+        cost_estimate=cost(11),
         name="interior",
-    )(staged, mask, lane, sval, spots)
-
-
-def bands_kernel(y0i, y1i, y2i, y3, maski, twice, known, sea, second, codes, addrs, twin, other,
-                 y0, y1, y2, mask, pay, terms, g1, g2, g3, g4, at_ref, sem):
-    fetch = Fetch(addrs, at_ref, sem)
-    fetch.start()
+    )(staged, mask, lane, sval, addrs, spots, tallies)
+
+
+def bands_kernel(y0i, y1i, y2i, y3, f1i, f2i, f3i, maski, twice, known, sea, totali, second, codes, addrs, tallies, twin, other,
+                 y0, y1, y2, f1, f2, f3, mask, pay, terms, extra, at_ref, n_ref, sems):
+    fetches = [Fetch(addrs, at_ref, sems), Fetch(tallies, n_ref, sems.at[pl.ds(NT, 1)])]
+    for fetch in fetches:
+        fetch.start()
     lower = jnp.where(even(), ROWS + H, 0)
     for halo, first in ((twin, lower), (other, ROWS + H - lower)):
         base = pl.multiple_of(first * COL, 8)
@@ -331,98 +385,77 @@
         for j in range(H):
             mask[pl.ds(base + j * CT, CT), :] = halo[pl.ds(H * COL + j * CT, CT), :]
     for src, dst, reach in ((y0, y1, 2), (y1, y2, 1), (y2, y3, 0)):
-        loop(-reach, 2 - reach, lambda at: forward_row(src, dst, mask, at))
-        loop(ROWS - 3 + reach, ROWS - 1 + reach, lambda at: forward_row(src, dst, mask, at))
-    fetch.wait()
-    many = 8
-
-    def group(i, _):
-        for u in range(many):
-            s = i * many + u
-            third = at_ref[2 * CAP + s]
-            g1[pl.ds(s, 1), :] = y1[pl.ds(at_ref[s], 1), :]
-            g2[pl.ds(s, 1), :] = y2[pl.ds(at_ref[CAP + s], 1), :]
-            g3[pl.ds(s, 1), :] = y3[pl.ds(third, 1), :]
-            g4[pl.ds(s, 1), :] = y2[pl.ds(third, 1), :]
-        return 0
-
-    lax.fori_loop(0, CAP // many, group, 0)
-    acc = jnp.zeros((8, LN), F32)
-    for t, g in enumerate((g1, g2, g3)):
-        for q in range(CAP // LN):
-            part, rows = pl.ds(q * LN, LN), pl.ds(t * CAP + q * LN, LN)
-            d = g[part, :] * twice[rows, :] - known[rows, :]
-            acc = acc + jnp.sum((d * d).reshape(LN // 8, 8, LN), axis=0)
-            if t == NT - 1:
-                d = d * (5.0 * sea[part, :])
-                z = g4[part, :]
-                e = jnp.sum(((z * z) * d).T, axis=0, keepdims=True)
-                pay[pl.ds(12 + q, 1), :] = e * second[0, :, part]
-            else:
-                d = 5.0 * d
-            terms[rows, :] = d
-            pay[pl.ds(4 * t + q, 1), :] = jnp.sum(d.T, axis=0, keepdims=True)
+        rims(reach, lambda at: forward_row(src, dst, mask, at))
+    for fetch in fetches:
+        fetch.wait()
+    ups, downs = tally_of(n_ref)
+    most = 0
+    for t in range(NT):
+        most = jnp.maximum(most, (jnp.maximum(ups[t], downs[t]) + t) // (t + 1))
+
+    def item(i, acc):
+        for t, (y, f) in ((2, (y3, f3)), (1, (y2, f2)), (0, (y1, f1))):
+            for u in range(t + 1):
+                j = i * (t + 1) + u
+                near = jnp.minimum(j, CAP - 1)
+                for n, slot in ((ups[t], near), (downs[t], CAP - 1 - near)):
+                    ok = j < n
+                    row = t * CAP + slot
+                    spot = pl.ds(at_ref[row], 1)
+                    d = jnp.where(ok, y[spot, :] * twice[pl.ds(row, 1), :] - known[pl.ds(row, 1), :], 0.0)
+                    acc = acc + d * d
+                    if t == NT - 1:
+                        d = d * (5.0 * sea[pl.ds(slot, 1), :])
+                        z = y2[spot, :]
+                        extra[pl.ds(jnp.where(ok, slot, CAP), 1), :] = (z * z) * d
+                    else:
+                        d = 5.0 * d
+                    f[spot, :] = f[spot, :] + d
+                    terms[pl.ds(jnp.where(ok, row, NT * CAP), 1), :] = d
+        return acc
+
+    acc = lax.fori_loop(0, most, item, jnp.zeros((1, LN), F32))
+    for q in range(CAP // LN):
+        for t in range(NT):
+
+            @pl.when(jnp.logical_or(ups[t] > q * LN, downs[t] > CAP - (q + 1) * LN))
+            def _():
+                pay[pl.ds(4 * t + q, 1), :] = jnp.sum(terms[pl.ds(t * CAP + q * LN, LN), :].T, axis=0, keepdims=True)
+                if t == NT - 1:
+                    e = jnp.sum(extra[pl.ds(q * LN, LN), :].T, axis=0, keepdims=True)
+                    pay[pl.ds(12 + q, 1), :] = e * second[0, :, pl.ds(q * LN, LN)]
+
     pay[pl.ds(CODE, CODE), :] = codes[...]
-    pay[pl.ds(2 * CODE, 8), :] = acc
-
-
-def bands(y0, y1, y2, y3, mask, twice, known, sea, second, codes, addrs, above, below):
-    rows = pltpu.VMEM((CAP, LN), F32)
+    pay[pl.ds(2 * CODE, 8), :] = totali[...] + jnp.where(sublanes() == 0, jnp.broadcast_to(acc, (8, LN)), 0.0)
+
+
+def bands(y0, y1, y2, y3, f1, f2, f3, mask, twice, known, sea, total, second, codes, addrs, tallies, twin, other):
     return pl.pallas_call(
         bands_kernel,
-        out_shape=[FIELD] * 3
-        + [
-            MASK,
-            jax.ShapeDtypeStruct((PAY, LN), F32),
-            jax.ShapeDtypeStruct((NT * CAP, LN), F32),
+        out_shape=[FIELD] * 6 + [MASK, jax.ShapeDtypeStruct((PAY, LN), F32)],
+        in_specs=[VM] * 14 + [ANY] * 2 + [VM] * 2,
+        out_specs=[VM] * 8,
+        input_output_aliases={0: 0, 1: 1, 2: 2, 4: 3, 5: 4, 6: 5, 7: 6},
+        scratch_shapes=[
+            pltpu.VMEM((NT * CAP + 8, LN), F32),
+            pltpu.VMEM((CAP + 8, LN), F32),
+            pltpu.SMEM((NT * CAP,), I32),
+            pltpu.SMEM((LN,), F32),
+            pltpu.SemaphoreType.DMA((NT + 1,)),
         ],
-        in_specs=[VM] * 10 + [ANY] + [VM] * 2,
-        out_specs=[VM] * 6,
-        input_output_aliases={0: 0, 1: 1, 2: 2, 4: 3},
-        scratch_shapes=[rows, rows, rows, rows, pltpu.SMEM((NT * CAP,), I32), pltpu.SemaphoreType.DMA((NT,))],
         compiler_params=params(4),
         cost_estimate=cost(5),
         name="bands",
-    )(y0, y1, y2, y3, mask, twice, known, sea, second, codes, addrs, above, below)
-
-
-def scatter_kernel(f1i, f2i, f3i, terms, addrs, f1, f2, f3, at_ref, sem):
-    fetch = Fetch(addrs, at_ref, sem)
-    fetch.start()
-    fetch.wait()
-
-    def group(i, _):
-        for u in range(8):
-            s = i * 8 + u
-            for t, f in enumerate((f1, f2, f3)):
-                spot = pl.ds(at_ref[t * CAP + s], 1)
-                f[spot, :] = f[spot, :] + terms[pl.ds(t * CAP + s, 1), :]
-        return 0
-
-    lax.fori_loop(0, CAP // 8, group, 0)
-
-
-def scatter(f1, f2, f3, terms, addrs):
+    )(y0, y1, y2, y3, f1, f2, f3, mask, twice, known, sea, total, second, codes, addrs, tallies, twin, other)
+
+
+def adjoint_kernel(first, last, unroll, src, state, forcing, mask, out):
+    loop(first, last, lambda at: adjoint_row(src, state, out, mask, at), unroll)
+
+
+def adjoint(first, last, unroll, src, state, forcing, mask):
     return pl.pallas_call(
-        scatter_kernel,
-        out_shape=[FIELD] * 3,
-        in_specs=[VM] * 4 + [ANY],
-        out_specs=[VM] * 3,
-        input_output_aliases={0: 0, 1: 1, 2: 2},
-        scratch_shapes=[pltpu.SMEM((NT * CAP,), I32), pltpu.SemaphoreType.DMA((NT,))],
-        compiler_params=params(2),
-        cost_estimate=cost(3),
-        name="scatter",
-    )(f1, f2, f3, terms, addrs)
-
-
-def adjoint_kernel(first, last, src, state, forcing, mask, out):
-    loop(first, last, lambda at: adjoint_row(src, state, out, mask, at))
-
-
-def adjoint(first, last, src, state, forcing, mask):
-    return pl.pallas_call(
-        functools.partial(adjoint_kernel, first, last),
+        functools.partial(adjoint_kernel, first, last, unroll),
         out_shape=FIELD,
         in_specs=[VM] * 4,
         out_specs=VM,
@@ -433,24 +466,8 @@
     )(src, state, forcing, mask)
 
 
-def middle_kernel(f1, y0, grad):
-    loop(3, 12, lambda at: gradient_row(f1, y0, grad, at))
-
-
-def middle(f1, y0):
-    return pl.pallas_call(
-        middle_kernel,
-        out_shape=jax.ShapeDtypeStruct((ROWS * COL, LN), F32),
-        in_specs=[VM] * 2,
-        out_specs=VM,
-        compiler_params=params(2),
-        cost_estimate=cost(2),
-        name="middle",
-    )(f1, y0)
-
-
-def finish_kernel(scale, y0, y1, y2, f1i, f2i, f3i, mask, gradi, twin, other, x, y, f1, f2, f3, grad, out, misfit,
-                  staged, a_ref, b_ref, ca, cb, sems):
+def finish_kernel(scale, y0, y1, y2, f1i, f2i, f3i, mask, twin, other, x, y, f1, f2, f3, out, misfit, grad, staged,
+                  a_ref, b_ref, ca, cb, sems):
     misfit[...] = jnp.sum(x[...] + y[...], keepdims=True) * scale
 
     def fetches(above, below):
@@ -469,6 +486,7 @@
     for q in range(COL // 8):
         for buf in (ca, cb):
             buf[pl.ds(q * 8, 8), :] = jnp.zeros((8, LN), F32)
+    loop(3, 12, lambda at: gradient_row(f1, y0, grad, at), 5)
     for f in fetches(twin, other):
         f.wait()
     counts = CODE * LN + 12 * LN
@@ -504,10 +522,8 @@
             spot = pl.ds(at * COL + q * 8, 8)
             f2[spot, :] = f2[spot, :] + side[pl.ds(q * 8, 8), :]
     for src, state, dst, reach in ((f3, y2, f2, 2), (f2, y1, f1, 1)):
-        loop(-reach, 2 - reach, lambda at: adjoint_row(src, state, dst, mask, at))
-        loop(ROWS - 3 + reach, ROWS - 1 + reach, lambda at: adjoint_row(src, state, dst, mask, at))
-    loop(0, 2, lambda at: gradient_row(f1, y0, grad, at))
-    loop(ROWS - 3, ROWS - 1, lambda at: gradient_row(f1, y0, grad, at))
+        rims(reach, lambda at: adjoint_row(src, state, dst, mask, at))
+    rims(0, lambda at: gradient_row(f1, y0, grad, at))
 
     def copy(c):
         return pltpu.make_async_copy(staged.at[c], out.at[:, :, pl.ds(c * LN, LN)], sems.at[c])
@@ -519,25 +535,22 @@
                 staged[c, k, pl.ds(half * 8, 8), :] = v
             return 0
 
-        lax.fori_loop(0, LV, turn, 0, unroll=8)
+        for k in range(LV):
+            turn(k, 0)
         copy(c).start()
     for c in range(CT):
         copy(c).wait()
 
 
-def finish(y0, y1, y2, f1, f2, f3, mask, grad, twin, other, x, y, scale):
+def finish(y0, y1, y2, f1, f2, f3, mask, twin, other, x, y, scale):
     return pl.pallas_call(
         functools.partial(finish_kernel, scale),
-        out_shape=[FIELD] * 3
-        + [
-            jax.ShapeDtypeStruct((ROWS * COL, LN), F32),
-            jax.ShapeDtypeStruct((LV, ROWS, CT * LN), F32),
-            jax.ShapeDtypeStruct((1, 1), F32),
-        ],
-        in_specs=[VM] * 8 + [ANY] * 2 + [VM] * 2,
-        out_specs=[VM] * 4 + [ANY, VM],
-        input_output_aliases={3: 0, 4: 1, 5: 2, 7: 3},
+        out_shape=[FIELD] * 3 + [jax.ShapeDtypeStruct((LV, ROWS, CT * LN), F32), jax.ShapeDtypeStruct((1, 1), F32)],
+        in_specs=[VM] * 7 + [ANY] * 2 + [VM] * 2,
+        out_specs=[VM] * 3 + [ANY, VM],
+        input_output_aliases={3: 0, 4: 1, 5: 2},
         scratch_shapes=[
+            pltpu.VMEM((ROWS * COL, LN), F32),
             pltpu.VMEM((CT, LV, ROWS, LN), F32),
             pltpu.SMEM((PAY * LN,), F32),
             pltpu.SMEM((PAY * LN,), F32),
@@ -545,10 +558,10 @@
             pltpu.VMEM((COL, LN), F32),
             pltpu.SemaphoreType.DMA((CT + 2,)),
         ],
-        compiler_params=params(6),
-        cost_estimate=cost(6),
+        compiler_params=params(14),
+        cost_estimate=cost(7),
         name="finish",
-    )(y0, y1, y2, f1, f2, f3, mask, grad, twin, other, x, y)[4:]
+    )(y0, y1, y2, f1, f2, f3, mask, twin, other, x, y)[3:]
 
 
 def add_kernel(first, pay, twin, out):
@@ -567,22 +580,21 @@
     )(a, b)
 
 
-def sum_along(pay, twin, stages):
+def sum_along(pay, twin, stages, held):
     size = lax.axis_size("along")
     steps = [1 << i for i in range(1, size.bit_length() - 1)]
-    held = stages[0]()
     x = add(2 * CODE, pay, twin)
     other = jnp.zeros_like(x)
     if size & (size - 1):
         x, steps = lax.psum(0.5 * x, "along"), []
-    for i in range(max(len(steps), len(stages) - 1)):
+    for i in range(max(len(steps), len(stages))):
         if i < len(steps):
             if i > 0:
                 x = add(0, x, other)
             x, held = lax.optimization_barrier((x, held))
             other = lax.ppermute(x, "along", [(p, p ^ steps[i]) for p in range(size)])
-        if i + 1 < len(stages):
-            held = stages[i + 1](*held)
+        if i < len(stages):
+            held = stages[i](*held)
     return x, other, held
 
 
@@ -595,20 +607,20 @@
     staged, twin, other, mask = edges(basic_state, land_sea)
     other = lax.ppermute(other, "along", others)
     twin = lax.ppermute(twin, "along", twins)
-    addrs, sval, lane, spots, second, codes = order(cells, obs_count, value)
-    y0, y1, y2, y3, f1, f2, f3, twice, known, sea = interior(staged, mask, lane, sval, spots)
-    y0, y1, y2, mask, pay, terms = bands(y0, y1, y2, y3, mask, twice, known, sea, second, codes, addrs, twin, other)
+    addrs, sval, lane, spots, second, tallies, codes = order(cells, obs_count, value)
+    y0, y1, y2, y3, f1, f2, f3, twice, known, sea, total = interior(staged, mask, lane, sval, addrs, spots, tallies)
+    y0, y1, y2, f1, f2, f3, mask, pay = bands(
+        y0, y1, y2, y3, f1, f2, f3, mask, twice, known, sea, total, second, codes, addrs, tallies, twin, other
+    )
     other = lax.ppermute(pay, "along", others)
     twin = lax.ppermute(pay, "along", twins)
     stages = (
-        lambda: scatter(f1, f2, f3, terms, addrs),
-        lambda a, b, c: (a, adjoint(1, 14, c, y2, b, mask), c),
-        lambda a, b, c: (adjoint(2, 13, b, y1, a, mask), b, c),
-        lambda a, b, c: (a, b, c, middle(a, y0)),
+        lambda a, b, c: (a, adjoint(1, 14, 7, c, y2, b, mask), c),
+        lambda a, b, c: (adjoint(2, 13, 6, b, y1, a, mask), b, c),
     )
-    x, y, held = sum_along(pay, twin, stages)
+    x, y, held = sum_along(pay, twin, stages, (f1, f2, f3))
     scale = 1.0 / (2.0 * size * obs_cells.shape[1] * obs_cells.shape[2])
-    gradient, misfit = finish(y0, y1, y2, *held[:3], mask, held[3], twin.reshape(-1), other.reshape(-1), x, y, scale)
+    gradient, misfit = finish(y0, y1, y2, *held, mask, twin.reshape(-1), other.reshape(-1), x, y, scale)
     misfit = misfit.reshape(1)
     return gradient, misfit
 

time: 53 us -> 48.4 us (0.913)
  Pallas kernels: 35.5 us -> 30.7 us
  waiting for transfers between devices: 0.32 us -> 2.13 us
  starting transfers between devices: 16.3 us -> 14.8 us
    pallas_call x6 -> x4, Pallas kernels: 15.7 us -> 8.98 us  [the longest x1 4.51 us: bands(): pl.pallas_call(bands_kernel, out_shape=[FIELD] * 6 + [MASK, jax.ShapeDtyp...]
    pallas_call x1, Pallas kernels: 8.41 us -> 10.3 us  [interior(): pl.pallas_call(interior_kernel, out_shape=[FIELD] * 7 + [rows, rows, jax....]
    ppermute x3, waiting for transfers between devices: 0.31 us -> 1.94 us  [sum_along(): other = lax.ppermute(x, 'along', [(p, p ^ steps[i]) for p in range(size)])]
    ppermute x1, starting transfers between devices: 5.19 us -> 4.18 us  [local(): twin = lax.ppermute(pay, 'along', twins)]
  transfers between devices with their start and end apart: 7 -> 7, of which waited for: 1 -> 4; matrix products, arithmetic and copies ran while one was open for 0% -> 0% of each run, Pallas kernels for 36% -> 31%
where the time goes in v3:
time: 48.4 us
  Pallas kernels  30.7 us (63%)
  starting transfers between devices  14.8 us (31%)
  waiting for transfers between devices  2.13 us (4%)
  between operations  0.88 us (2%)
    pallas_call x1, Pallas kernels, interior(): pl.pallas_call(interior_kernel, out_shape=[FIELD] * 7 + [rows, rows, jax....  10.3 us
    pallas_call x1, Pallas kernels, finish(): pl.pallas_call(functools.partial(finish_kernel, scale), out_shape=[FIELD]...  9.45 us
    ppermute x3, starting transfers between devices, sum_along(): other = lax.ppermute(x, 'along', [(p, p ^ steps[i]) for p in range(size)])  8.73 us
    pallas_call x1, Pallas kernels, bands(): pl.pallas_call(bands_kernel, out_shape=[FIELD] * 6 + [MASK, jax.ShapeDtyp...  4.51 us
    ppermute x1, starting transfers between devices, local(): twin = lax.ppermute(pay, 'along', twins)  4.18 us
    pallas_call x2, Pallas kernels, adjoint(): pl.pallas_call(functools.partial(adjoint_kernel, first, last, unroll), ou...  2.9 us
    ppermute x3, waiting for transfers between devices, sum_along(): other = lax.ppermute(x, 'along', [(p, p ^ steps[i]) for p in range(size)])  1.94 us
    pallas_call x1, Pallas kernels, edges(): pl.pallas_call(edges_kernel, out_shape=[jax.ShapeDtypeStruct((CT, LV, ROW...  1.87 us
  transfers between devices with their start and end apart: 7, of which 4 were waited for; matrix products, arithmetic and copies ran while one was open for 0% of the time, Pallas kernels for 31%

profile of v3, /device:TPU:0, one launch (start us, length us, event | category | flops | bytes accessed | tf_op | source)
XLA Modules:
  0.0 48.4 jit_solution(4661867419583409274)
XLA Ops:
  0.6 1.9 %edges.1 = (f32[8,40,16,128]{3,2,1,0:T(8,128)S(1)}, f32[984,128]{1,0:T(8,128)S(1)}, f32[984,128]{1,0:T(8,128)S(1)}, f32[176,128]{1,0:T(8,128)S(1)}) custom-call(f32[40,16,1024]{2,1,0:T(8,128)} %basic.1, s32[16,1024]{1,0:T(8,128)} %land_at.1), custom_call_target="tpu_custom_call" | custom-call | bytes 6000000 | tf_op jit(solution)/shard_map/edges/pallas_call | solution.py:170
  2.5 0.5 %collective-permute-start = (f32[984,128]{1,0:T(8,128)S(1)}, f32[984,128]{1,0:T(8,128)S(1)}, u32[]{:S(2)}, u32[]{:S(2)}) collective-permute-start(f32[984,128]{1,0:T(8,128)S(1)} %get-tuple-element.66), channel_id=1, source_target_pairs={{0,1},{1,0},{2,3},{3,2},{4,5},{5,4},{6,7},{7,6},{8,9},{9,8},{10,11... | collective-permute-start | bytes 1511432 | tf_op jit(solution)/shard_map/ppermute | solution.py:609
  3.0 0.7 %collective-permute-start.1 = (f32[984,128]{1,0:T(8,128)S(1)}, f32[984,128]{1,0:T(8,128)S(1)}, u32[]{:S(2)}, u32[]{:S(2)}) collective-permute-start(f32[984,128]{1,0:T(8,128)S(1)} %get-tuple-element.67), channel_id=1, source_target_pairs={{1,2},{2,1},{3,4},{4,3},{5,6},{6,5},{7,8},{8,7},{9,10},{10,9},{11,... | collective-permute-start | bytes 1511432 | tf_op jit(solution)/shard_map/ppermute | solution.py:608
  3.7 1.6 %order.1 = (s32[3,1,512]{2,1,0:T(1,128)S(1)}, f32[3,1,512]{2,1,0:T(1,128)S(1)}, f32[3,1,512]{2,1,0:T(1,128)S(1)}, s32[1,1,512]{2,1,0:T(1,128)S(1)}, f32[1,1,512]...) custom-call(s32[3,1,512]{2,1,0:T(1,128)} %bitcast.7, s32[1,3]{1,0:T(1,128)} %count_at.1, ...), custom_call_target="tpu_custom_call" | custom-call | bytes 6000000 | tf_op jit(solution)/shard_map/order/pallas_call | solution.py:256
  5.3 10.3 %interior.1 = (f32[7040,128]{1,0:T(8,128)S(1)}, f32[7040,128]{1,0:T(8,128)S(1)}, f32[7040,128]{1,0:T(8,128)S(1)}, f32[7040,128]{1,0:T(8,128)S(1)}, f32[7040,128]...) custom-call(f32[8,40,16,128]{3,2,1,0:T(8,128)S(1)} %get-tuple-elemen, ...), custom_call_target="tpu_custom_call" | custom-call | bytes 33000000 | tf_op jit(solution)/shard_map/interior/pallas_call | solution.py:353
  15.7 0.0 collective-permute-done.twin
  15.7 0.0 collective-permute-done.1.other
  15.7 4.5 %bands.1 = (f32[7040,128]{1,0:T(8,128)S(1)}, f32[7040,128]{1,0:T(8,128)S(1)}, f32[7040,128]{1,0:T(8,128)S(1)}, f32[7040,128]{1,0:T(8,128)S(1)}, f32[7040,128]{1,...) custom-call(f32[7040,128]{1,0:T(8,128)S(1)} %get-tuple-element.53.y0, ...), custom_call_target="tpu_custom_call", output_to_operand_aliasing={{0}: (0, {}), {1}: (1, {}), {2}: (2, {}), {3}: (4, {}), {4}... | custom-call | bytes 15000000 | tf_op jit(solution)/shard_map/bands/pallas_call | solution.py:433
  20.2 4.2 %collective-permute-start.2 = (f32[40,128]{1,0:T(8,128)S(1)}, f32[40,128]{1,0:T(8,128)S(1)}, u32[]{:S(2)}, u32[]{:S(2)}) collective-permute-start(f32[40,128]{1,0:T(8,128)S(1)} %get-tuple-element.71.pay), channel_id=1, source_target_pairs={{0,1},{1,0},{2,3},{3,2},{4,5},{5,4},{6,7},{7,6},{8,9},{9,8},{10,11... | collective-permute-start | bytes 61448 | tf_op jit(solution)/shard_map/ppermute | solution.py:616
  24.4 0.7 %collective-permute-start.5 = (f32[40,128]{1,0:T(8,128)S(1)}, f32[40,128]{1,0:T(8,128)S(1)}, u32[]{:S(2)}, u32[]{:S(2)}) collective-permute-start(f32[40,128]{1,0:T(8,128)S(1)} %get-tuple-element.71.pay), channel_id=1, source_target_pairs={{1,2},{2,1},{3,4},{4,3},{5,6},{6,5},{7,8},{8,7},{9,10},{10,9},{11,... | collective-permute-start | bytes 61448 | tf_op jit(solution)/shard_map/ppermute | solution.py:615
  25.0 0.2 collective-permute-done.2.twin
  25.2 2.8 %collective-permute-start.3 = (f32[8,128]{1,0:T(8,128)S(1)}, f32[8,128]{1,0:T(8,128)S(1)}, u32[]{:S(2)}, u32[]{:S(2)}) collective-permute-start(f32[8,128]{1,0:T(8,128)S(1)} %add.3.pay), channel_id=1, source_target_pairs={{0,2},{1,3},{2,0},{3,1},{4,6},{5,7},{6,4},{7,5},{8,10},{9,11},{10,... | collective-permute-start | bytes 12296 | tf_op jit(solution)/shard_map/ppermute | solution.py:595
  28.0 1.5 %adjoint.2.src.f2i = f32[7040,128]{1,0:T(8,128)S(1)} custom-call(f32[7040,128]{1,0:T(8,128)S(1)} %get-tuple-element.86.src.f3i, f32[7040,128]{1,0:T(8,128)S(1)} %get-tuple-element.70.state.y2, f32[7040,128]{1,0:T(8,128)S(1)} %get-tuple-element.78.forcing, f32[176,128]{1,0:T(8,128)S(1)} %get-tuple-element.79.mask), custom_call_target="tpu_custom_call", output_to_operand_aliasing={{}: (2, {})} | custom-call | bytes 6000000 | tf_op jit(solution)/shard_map/adjoint/pallas_call | solution.py:457
  29.6 0.1 collective-permute-done.3.twin
  29.7 2.9 %collective-permute-start.4 = (f32[8,128]{1,0:T(8,128)S(1)}, f32[8,128]{1,0:T(8,128)S(1)}, u32[]{:S(2)}, u32[]{:S(2)}) collective-permute-start(f32[8,128]{1,0:T(8,128)S(1)} %add.4.pay), channel_id=1, source_target_pairs={{0,4},{1,5},{2,6},{3,7},{4,0},{5,1},{6,2},{7,3},{8,12},{9,13},{10,... | collective-permute-start | bytes 12296 | tf_op jit(solution)/shard_map/ppermute | solution.py:595
  32.7 1.3 %adjoint.3.f1i = f32[7040,128]{1,0:T(8,128)S(1)} custom-call(f32[7040,128]{1,0:T(8,128)S(1)} %adjoint.2.src.f2i, f32[7040,128]{1,0:T(8,128)S(1)} %get-tuple-element.69.state.y1, f32[7040,128]{1,0:T(8,128)S(1)} %get-tuple-element.82.forcing, f32[176,128]{1,0:T(8,128)S(1)} %get-tuple-element.79.mask), custom_call_target="tpu_custom_call", output_to_operand_aliasing={{}: (2, {})} | custom-call | bytes 6000000 | tf_op jit(solution)/shard_map/adjoint/pallas_call | solution.py:457
  34.0 0.2 collective-permute-done.4.twin
  34.3 3.0 %collective-permute-start.6 = (f32[8,128]{1,0:T(8,128)S(1)}, f32[8,128]{1,0:T(8,128)S(1)}, u32[]{:S(2)}, u32[]{:S(2)}) collective-permute-start(f32[8,128]{1,0:T(8,128)S(1)} %add.5.x), channel_id=1, source_target_pairs={{0,8},{1,9},{2,10},{3,11},{4,12},{5,13},{6,14},{7,15},{8,0},{9,1},... | collective-permute-start | bytes 12296 | tf_op jit(solution)/shard_map/ppermute | solution.py:595
  37.2 0.0 collective-permute-done.5
  37.2 1.6 %collective-permute-done.6.y = f32[8,128]{1,0:T(8,128)S(1)} collective-permute-done((f32[8,128]{1,0:T(8,128)S(1)}, f32[8,128]{1,0:T(8,128)S(1)}, u32[]{:S(2)}, u32[]{:S(2)}) %collective-permute-start.6) | collective-permute-done | bytes 4128 | tf_op jit(solution)/shard_map/ppermute | solution.py:595
  38.8 9.4 %finish.1 = (f32[7040,128]{1,0:T(8,128)S(1)}, f32[7040,128]{1,0:T(8,128)S(1)}, f32[7040,128]{1,0:T(8,128)S(1)}, f32[40,16,1024]{2,1,0:T(8,128)}, f32[1,1]{1,0:T(1,128)}) custom-call(f32[7040,128]{1,0:T(8,128)S(1)} %get-tuple-element.68.y0, f32[7040,128]{1,0:T(8,128)S(1)} %get-tuple-element.69.state.y1, ...), custom_call_target="tpu_custom_call", output_to_operand_aliasing={{0}: (3, {}), {1}: (4, {}), {2}: (5, {})} | custom-call | bytes 21000000 | tf_op jit(solution)/shard_map/finish/pallas_call | solution.py:546
  (3 shorter events, 0.0 us)
Async XLA Ops:
  2.5 13.1 %collective-permute-start = (f32[984,128]{1,0:T(8,128)S(1)}, f32[984,128]{1,0:T(8,128)S(1)}, u32[]{:S(2)}, u32[]{:S(2)}) collective-permute-start(f32[984,128]{1,0:T(8,128)S(1)} %get-tuple-element.66), channel_id=1, source_target_pairs={{0,1},{1,0},{2,3},{3,2},{4,5},{5,4},{6,7},{7,6},{8,9},{9,8},{10,11... | collective-permute-start | bytes 1511432 | tf_op jit(solution)/shard_map/ppermute | solution.py:609
  3.0 12.6 %collective-permute-start.1 = (f32[984,128]{1,0:T(8,128)S(1)}, f32[984,128]{1,0:T(8,128)S(1)}, u32[]{:S(2)}, u32[]{:S(2)}) collective-permute-start(f32[984,128]{1,0:T(8,128)S(1)} %get-tuple-element.67), channel_id=1, source_target_pairs={{1,2},{2,1},{3,4},{4,3},{5,6},{6,5},{7,8},{8,7},{9,10},{10,9},{11,... | collective-permute-start | bytes 1511432 | tf_op jit(solution)/shard_map/ppermute | solution.py:608
  20.2 5.0 %collective-permute-start.2 = (f32[40,128]{1,0:T(8,128)S(1)}, f32[40,128]{1,0:T(8,128)S(1)}, u32[]{:S(2)}, u32[]{:S(2)}) collective-permute-start(f32[40,128]{1,0:T(8,128)S(1)} %get-tuple-element.71.pay), channel_id=1, source_target_pairs={{0,1},{1,0},{2,3},{3,2},{4,5},{5,4},{6,7},{7,6},{8,9},{9,8},{10,11... | collective-permute-start | bytes 61448 | tf_op jit(solution)/shard_map/ppermute | solution.py:616
  24.4 12.9 %collective-permute-start.5 = (f32[40,128]{1,0:T(8,128)S(1)}, f32[40,128]{1,0:T(8,128)S(1)}, u32[]{:S(2)}, u32[]{:S(2)}) collective-permute-start(f32[40,128]{1,0:T(8,128)S(1)} %get-tuple-element.71.pay), channel_id=1, source_target_pairs={{1,2},{2,1},{3,4},{4,3},{5,6},{6,5},{7,8},{8,7},{9,10},{10,9},{11,... | collective-permute-start | bytes 61448 | tf_op jit(solution)/shard_map/ppermute | solution.py:615
  25.2 4.5 %collective-permute-start.3 = (f32[8,128]{1,0:T(8,128)S(1)}, f32[8,128]{1,0:T(8,128)S(1)}, u32[]{:S(2)}, u32[]{:S(2)}) collective-permute-start(f32[8,128]{1,0:T(8,128)S(1)} %add.3.pay), channel_id=1, source_target_pairs={{0,2},{1,3},{2,0},{3,1},{4,6},{5,7},{6,4},{7,5},{8,10},{9,11},{10,... | collective-permute-start | bytes 12296 | tf_op jit(solution)/shard_map/ppermute | solution.py:595
  29.7 4.5 %collective-permute-start.4 = (f32[8,128]{1,0:T(8,128)S(1)}, f32[8,128]{1,0:T(8,128)S(1)}, u32[]{:S(2)}, u32[]{:S(2)}) collective-permute-start(f32[8,128]{1,0:T(8,128)S(1)} %add.4.pay), channel_id=1, source_target_pairs={{0,4},{1,5},{2,6},{3,7},{4,0},{5,1},{6,2},{7,3},{8,12},{9,13},{10,... | collective-permute-start | bytes 12296 | tf_op jit(solution)/shard_map/ppermute | solution.py:595
  34.3 4.6 %collective-permute-start.6 = (f32[8,128]{1,0:T(8,128)S(1)}, f32[8,128]{1,0:T(8,128)S(1)}, u32[]{:S(2)}, u32[]{:S(2)}) collective-permute-start(f32[8,128]{1,0:T(8,128)S(1)} %add.5.x), channel_id=1, source_target_pairs={{0,8},{1,9},{2,10},{3,11},{4,12},{5,13},{6,14},{7,15},{8,0},{9,1},... | collective-permute-start | bytes 12296 | tf_op jit(solution)/shard_map/ppermute | solution.py:595

commit v4 on v3

--- a/solution.py
+++ b/solution.py
@@ -466,54 +466,70 @@
     )(src, state, forcing, mask)
 
 
-def finish_kernel(scale, y0, y1, y2, f1i, f2i, f3i, mask, twin, other, x, y, f1, f2, f3, out, misfit, grad, staged,
-                  a_ref, b_ref, ca, cb, sems):
-    misfit[...] = jnp.sum(x[...] + y[...], keepdims=True) * scale
-
+SIDE = 28 * LN
+LANES, ADDRS, FARS = 0, 12 * LN, 24 * LN
+
+
+def edge_terms_kernel(y0, y1, y2, f1i, f2i, f3i, mask, twin, other, twin_flat, other_flat,
+                      f1, f2, f3, grad, a_ref, b_ref, ca, cb, lines, line_ref, sems):
     def fetches(above, below):
-        return [pltpu.make_async_copy(src, dst, sems.at[CT + i]) for i, (src, dst) in enumerate(((above, a_ref), (below, b_ref)))]
+        return [pltpu.make_async_copy(src, dst, sems.at[i]) for i, (src, dst) in enumerate(((above, a_ref), (below, b_ref)))]
 
     @pl.when(even())
     def _():
-        for f in fetches(other, twin):
+        for f in fetches(other_flat, twin_flat):
             f.start()
 
     @pl.when(jnp.logical_not(even()))
     def _():
-        for f in fetches(twin, other):
+        for f in fetches(twin_flat, other_flat):
             f.start()
 
+    slot = lax.broadcasted_iota(I32, (1, LN), 1)
+    for side, (x, y) in enumerate(((other, twin), (twin, other))):
+        counts = jnp.where(even(), x[pl.ds(CODE + 12, 1), :], y[pl.ds(CODE + 12, 1), :]).astype(I32)
+        for t in range(NT):
+            n = jnp.sum(jnp.where(slot == (1 - side) * NT + t, counts, 0), axis=1, keepdims=True)
+            for q in range(CAP // LN):
+                row = pl.ds(CODE + 4 * t + q, 1)
+                code = jnp.where(even(), x[row, :], y[row, :]).astype(I32)
+                at = slot + q * LN
+                live = at >= CAP - n if side == 0 else at < n
+                base = side * SIDE + (4 * t + q) * LN
+                addr = jnp.where(live, code >> 7, 0)
+                lines[0, :, pl.ds(base + LANES, LN)] = jnp.where(live, code & (LN - 1), -1)
+                lines[0, :, pl.ds(base + ADDRS, LN)] = addr
+                if t == NT - 1:
+                    far = addr - (1 if side == 0 else ROWS + H + 1) * COL
+                    far = jnp.where(jnp.logical_and(far >= 0, far < COL), far, 0)
+                    lines[0, :, pl.ds(side * SIDE + FARS + q * LN, LN)] = far
+    prepared = Fetch(lines, line_ref, sems.at[pl.ds(2, 1)])
+    prepared.start()
     for q in range(COL // 8):
         for buf in (ca, cb):
             buf[pl.ds(q * 8, 8), :] = jnp.zeros((8, LN), F32)
     loop(3, 12, lambda at: gradient_row(f1, y0, grad, at), 5)
-    for f in fetches(twin, other):
+    for f in fetches(twin_flat, other_flat):
         f.wait()
-    counts = CODE * LN + 12 * LN
-    lane = lax.broadcasted_iota(I32, (1, LN), 1)
-    na = [a_ref[counts + NT + t].astype(I32) for t in range(NT)]
-    nb = [b_ref[counts + t].astype(I32) for t in range(NT)]
+    prepared.wait()
+    counts = (CODE + 12) * LN
     most = 0
     for t in range(NT):
-        most = jnp.maximum(most, (jnp.maximum(na[t], nb[t]) + t) // (t + 1))
+        n = jnp.maximum(a_ref[counts + NT + t].astype(I32), b_ref[counts + t].astype(I32))
+        most = jnp.maximum(most, (n + t) // (t + 1))
 
     def item(i, _):
         for t, f in ((2, f3), (1, f2), (0, f1)):
             for u in range(t + 1):
-                j = i * (t + 1) + u
-                slot_of = jnp.minimum(j, CAP - 1)
-                for ref, n, slot, side in ((a_ref, na[t], CAP - 1 - slot_of, ca), (b_ref, nb[t], slot_of, cb)):
-                    code = ref[CODE * LN + t * CAP + slot].astype(I32)
-                    hit = lane == jnp.where(j < n, code & (LN - 1), -1)
-                    addr = code >> 7
-                    spot = pl.ds(addr, 1)
-                    f[spot, :] = f[spot, :] + jnp.where(hit, ref[t * CAP + slot], 0.0)
+                near = jnp.minimum(i * (t + 1) + u, CAP - 1)
+                for ref, slot_at, first, side in ((a_ref, CAP - 1 - near, 0, ca), (b_ref, near, SIDE, cb)):
+                    at = t * CAP + slot_at
+                    hit = slot == line_ref[first + LANES + at]
+                    spot = pl.ds(line_ref[first + ADDRS + at], 1)
+                    f[spot, :] = f[spot, :] + jnp.where(hit, ref[at], 0.0)
                     if t == NT - 1:
-                        start = (1 if side is ca else ROWS + H + 1) * COL
-                        far = addr - start
-                        inside = jnp.logical_and(far >= 0, far < COL)
-                        spot = pl.ds(jnp.where(inside, far, 0), 1)
-                        side[spot, :] = side[spot, :] + jnp.where(hit, ref[12 * LN + slot], 0.0)
+                        spot = pl.ds(line_ref[first + FARS + slot_at], 1)
+                        side[spot, :] = side[spot, :] + jnp.where(hit, ref[12 * LN + slot_at], 0.0)
         return 0
 
     lax.fori_loop(0, most, item, 0)
@@ -523,45 +539,63 @@
             f2[spot, :] = f2[spot, :] + side[pl.ds(q * 8, 8), :]
     for src, state, dst, reach in ((f3, y2, f2, 2), (f2, y1, f1, 1)):
         rims(reach, lambda at: adjoint_row(src, state, dst, mask, at))
-    rims(0, lambda at: gradient_row(f1, y0, grad, at))
-
-    def copy(c):
-        return pltpu.make_async_copy(staged.at[c], out.at[:, :, pl.ds(c * LN, LN)], sems.at[c])
-
-    for c in range(CT):
-        def turn(k, _):
-            for half in range(2):
-                v = grad[pl.ds(half * 8 * COL + c * LV + k, 8, stride=COL), :]
-                staged[c, k, pl.ds(half * 8, 8), :] = v
-            return 0
-
-        for k in range(LV):
-            turn(k, 0)
-        copy(c).start()
-    for c in range(CT):
-        copy(c).wait()
-
-
-def finish(y0, y1, y2, f1, f2, f3, mask, twin, other, x, y, scale):
-    return pl.pallas_call(
-        functools.partial(finish_kernel, scale),
-        out_shape=[FIELD] * 3 + [jax.ShapeDtypeStruct((LV, ROWS, CT * LN), F32), jax.ShapeDtypeStruct((1, 1), F32)],
-        in_specs=[VM] * 7 + [ANY] * 2 + [VM] * 2,
-        out_specs=[VM] * 3 + [ANY, VM],
+
+
+def edge_terms(y0, y1, y2, f1, f2, f3, mask, twin, other):
+    return pl.pallas_call(
+        edge_terms_kernel,
+        out_shape=[FIELD] * 3 + [jax.ShapeDtypeStruct((ROWS * COL, LN), F32)],
+        in_specs=[VM] * 9 + [ANY] * 2,
+        out_specs=[VM] * 4,
         input_output_aliases={3: 0, 4: 1, 5: 2},
         scratch_shapes=[
-            pltpu.VMEM((ROWS * COL, LN), F32),
-            pltpu.VMEM((CT, LV, ROWS, LN), F32),
             pltpu.SMEM((PAY * LN,), F32),
             pltpu.SMEM((PAY * LN,), F32),
             pltpu.VMEM((COL, LN), F32),
             pltpu.VMEM((COL, LN), F32),
-            pltpu.SemaphoreType.DMA((CT + 2,)),
+            pltpu.VMEM((1, 1, 2 * SIDE), I32),
+            pltpu.SMEM((2 * SIDE,), I32),
+            pltpu.SemaphoreType.DMA((3,)),
         ],
-        compiler_params=params(14),
-        cost_estimate=cost(7),
+        compiler_params=params(4),
+        cost_estimate=cost(5),
+        name="edge_terms",
+    )(y0, y1, y2, f1, f2, f3, mask, twin, other, twin.reshape(-1), other.reshape(-1))
+
+
+def finish_kernel(scale, y0, f1, gradi, x, y, grad, out, misfit, staged, sems):
+    misfit[...] = jnp.sum(x[...] + y[...], keepdims=True) * scale
+    rims(0, lambda at: gradient_row(f1, y0, grad, at))
+
+    def copy(c):
+        return pltpu.make_async_copy(staged.at[c], out.at[:, :, pl.ds(c * LN, LN)], sems.at[c])
+
+    for c in range(CT):
+        for k in range(LV):
+            for half in range(2):
+                v = grad[pl.ds(half * 8 * COL + c * LV + k, 8, stride=COL), :]
+                staged[c, k, pl.ds(half * 8, 8), :] = v
+        copy(c).start()
+    for c in range(CT):
+        copy(c).wait()
+
+
+def finish(y0, f1, grad, x, y, scale):
+    return pl.pallas_call(
+        functools.partial(finish_kernel, scale),
+        out_shape=[
+            jax.ShapeDtypeStruct((ROWS * COL, LN), F32),
+            jax.ShapeDtypeStruct((LV, ROWS, CT * LN), F32),
+            jax.ShapeDtypeStruct((1, 1), F32),
+        ],
+        in_specs=[VM] * 5,
+        out_specs=[VM, ANY, VM],
+        input_output_aliases={2: 0},
+        scratch_shapes=[pltpu.VMEM((CT, LV, ROWS, LN), F32), pltpu.SemaphoreType.DMA((CT,))],
+        compiler_params=params(8),
+        cost_estimate=cost(4),
         name="finish",
-    )(y0, y1, y2, f1, f2, f3, mask, twin, other, x, y)[3:]
+    )(y0, f1, grad, x, y)[1:]
 
 
 def add_kernel(first, pay, twin, out):
@@ -617,10 +651,11 @@
     stages = (
         lambda a, b, c: (a, adjoint(1, 14, 7, c, y2, b, mask), c),
         lambda a, b, c: (adjoint(2, 13, 6, b, y1, a, mask), b, c),
+        lambda a, b, c: edge_terms(y0, y1, y2, a, b, c, mask, twin, other),
     )
     x, y, held = sum_along(pay, twin, stages, (f1, f2, f3))
     scale = 1.0 / (2.0 * size * obs_cells.shape[1] * obs_cells.shape[2])
-    gradient, misfit = finish(y0, y1, y2, *held, mask, twin.reshape(-1), other.reshape(-1), x, y, scale)
+    gradient, misfit = finish(y0, held[0], held[3], x, y, scale)
     misfit = misfit.reshape(1)
     return gradient, misfit
 

time: 48.4 us -> 47.1 us (0.973); the launches traced: 48.4 us -> 46.5 us
  waiting for transfers between devices: 2.13 us -> 0.58 us
  Pallas kernels: 30.7 us -> 29.9 us
    ppermute x3, starting transfers between devices: 8.73 us -> 10.3 us  [sum_along(): other = lax.ppermute(x, 'along', [(p, p ^ steps[i]) for p in range(size)])]
    ppermute x3, waiting for transfers between devices: 1.94 us -> 0.39 us  [sum_along(): other = lax.ppermute(x, 'along', [(p, p ^ steps[i]) for p in range(size)])]
    ppermute x1, starting transfers between devices: 4.18 us -> 3 us  [local(): twin = lax.ppermute(pay, 'along', twins)]
    pallas_call x1 -> x2, Pallas kernels: 9.45 us -> 8.49 us  [the longest x1 4.59 us: finish(): pl.pallas_call(functools.partial(finish_kernel, scale), out_shape=[jax.Sh...]
  transfers between devices with their start and end apart: 7 -> 7, of which waited for: 4 -> 3; matrix products, arithmetic and copies ran while one was open for 0% -> 0% of each run, Pallas kernels for 31% -> 40%
where the time goes in v4:
time: 47.1 us; the launch traced here: 46.5 us
  Pallas kernels  29.9 us (63%)
  starting transfers between devices  15.2 us (32%)
  between operations  0.89 us (2%)
  waiting for transfers between devices  0.58 us (1%)
    ppermute x3, starting transfers between devices, sum_along(): other = lax.ppermute(x, 'along', [(p, p ^ steps[i]) for p in range(size)])  10.3 us
    pallas_call x1, Pallas kernels, interior(): pl.pallas_call(interior_kernel, out_shape=[FIELD] * 7 + [rows, rows, jax....  10.3 us
    pallas_call x1, Pallas kernels, bands(): pl.pallas_call(bands_kernel, out_shape=[FIELD] * 6 + [MASK, jax.ShapeDtyp...  4.71 us
    pallas_call x1, Pallas kernels, finish(): pl.pallas_call(functools.partial(finish_kernel, scale), out_shape=[jax.Sh...  4.59 us
    pallas_call x1, Pallas kernels, edge_terms(): pl.pallas_call(edge_terms_kernel, out_shape=[FIELD] * 3 + [jax.ShapeDtype...  3.9 us
    ppermute x1, starting transfers between devices, local(): twin = lax.ppermute(pay, 'along', twins)  3 us
    pallas_call x2, Pallas kernels, adjoint(): pl.pallas_call(functools.partial(adjoint_kernel, first, last, unroll), ou...  2.88 us
    pallas_call x1, Pallas kernels, edges(): pl.pallas_call(edges_kernel, out_shape=[jax.ShapeDtypeStruct((CT, LV, ROW...  1.87 us
  transfers between devices with their start and end apart: 7, of which 3 were waited for; matrix products, arithmetic and copies ran while one was open for 0% of the time, Pallas kernels for 40%

profile of v4, /device:TPU:0, one launch (start us, length us, event | category | flops | bytes accessed | tf_op | source)
XLA Modules:
  0.0 46.5 jit_solution(11805114993295066090)
XLA Ops:
  0.6 1.9 %edges.1 = (f32[8,40,16,128]{3,2,1,0:T(8,128)S(1)}, f32[984,128]{1,0:T(8,128)S(1)}, f32[984,128]{1,0:T(8,128)S(1)}, f32[176,128]{1,0:T(8,128)S(1)}) custom-call(f32[40,16,1024]{2,1,0:T(8,128)} %basic.1, s32[16,1024]{1,0:T(8,128)} %land_at.1), custom_call_target="tpu_custom_call" | custom-call | bytes 6000000 | tf_op jit(solution)/shard_map/edges/pallas_call | solution.py:170
  2.5 0.5 %collective-permute-start = (f32[984,128]{1,0:T(8,128)S(1)}, f32[984,128]{1,0:T(8,128)S(1)}, u32[]{:S(2)}, u32[]{:S(2)}) collective-permute-start(f32[984,128]{1,0:T(8,128)S(1)} %get-tuple-element.68), channel_id=1, source_target_pairs={{0,1},{1,0},{2,3},{3,2},{4,5},{5,4},{6,7},{7,6},{8,9},{9,8},{10,11... | collective-permute-start | bytes 1511432 | tf_op jit(solution)/shard_map/ppermute | solution.py:643
  3.0 0.7 %collective-permute-start.1 = (f32[984,128]{1,0:T(8,128)S(1)}, f32[984,128]{1,0:T(8,128)S(1)}, u32[]{:S(2)}, u32[]{:S(2)}) collective-permute-start(f32[984,128]{1,0:T(8,128)S(1)} %get-tuple-element.69), channel_id=1, source_target_pairs={{1,2},{2,1},{3,4},{4,3},{5,6},{6,5},{7,8},{8,7},{9,10},{10,9},{11,... | collective-permute-start | bytes 1511432 | tf_op jit(solution)/shard_map/ppermute | solution.py:642
  3.7 1.6 %order.1 = (s32[3,1,512]{2,1,0:T(1,128)S(1)}, f32[3,1,512]{2,1,0:T(1,128)S(1)}, f32[3,1,512]{2,1,0:T(1,128)S(1)}, s32[1,1,512]{2,1,0:T(1,128)S(1)}, f32[1,1,512]...) custom-call(s32[3,1,512]{2,1,0:T(1,128)} %bitcast.7, s32[1,3]{1,0:T(1,128)} %count_at.1, ...), custom_call_target="tpu_custom_call" | custom-call | bytes 6000000 | tf_op jit(solution)/shard_map/order/pallas_call | solution.py:256
  5.3 10.3 %interior.1 = (f32[7040,128]{1,0:T(8,128)S(1)}, f32[7040,128]{1,0:T(8,128)S(1)}, f32[7040,128]{1,0:T(8,128)S(1)}, f32[7040,128]{1,0:T(8,128)S(1)}, f32[7040,128]...) custom-call(f32[8,40,16,128]{3,2,1,0:T(8,128)S(1)} %get-tuple-elemen, ...), custom_call_target="tpu_custom_call" | custom-call | bytes 33000000 | tf_op jit(solution)/shard_map/interior/pallas_call | solution.py:353
  15.6 0.0 collective-permute-done.twin
  15.7 0.0 collective-permute-done.1.other
  15.7 4.7 %bands.1 = (f32[7040,128]{1,0:T(8,128)S(1)}, f32[7040,128]{1,0:T(8,128)S(1)}, f32[7040,128]{1,0:T(8,128)S(1)}, f32[7040,128]{1,0:T(8,128)S(1)}, f32[7040,128]{1,...) custom-call(f32[7040,128]{1,0:T(8,128)S(1)} %get-tuple-element.55.y0, ...), custom_call_target="tpu_custom_call", output_to_operand_aliasing={{0}: (0, {}), {1}: (1, {}), {2}: (2, {}), {3}: (4, {}), {4}... | custom-call | bytes 15000000 | tf_op jit(solution)/shard_map/bands/pallas_call | solution.py:433
  20.4 3.0 %collective-permute-start.2 = (f32[40,128]{1,0:T(8,128)S(1)}, f32[40,128]{1,0:T(8,128)S(1)}, u32[]{:S(2)}, u32[]{:S(2)}) collective-permute-start(f32[40,128]{1,0:T(8,128)S(1)} %get-tuple-element.73.pay), channel_id=1, source_target_pairs={{0,1},{1,0},{2,3},{3,2},{4,5},{5,4},{6,7},{7,6},{8,9},{9,8},{10,11... | collective-permute-start | bytes 61448 | tf_op jit(solution)/shard_map/ppermute | solution.py:650
  23.4 0.7 %collective-permute-start.5 = (f32[40,128]{1,0:T(8,128)S(1)}, f32[40,128]{1,0:T(8,128)S(1)}, u32[]{:S(2)}, u32[]{:S(2)}) collective-permute-start(f32[40,128]{1,0:T(8,128)S(1)} %get-tuple-element.73.pay), channel_id=1, source_target_pairs={{1,2},{2,1},{3,4},{4,3},{5,6},{6,5},{7,8},{8,7},{9,10},{10,9},{11,... | collective-permute-start | bytes 61448 | tf_op jit(solution)/shard_map/ppermute | solution.py:649
  24.1 0.2 collective-permute-done.2.twin
  24.2 3.5 %collective-permute-start.3 = (f32[8,128]{1,0:T(8,128)S(1)}, f32[8,128]{1,0:T(8,128)S(1)}, u32[]{:S(2)}, u32[]{:S(2)}) collective-permute-start(f32[8,128]{1,0:T(8,128)S(1)} %add.3.pay), channel_id=1, source_target_pairs={{0,2},{1,3},{2,0},{3,1},{4,6},{5,7},{6,4},{7,5},{8,10},{9,11},{10,... | collective-permute-start | bytes 12296 | tf_op jit(solution)/shard_map/ppermute | solution.py:629
  27.7 1.5 %adjoint.2.src.f2i = f32[7040,128]{1,0:T(8,128)S(1)} custom-call(f32[7040,128]{1,0:T(8,128)S(1)} %get-tuple-element.88.src.f3i, f32[7040,128]{1,0:T(8,128)S(1)} %get-tuple-element.72.state.y2, f32[7040,128]{1,0:T(8,128)S(1)} %get-tuple-element.80.forcing, f32[176,128]{1,0:T(8,128)S(1)} %get-tuple-element.81.mask), custom_call_target="tpu_custom_call", output_to_operand_aliasing={{}: (2, {})} | custom-call | bytes 6000000 | tf_op jit(solution)/shard_map/adjoint/pallas_call | solution.py:457
  29.3 0.1 collective-permute-done.3.twin
  29.4 3.5 %collective-permute-start.4 = (f32[8,128]{1,0:T(8,128)S(1)}, f32[8,128]{1,0:T(8,128)S(1)}, u32[]{:S(2)}, u32[]{:S(2)}) collective-permute-start(f32[8,128]{1,0:T(8,128)S(1)} %add.4.pay), channel_id=1, source_target_pairs={{0,4},{1,5},{2,6},{3,7},{4,0},{5,1},{6,2},{7,3},{8,12},{9,13},{10,... | collective-permute-start | bytes 12296 | tf_op jit(solution)/shard_map/ppermute | solution.py:629
  32.9 1.3 %adjoint.3.f1i = f32[7040,128]{1,0:T(8,128)S(1)} custom-call(f32[7040,128]{1,0:T(8,128)S(1)} %adjoint.2.src.f2i, f32[7040,128]{1,0:T(8,128)S(1)} %get-tuple-element.71.state.y1, f32[7040,128]{1,0:T(8,128)S(1)} %get-tuple-element.84.forcing, f32[176,128]{1,0:T(8,128)S(1)} %get-tuple-element.81.mask), custom_call_target="tpu_custom_call", output_to_operand_aliasing={{}: (2, {})} | custom-call | bytes 6000000 | tf_op jit(solution)/shard_map/adjoint/pallas_call | solution.py:457
  34.2 0.2 collective-permute-done.4.twin
  34.5 3.4 %collective-permute-start.6 = (f32[8,128]{1,0:T(8,128)S(1)}, f32[8,128]{1,0:T(8,128)S(1)}, u32[]{:S(2)}, u32[]{:S(2)}) collective-permute-start(f32[8,128]{1,0:T(8,128)S(1)} %add.5.x), channel_id=1, source_target_pairs={{0,8},{1,9},{2,10},{3,11},{4,12},{5,13},{6,14},{7,15},{8,0},{9,1},... | collective-permute-start | bytes 12296 | tf_op jit(solution)/shard_map/ppermute | solution.py:629
  37.9 0.0 collective-permute-done.5.other
  37.9 3.9 %edge_terms.1 = (f32[7040,128]{1,0:T(8,128)S(1)}, f32[7040,128]{1,0:T(8,128)S(1)}, f32[7040,128]{1,0:T(8,128)S(1)}, f32[5120,128]{1,0:T(8,128)S(1)}) custom-call(f32[7040,128]{1,0:T(8,128)S(1)} %get-tuple-element.70.y0, f32[7040,128]{1,0:T(8,128)S(1)} %get-tuple-element.71.state.y1, ...), custom_call_target="tpu_custom_call", output_to_operand_aliasing={{0}: (3, {}), {1}: (4, {}), {2}: (5, {})} | custom-call | bytes 15000000 | tf_op jit(solution)/shard_map/edge_terms/pallas_call | solution.py:545
  41.8 0.0 collective-permute-done.6.y
  41.8 4.6 %finish.1 = (f32[5120,128]{1,0:T(8,128)S(1)}, f32[40,16,1024]{2,1,0:T(8,128)}, f32[1,1]{1,0:T(1,128)}) custom-call(f32[7040,128]{1,0:T(8,128)S(1)} %get-tuple-element.70.y0, f32[7040,128]{1,0:T(8,128)S(1)} %get-tuple-element.89.f1, f32[5120,128]{1,0:T(8,128)S(1)} %get-tuple-element.90.gradi, f32[8,128]{1,0:T(8,128)S(1)} %add.5.x, ...), custom_call_target="tpu_custom_call", output_to_operand_aliasing={{0}: (2, {})} | custom-call | bytes 12000000 | tf_op jit(solution)/shard_map/finish/pallas_call | solution.py:584
  (3 shorter events, 0.0 us)
Async XLA Ops:
  2.5 13.1 %collective-permute-start = (f32[984,128]{1,0:T(8,128)S(1)}, f32[984,128]{1,0:T(8,128)S(1)}, u32[]{:S(2)}, u32[]{:S(2)}) collective-permute-start(f32[984,128]{1,0:T(8,128)S(1)} %get-tuple-element.68), channel_id=1, source_target_pairs={{0,1},{1,0},{2,3},{3,2},{4,5},{5,4},{6,7},{7,6},{8,9},{9,8},{10,11... | collective-permute-start | bytes 1511432 | tf_op jit(solution)/shard_map/ppermute | solution.py:643
  3.0 12.6 %collective-permute-start.1 = (f32[984,128]{1,0:T(8,128)S(1)}, f32[984,128]{1,0:T(8,128)S(1)}, u32[]{:S(2)}, u32[]{:S(2)}) collective-permute-start(f32[984,128]{1,0:T(8,128)S(1)} %get-tuple-element.69), channel_id=1, source_target_pairs={{1,2},{2,1},{3,4},{4,3},{5,6},{6,5},{7,8},{8,7},{9,10},{10,9},{11,... | collective-permute-start | bytes 1511432 | tf_op jit(solution)/shard_map/ppermute | solution.py:642
  20.4 3.8 %collective-permute-start.2 = (f32[40,128]{1,0:T(8,128)S(1)}, f32[40,128]{1,0:T(8,128)S(1)}, u32[]{:S(2)}, u32[]{:S(2)}) collective-permute-start(f32[40,128]{1,0:T(8,128)S(1)} %get-tuple-element.73.pay), channel_id=1, source_target_pairs={{0,1},{1,0},{2,3},{3,2},{4,5},{5,4},{6,7},{7,6},{8,9},{9,8},{10,11... | collective-permute-start | bytes 61448 | tf_op jit(solution)/shard_map/ppermute | solution.py:650
  23.4 14.5 %collective-permute-start.5 = (f32[40,128]{1,0:T(8,128)S(1)}, f32[40,128]{1,0:T(8,128)S(1)}, u32[]{:S(2)}, u32[]{:S(2)}) collective-permute-start(f32[40,128]{1,0:T(8,128)S(1)} %get-tuple-element.73.pay), channel_id=1, source_target_pairs={{1,2},{2,1},{3,4},{4,3},{5,6},{6,5},{7,8},{8,7},{9,10},{10,9},{11,... | collective-permute-start | bytes 61448 | tf_op jit(solution)/shard_map/ppermute | solution.py:649
  24.2 5.2 %collective-permute-start.3 = (f32[8,128]{1,0:T(8,128)S(1)}, f32[8,128]{1,0:T(8,128)S(1)}, u32[]{:S(2)}, u32[]{:S(2)}) collective-permute-start(f32[8,128]{1,0:T(8,128)S(1)} %add.3.pay), channel_id=1, source_target_pairs={{0,2},{1,3},{2,0},{3,1},{4,6},{5,7},{6,4},{7,5},{8,10},{9,11},{10,... | collective-permute-start | bytes 12296 | tf_op jit(solution)/shard_map/ppermute | solution.py:629
  29.4 5.0 %collective-permute-start.4 = (f32[8,128]{1,0:T(8,128)S(1)}, f32[8,128]{1,0:T(8,128)S(1)}, u32[]{:S(2)}, u32[]{:S(2)}) collective-permute-start(f32[8,128]{1,0:T(8,128)S(1)} %add.4.pay), channel_id=1, source_target_pairs={{0,4},{1,5},{2,6},{3,7},{4,0},{5,1},{6,2},{7,3},{8,12},{9,13},{10,... | collective-permute-start | bytes 12296 | tf_op jit(solution)/shard_map/ppermute | solution.py:629
  34.5 7.3 %collective-permute-start.6 = (f32[8,128]{1,0:T(8,128)S(1)}, f32[8,128]{1,0:T(8,128)S(1)}, u32[]{:S(2)}, u32[]{:S(2)}) collective-permute-start(f32[8,128]{1,0:T(8,128)S(1)} %add.5.x), channel_id=1, source_target_pairs={{0,8},{1,9},{2,10},{3,11},{4,12},{5,13},{6,14},{7,15},{8,0},{9,1},... | collective-permute-start | bytes 12296 | tf_op jit(solution)/shard_map/ppermute | solution.py:629

commit v5 on v4

--- a/solution.py
+++ b/solution.py
@@ -563,39 +563,54 @@
     )(y0, y1, y2, f1, f2, f3, mask, twin, other, twin.reshape(-1), other.reshape(-1))
 
 
-def finish_kernel(scale, y0, f1, gradi, x, y, grad, out, misfit, staged, sems):
-    misfit[...] = jnp.sum(x[...] + y[...], keepdims=True) * scale
+def finish_kernel(y0, f1, gradi, grad, out, staged, sems):
     rims(0, lambda at: gradient_row(f1, y0, grad, at))
 
     def copy(c):
         return pltpu.make_async_copy(staged.at[c], out.at[:, :, pl.ds(c * LN, LN)], sems.at[c])
 
     for c in range(CT):
-        for k in range(LV):
+
+        def turn(k, _):
             for half in range(2):
                 v = grad[pl.ds(half * 8 * COL + c * LV + k, 8, stride=COL), :]
                 staged[c, k, pl.ds(half * 8, 8), :] = v
+            return 0
+
+        lax.fori_loop(0, LV, turn, 0, unroll=8)
         copy(c).start()
     for c in range(CT):
         copy(c).wait()
 
 
-def finish(y0, f1, grad, x, y, scale):
-    return pl.pallas_call(
-        functools.partial(finish_kernel, scale),
-        out_shape=[
-            jax.ShapeDtypeStruct((ROWS * COL, LN), F32),
-            jax.ShapeDtypeStruct((LV, ROWS, CT * LN), F32),
-            jax.ShapeDtypeStruct((1, 1), F32),
-        ],
-        in_specs=[VM] * 5,
-        out_specs=[VM, ANY, VM],
+def finish(y0, f1, grad):
+    return pl.pallas_call(
+        finish_kernel,
+        out_shape=[jax.ShapeDtypeStruct((ROWS * COL, LN), F32), jax.ShapeDtypeStruct((LV, ROWS, CT * LN), F32)],
+        in_specs=[VM] * 3,
+        out_specs=[VM, ANY],
         input_output_aliases={2: 0},
         scratch_shapes=[pltpu.VMEM((CT, LV, ROWS, LN), F32), pltpu.SemaphoreType.DMA((CT,))],
         compiler_params=params(8),
         cost_estimate=cost(4),
         name="finish",
-    )(y0, f1, grad, x, y)[1:]
+    )(y0, f1, grad)
+
+
+def total_kernel(scale, x, y, out):
+    out[...] = jnp.sum(x[...] + y[...], keepdims=True) * scale
+
+
+def total(x, y, scale):
+    return pl.pallas_call(
+        functools.partial(total_kernel, scale),
+        out_shape=jax.ShapeDtypeStruct((1, 1), F32),
+        in_specs=[VM, VM],
+        out_specs=VM,
+        compiler_params=params(1),
+        cost_estimate=cost(0.1),
+        name="total",
+    )(x, y).reshape(1)
 
 
 def add_kernel(first, pay, twin, out):
@@ -642,21 +657,24 @@
     other = lax.ppermute(other, "along", others)
     twin = lax.ppermute(twin, "along", twins)
     addrs, sval, lane, spots, second, tallies, codes = order(cells, obs_count, value)
-    y0, y1, y2, y3, f1, f2, f3, twice, known, sea, total = interior(staged, mask, lane, sval, addrs, spots, tallies)
+    y0, y1, y2, y3, f1, f2, f3, twice, known, sea, squares = interior(staged, mask, lane, sval, addrs, spots, tallies)
     y0, y1, y2, f1, f2, f3, mask, pay = bands(
-        y0, y1, y2, y3, f1, f2, f3, mask, twice, known, sea, total, second, codes, addrs, tallies, twin, other
+        y0, y1, y2, y3, f1, f2, f3, mask, twice, known, sea, squares, second, codes, addrs, tallies, twin, other
     )
     other = lax.ppermute(pay, "along", others)
     twin = lax.ppermute(pay, "along", twins)
+    def inner(a, b, c):
+        b = adjoint(1, 14, 7, c, y2, b, mask)
+        return adjoint(2, 13, 6, b, y1, a, mask), b, c
+
     stages = (
-        lambda a, b, c: (a, adjoint(1, 14, 7, c, y2, b, mask), c),
-        lambda a, b, c: (adjoint(2, 13, 6, b, y1, a, mask), b, c),
+        inner,
         lambda a, b, c: edge_terms(y0, y1, y2, a, b, c, mask, twin, other),
+        lambda a, b, c, g: finish(y0, a, g),
     )
     x, y, held = sum_along(pay, twin, stages, (f1, f2, f3))
-    scale = 1.0 / (2.0 * size * obs_cells.shape[1] * obs_cells.shape[2])
-    gradient, misfit = finish(y0, held[0], held[3], x, y, scale)
-    misfit = misfit.reshape(1)
+    gradient = held[1]
+    misfit = total(x, y, 1.0 / (2.0 * size * obs_cells.shape[1] * obs_cells.shape[2]))
     return gradient, misfit
 
 

time: 47.1 us -> 44.1 us (0.936); the launches traced: 46.5 us -> 44.1 us
  starting transfers between devices: 15.2 us -> 14.2 us
  Pallas kernels: 29.9 us -> 29 us
    ppermute x3, starting transfers between devices: 10.3 us -> 9.06 us  [sum_along(): other = lax.ppermute(x, 'along', [(p, p ^ steps[i]) for p in range(size)])]
    pallas_call x1 -> x2, Pallas kernels: 4.59 us -> 3.76 us  [the longest x1 3.13 us: finish(): pl.pallas_call(finish_kernel, out_shape=[jax.ShapeDtypeStruct((ROWS * COL...]
  transfers between devices with their start and end apart: 7 -> 7, of which waited for: 3 -> 1; matrix products, arithmetic and copies ran while one was open for 0% -> 0% of each run, Pallas kernels for 40% -> 50%
where the time goes in v5:
time: 44.1 us
  Pallas kernels  29 us (66%)
  starting transfers between devices  14.2 us (32%)
  between operations  0.77 us (2%)
    pallas_call x1, Pallas kernels, interior(): pl.pallas_call(interior_kernel, out_shape=[FIELD] * 7 + [rows, rows, jax....  10.3 us
    ppermute x3, starting transfers between devices, sum_along(): other = lax.ppermute(x, 'along', [(p, p ^ steps[i]) for p in range(size)])  9.06 us
    pallas_call x1, Pallas kernels, bands(): pl.pallas_call(bands_kernel, out_shape=[FIELD] * 6 + [MASK, jax.ShapeDtyp...  4.53 us
    pallas_call x1, Pallas kernels, edge_terms(): pl.pallas_call(edge_terms_kernel, out_shape=[FIELD] * 3 + [jax.ShapeDtype...  4 us
    ppermute x1, starting transfers between devices, local(): twin = lax.ppermute(pay, 'along', twins)  3.25 us
    pallas_call x1, Pallas kernels, finish(): pl.pallas_call(finish_kernel, out_shape=[jax.ShapeDtypeStruct((ROWS * COL...  3.13 us
    pallas_call x2, Pallas kernels, adjoint(): pl.pallas_call(functools.partial(adjoint_kernel, first, last, unroll), ou...  2.88 us
    pallas_call x1, Pallas kernels, edges(): pl.pallas_call(edges_kernel, out_shape=[jax.ShapeDtypeStruct((CT, LV, ROW...  1.87 us
  transfers between devices with their start and end apart: 7, of which 1 were waited for; matrix products, arithmetic and copies ran while one was open for 0% of the time, Pallas kernels for 50%

profile of v5, /device:TPU:0, one launch (start us, length us, event | category | flops | bytes accessed | tf_op | source)
XLA Modules:
  0.0 44.1 jit_solution(3885321731092208122)
XLA Ops:
  0.6 1.9 %edges.1 = (f32[8,40,16,128]{3,2,1,0:T(8,128)S(1)}, f32[984,128]{1,0:T(8,128)S(1)}, f32[984,128]{1,0:T(8,128)S(1)}, f32[176,128]{1,0:T(8,128)S(1)}) custom-call(f32[40,16,1024]{2,1,0:T(8,128)} %basic.1, s32[16,1024]{1,0:T(8,128)} %land_at.1), custom_call_target="tpu_custom_call" | custom-call | bytes 6000000 | tf_op jit(solution)/shard_map/edges/pallas_call | solution.py:170
  2.5 0.5 %collective-permute-start = (f32[984,128]{1,0:T(8,128)S(1)}, f32[984,128]{1,0:T(8,128)S(1)}, u32[]{:S(2)}, u32[]{:S(2)}) collective-permute-start(f32[984,128]{1,0:T(8,128)S(1)} %get-tuple-element.66), channel_id=1, source_target_pairs={{0,1},{1,0},{2,3},{3,2},{4,5},{5,4},{6,7},{7,6},{8,9},{9,8},{10,11... | collective-permute-start | bytes 1511432 | tf_op jit(solution)/shard_map/ppermute | solution.py:658
  3.0 0.7 %collective-permute-start.1 = (f32[984,128]{1,0:T(8,128)S(1)}, f32[984,128]{1,0:T(8,128)S(1)}, u32[]{:S(2)}, u32[]{:S(2)}) collective-permute-start(f32[984,128]{1,0:T(8,128)S(1)} %get-tuple-element.67), channel_id=1, source_target_pairs={{1,2},{2,1},{3,4},{4,3},{5,6},{6,5},{7,8},{8,7},{9,10},{10,9},{11,... | collective-permute-start | bytes 1511432 | tf_op jit(solution)/shard_map/ppermute | solution.py:657
  3.7 1.6 %order.1 = (s32[3,1,512]{2,1,0:T(1,128)S(1)}, f32[3,1,512]{2,1,0:T(1,128)S(1)}, f32[3,1,512]{2,1,0:T(1,128)S(1)}, s32[1,1,512]{2,1,0:T(1,128)S(1)}, f32[1,1,512]...) custom-call(s32[3,1,512]{2,1,0:T(1,128)} %bitcast.7, s32[1,3]{1,0:T(1,128)} %count_at.1, ...), custom_call_target="tpu_custom_call" | custom-call | bytes 6000000 | tf_op jit(solution)/shard_map/order/pallas_call | solution.py:256
  5.3 10.3 %interior.1 = (f32[7040,128]{1,0:T(8,128)S(1)}, f32[7040,128]{1,0:T(8,128)S(1)}, f32[7040,128]{1,0:T(8,128)S(1)}, f32[7040,128]{1,0:T(8,128)S(1)}, f32[7040,128]...) custom-call(f32[8,40,16,128]{3,2,1,0:T(8,128)S(1)} %get-tuple-elemen, ...), custom_call_target="tpu_custom_call" | custom-call | bytes 33000000 | tf_op jit(solution)/shard_map/interior/pallas_call | solution.py:353
  15.6 0.0 collective-permute-done.twin
  15.7 0.0 collective-permute-done.1.other
  15.7 4.5 %bands.1 = (f32[7040,128]{1,0:T(8,128)S(1)}, f32[7040,128]{1,0:T(8,128)S(1)}, f32[7040,128]{1,0:T(8,128)S(1)}, f32[7040,128]{1,0:T(8,128)S(1)}, f32[7040,128]{1,...) custom-call(f32[7040,128]{1,0:T(8,128)S(1)} %get-tuple-element.53.y0, ...), custom_call_target="tpu_custom_call", output_to_operand_aliasing={{0}: (0, {}), {1}: (1, {}), {2}: (2, {}), {3}: (4, {}), {4}... | custom-call | bytes 15000000 | tf_op jit(solution)/shard_map/bands/pallas_call | solution.py:433
  20.2 3.3 %collective-permute-start.2 = (f32[40,128]{1,0:T(8,128)S(1)}, f32[40,128]{1,0:T(8,128)S(1)}, u32[]{:S(2)}, u32[]{:S(2)}) collective-permute-start(f32[40,128]{1,0:T(8,128)S(1)} %get-tuple-element.69.pay), channel_id=1, source_target_pairs={{0,1},{1,0},{2,3},{3,2},{4,5},{5,4},{6,7},{7,6},{8,9},{9,8},{10,11... | collective-permute-start | bytes 61448 | tf_op jit(solution)/shard_map/ppermute | solution.py:665
  23.5 0.7 %collective-permute-start.5 = (f32[40,128]{1,0:T(8,128)S(1)}, f32[40,128]{1,0:T(8,128)S(1)}, u32[]{:S(2)}, u32[]{:S(2)}) collective-permute-start(f32[40,128]{1,0:T(8,128)S(1)} %get-tuple-element.69.pay), channel_id=1, source_target_pairs={{1,2},{2,1},{3,4},{4,3},{5,6},{6,5},{7,8},{8,7},{9,10},{10,9},{11,... | collective-permute-start | bytes 61448 | tf_op jit(solution)/shard_map/ppermute | solution.py:664
  24.1 0.2 collective-permute-done.2.twin
  24.3 2.8 %collective-permute-start.3 = (f32[8,128]{1,0:T(8,128)S(1)}, f32[8,128]{1,0:T(8,128)S(1)}, u32[]{:S(2)}, u32[]{:S(2)}) collective-permute-start(f32[8,128]{1,0:T(8,128)S(1)} %add.3.pay), channel_id=1, source_target_pairs={{0,2},{1,3},{2,0},{3,1},{4,6},{5,7},{6,4},{7,5},{8,10},{9,11},{10,... | collective-permute-start | bytes 12296 | tf_op jit(solution)/shard_map/ppermute | solution.py:644
  27.1 1.5 %adjoint.2.src.f2i = f32[7040,128]{1,0:T(8,128)S(1)} custom-call(f32[7040,128]{1,0:T(8,128)S(1)} %get-tuple-element.83.src.f3i, f32[7040,128]{1,0:T(8,128)S(1)} %get-tuple-element.75.state.y2, f32[7040,128]{1,0:T(8,128)S(1)} %get-tuple-element.76.forcing, f32[176,128]{1,0:T(8,128)S(1)} %get-tuple-element.77.mask), custom_call_target="tpu_custom_call", output_to_operand_aliasing={{}: (2, {})} | custom-call | bytes 6000000 | tf_op jit(solution)/shard_map/adjoint/pallas_call | solution.py:457
  28.7 1.3 %adjoint.3.f1i = f32[7040,128]{1,0:T(8,128)S(1)} custom-call(f32[7040,128]{1,0:T(8,128)S(1)} %adjoint.2.src.f2i, f32[7040,128]{1,0:T(8,128)S(1)} %get-tuple-element.78.state.y1, f32[7040,128]{1,0:T(8,128)S(1)} %get-tuple-element.79.forcing, f32[176,128]{1,0:T(8,128)S(1)} %get-tuple-element.77.mask), custom_call_target="tpu_custom_call", output_to_operand_aliasing={{}: (2, {})} | custom-call | bytes 6000000 | tf_op jit(solution)/shard_map/adjoint/pallas_call | solution.py:457
  30.0 0.0 collective-permute-done.3.twin
  30.0 2.4 %collective-permute-start.4 = (f32[8,128]{1,0:T(8,128)S(1)}, f32[8,128]{1,0:T(8,128)S(1)}, u32[]{:S(2)}, u32[]{:S(2)}) collective-permute-start(f32[8,128]{1,0:T(8,128)S(1)} %add.4.pay), channel_id=1, source_target_pairs={{0,4},{1,5},{2,6},{3,7},{4,0},{5,1},{6,2},{7,3},{8,12},{9,13},{10,... | collective-permute-start | bytes 12296 | tf_op jit(solution)/shard_map/ppermute | solution.py:644
  32.5 0.0 collective-permute-done.5.other
  32.5 4.0 %edge_terms.1 = (f32[7040,128]{1,0:T(8,128)S(1)}, f32[7040,128]{1,0:T(8,128)S(1)}, f32[7040,128]{1,0:T(8,128)S(1)}, f32[5120,128]{1,0:T(8,128)S(1)}) custom-call(f32[7040,128]{1,0:T(8,128)S(1)} %get-tuple-element.68.y0, f32[7040,128]{1,0:T(8,128)S(1)} %get-tuple-element.78.state.y1, ...), custom_call_target="tpu_custom_call", output_to_operand_aliasing={{0}: (3, {}), {1}: (4, {}), {2}: (5, {})} | custom-call | bytes 15000000 | tf_op jit(solution)/shard_map/edge_terms/pallas_call | solution.py:545
  36.5 0.0 collective-permute-done.4.twin
  36.5 3.8 %collective-permute-start.6 = (f32[8,128]{1,0:T(8,128)S(1)}, f32[8,128]{1,0:T(8,128)S(1)}, u32[]{:S(2)}, u32[]{:S(2)}) collective-permute-start(f32[8,128]{1,0:T(8,128)S(1)} %add.5.x), channel_id=1, source_target_pairs={{0,8},{1,9},{2,10},{3,11},{4,12},{5,13},{6,14},{7,15},{8,0},{9,1},... | collective-permute-start | bytes 12296 | tf_op jit(solution)/shard_map/ppermute | solution.py:644
  40.3 3.1 %finish.1 = (f32[5120,128]{1,0:T(8,128)S(1)}, f32[40,16,1024]{2,1,0:T(8,128)}) custom-call(f32[7040,128]{1,0:T(8,128)S(1)} %get-tuple-element.68.y0, f32[7040,128]{1,0:T(8,128)S(1)} %get-tuple-element.86.f1, f32[5120,128]{1,0:T(8,128)S(1)} %get-tuple-element.87.gradi), custom_call_target="tpu_custom_call", output_to_operand_aliasing={{0}: (2, {})} | custom-call | bytes 12000000 | tf_op jit(solution)/shard_map/finish/pallas_call | solution.py:587
  43.5 0.0 collective-permute-done.6.y
  43.5 0.6 %total.1 = f32[1,1]{1,0:T(1,128)} custom-call(f32[8,128]{1,0:T(8,128)S(1)} %add.5.x, f32[8,128]{1,0:T(8,128)S(1)} %collective-permute-done.6.y), custom_call_target="tpu_custom_call" | custom-call | bytes 300000 | tf_op jit(solution)/shard_map/total/pallas_call | solution.py:605
  (3 shorter events, 0.0 us)
Async XLA Ops:
  2.5 13.1 %collective-permute-start = (f32[984,128]{1,0:T(8,128)S(1)}, f32[984,128]{1,0:T(8,128)S(1)}, u32[]{:S(2)}, u32[]{:S(2)}) collective-permute-start(f32[984,128]{1,0:T(8,128)S(1)} %get-tuple-element.66), channel_id=1, source_target_pairs={{0,1},{1,0},{2,3},{3,2},{4,5},{5,4},{6,7},{7,6},{8,9},{9,8},{10,11... | collective-permute-start | bytes 1511432 | tf_op jit(solution)/shard_map/ppermute | solution.py:658
  3.0 12.6 %collective-permute-start.1 = (f32[984,128]{1,0:T(8,128)S(1)}, f32[984,128]{1,0:T(8,128)S(1)}, u32[]{:S(2)}, u32[]{:S(2)}) collective-permute-start(f32[984,128]{1,0:T(8,128)S(1)} %get-tuple-element.67), channel_id=1, source_target_pairs={{1,2},{2,1},{3,4},{4,3},{5,6},{6,5},{7,8},{8,7},{9,10},{10,9},{11,... | collective-permute-start | bytes 1511432 | tf_op jit(solution)/shard_map/ppermute | solution.py:657
  20.2 4.1 %collective-permute-start.2 = (f32[40,128]{1,0:T(8,128)S(1)}, f32[40,128]{1,0:T(8,128)S(1)}, u32[]{:S(2)}, u32[]{:S(2)}) collective-permute-start(f32[40,128]{1,0:T(8,128)S(1)} %get-tuple-element.69.pay), channel_id=1, source_target_pairs={{0,1},{1,0},{2,3},{3,2},{4,5},{5,4},{6,7},{7,6},{8,9},{9,8},{10,11... | collective-permute-start | bytes 61448 | tf_op jit(solution)/shard_map/ppermute | solution.py:665
  23.5 9.0 %collective-permute-start.5 = (f32[40,128]{1,0:T(8,128)S(1)}, f32[40,128]{1,0:T(8,128)S(1)}, u32[]{:S(2)}, u32[]{:S(2)}) collective-permute-start(f32[40,128]{1,0:T(8,128)S(1)} %get-tuple-element.69.pay), channel_id=1, source_target_pairs={{1,2},{2,1},{3,4},{4,3},{5,6},{6,5},{7,8},{8,7},{9,10},{10,9},{11,... | collective-permute-start | bytes 61448 | tf_op jit(solution)/shard_map/ppermute | solution.py:664
  24.3 5.7 %collective-permute-start.3 = (f32[8,128]{1,0:T(8,128)S(1)}, f32[8,128]{1,0:T(8,128)S(1)}, u32[]{:S(2)}, u32[]{:S(2)}) collective-permute-start(f32[8,128]{1,0:T(8,128)S(1)} %add.3.pay), channel_id=1, source_target_pairs={{0,2},{1,3},{2,0},{3,1},{4,6},{5,7},{6,4},{7,5},{8,10},{9,11},{10,... | collective-permute-start | bytes 12296 | tf_op jit(solution)/shard_map/ppermute | solution.py:644
  30.0 6.4 %collective-permute-start.4 = (f32[8,128]{1,0:T(8,128)S(1)}, f32[8,128]{1,0:T(8,128)S(1)}, u32[]{:S(2)}, u32[]{:S(2)}) collective-permute-start(f32[8,128]{1,0:T(8,128)S(1)} %add.4.pay), channel_id=1, source_target_pairs={{0,4},{1,5},{2,6},{3,7},{4,0},{5,1},{6,2},{7,3},{8,12},{9,13},{10,... | collective-permute-start | bytes 12296 | tf_op jit(solution)/shard_map/ppermute | solution.py:644
  36.5 7.0 %collective-permute-start.6 = (f32[8,128]{1,0:T(8,128)S(1)}, f32[8,128]{1,0:T(8,128)S(1)}, u32[]{:S(2)}, u32[]{:S(2)}) collective-permute-start(f32[8,128]{1,0:T(8,128)S(1)} %add.5.x), channel_id=1, source_target_pairs={{0,8},{1,9},{2,10},{3,11},{4,12},{5,13},{6,14},{7,15},{8,0},{9,1},... | collective-permute-start | bytes 12296 | tf_op jit(solution)/shard_map/ppermute | solution.py:644

commit v6 on v5

--- a/solution.py
+++ b/solution.py
@@ -270,12 +270,8 @@
     )(*(pltpu.with_memory_space_constraint(x, pltpu.HBM) for x in (cells, count, value)))
 
 
-def upright(line):
-    return jnp.broadcast_to(line, (LN, LN)).T
-
-
 def interior_kernel(staged, mask, lane, sval, addrs, spots, tallies, y0, y1, y2, y3, f1, f2, f3, twice, known, sea, total,
-                    g1, g2, g3, terms, at_ref, spot_ref, n_ref, sems):
+                    g1, g2, g3, terms, lying, at_ref, spot_ref, n_ref, sems):
     fetches = [Fetch(addrs, at_ref, sems), Fetch(spots, spot_ref, sems.at[pl.ds(NT, 1)]), Fetch(tallies, n_ref, sems.at[pl.ds(NT + 1, 1)])]
     for fetch in fetches:
         fetch.start()
@@ -319,15 +315,22 @@
 
     lax.fori_loop(0, CAP // 8, gather, 0)
     ups, downs = tally_of(n_ref)
+    for t in range(NT):
+        for q in range(CAP // LN):
+            part = pl.ds(q * LN, LN)
+            lying[pl.ds(4 * t + q, 1), :] = lane[t, :, part]
+            lying[pl.ds(12 + 4 * t + q, 1), :] = sval[t, :, part]
+    lying[pl.ds(24, LN - 24), :] = jnp.zeros((LN - 24, LN), F32)
+    uprights = lying[...].T
     ids = lax.broadcasted_iota(I32, (LN, LN), 1).astype(F32)
     slot = lax.broadcasted_iota(I32, (LN, LN), 0)
     acc = zero
     for t, g in enumerate((g1, g2, g3)):
         for q in range(CAP // LN):
             part = pl.ds(q * LN, LN)
-            hit = upright(lane[t, :, part]) == ids
+            hit = jnp.broadcast_to(uprights[:, 4 * t + q : 4 * t + q + 1], (LN, LN)) == ids
             rows = pl.ds(t * CAP + q * LN, LN)
-            two, have = jnp.where(hit, 2.0, 0.0), jnp.where(hit, upright(sval[t, :, part]), 0.0)
+            two, have = jnp.where(hit, 2.0, 0.0), jnp.where(hit, jnp.broadcast_to(uprights[:, 12 + 4 * t + q : 13 + 4 * t + q], (LN, LN)), 0.0)
             twice[rows, :] = two
             known[rows, :] = have
             early = jnp.logical_and(slot + q * LN >= ups[t], slot + q * LN < CAP - downs[t])
@@ -360,6 +363,7 @@
             few,
             few,
             pltpu.VMEM((NT * CAP, LN), F32),
+            pltpu.VMEM((LN, LN), F32),
             pltpu.SMEM((NT * CAP,), I32),
             pltpu.SMEM((CAP,), I32),
             pltpu.SMEM((LN,), F32),
@@ -391,12 +395,12 @@
     ups, downs = tally_of(n_ref)
     most = 0
     for t in range(NT):
-        most = jnp.maximum(most, (jnp.maximum(ups[t], downs[t]) + t) // (t + 1))
+        most = jnp.maximum(most, (jnp.maximum(ups[t], downs[t]) + 2 * t + 1) // (2 * t + 2))
 
     def item(i, acc):
         for t, (y, f) in ((2, (y3, f3)), (1, (y2, f2)), (0, (y1, f1))):
-            for u in range(t + 1):
-                j = i * (t + 1) + u
+            for u in range(2 * t + 2):
+                j = i * (2 * t + 2) + u
                 near = jnp.minimum(j, CAP - 1)
                 for n, slot in ((ups[t], near), (downs[t], CAP - 1 - near)):
                     ok = j < n
@@ -516,12 +520,12 @@
     most = 0
     for t in range(NT):
         n = jnp.maximum(a_ref[counts + NT + t].astype(I32), b_ref[counts + t].astype(I32))
-        most = jnp.maximum(most, (n + t) // (t + 1))
+        most = jnp.maximum(most, (n + 2 * t + 1) // (2 * t + 2))
 
     def item(i, _):
         for t, f in ((2, f3), (1, f2), (0, f1)):
-            for u in range(t + 1):
-                near = jnp.minimum(i * (t + 1) + u, CAP - 1)
+            for u in range(2 * t + 2):
+                near = jnp.minimum(i * (2 * t + 2) + u, CAP - 1)
                 for ref, slot_at, first, side in ((a_ref, CAP - 1 - near, 0, ca), (b_ref, near, SIDE, cb)):
                     at = t * CAP + slot_at
                     hit = slot == line_ref[first + LANES + at]

time: 44.1 us -> 43.9 us (level)
  starting transfers between devices: 14.2 us -> 13.1 us
  Pallas kernels: 29 us -> 29.7 us
    ppermute x3, starting transfers between devices: 9.06 us -> 7.23 us  [sum_along(): other = lax.ppermute(x, 'along', [(p, p ^ steps[i]) for p in range(size)])]
    ppermute x1, starting transfers between devices: 3.25 us -> 4.05 us  [local(): twin = lax.ppermute(pay, 'along', twins)]
    pallas_call x1, Pallas kernels: 4 us -> 4.63 us  [edge_terms(): pl.pallas_call(edge_terms_kernel, out_shape=[FIELD] * 3 + [jax.ShapeDtype...]
  transfers between devices with their start and end apart: 7 -> 7, of which waited for: 1 -> 1; matrix products, arithmetic and copies ran while one was open for 0% -> 0% of each run, Pallas kernels for 50% -> 52%
where the time goes in v6:
time: 43.9 us; the launch traced here: 43.8 us
  Pallas kernels  29.7 us (68%)
  starting transfers between devices  13.1 us (30%)
  between operations  0.77 us (2%)
    pallas_call x1, Pallas kernels, interior(): pl.pallas_call(interior_kernel, out_shape=[FIELD] * 7 + [rows, rows, jax....  10.5 us
    ppermute x3, starting transfers between devices, sum_along(): other = lax.ppermute(x, 'along', [(p, p ^ steps[i]) for p in range(size)])  7.23 us
    pallas_call x1, Pallas kernels, edge_terms(): pl.pallas_call(edge_terms_kernel, out_shape=[FIELD] * 3 + [jax.ShapeDtype...  4.63 us
    pallas_call x1, Pallas kernels, bands(): pl.pallas_call(bands_kernel, out_shape=[FIELD] * 6 + [MASK, jax.ShapeDtyp...  4.49 us
    ppermute x1, starting transfers between devices, local(): twin = lax.ppermute(pay, 'along', twins)  4.05 us
    pallas_call x1, Pallas kernels, finish(): pl.pallas_call(finish_kernel, out_shape=[jax.ShapeDtypeStruct((ROWS * COL...  3.13 us
    pallas_call x2, Pallas kernels, adjoint(): pl.pallas_call(functools.partial(adjoint_kernel, first, last, unroll), ou...  2.88 us
    pallas_call x1, Pallas kernels, edges(): pl.pallas_call(edges_kernel, out_shape=[jax.ShapeDtypeStruct((CT, LV, ROW...  1.87 us
  transfers between devices with their start and end apart: 7, of which 1 were waited for; matrix products, arithmetic and copies ran while one was open for 0% of the time, Pallas kernels for 52%

profile of v6, /device:TPU:0, one launch (start us, length us, event | category | flops | bytes accessed | tf_op | source)
XLA Modules:
  0.0 43.8 jit_solution(7993301638535656530)
XLA Ops:
  0.6 1.9 %edges.1 = (f32[8,40,16,128]{3,2,1,0:T(8,128)S(1)}, f32[984,128]{1,0:T(8,128)S(1)}, f32[984,128]{1,0:T(8,128)S(1)}, f32[176,128]{1,0:T(8,128)S(1)}) custom-call(f32[40,16,1024]{2,1,0:T(8,128)} %basic.1, s32[16,1024]{1,0:T(8,128)} %land_at.1), custom_call_target="tpu_custom_call" | custom-call | bytes 6000000 | tf_op jit(solution)/shard_map/edges/pallas_call | solution.py:170
  2.5 0.5 %collective-permute-start = (f32[984,128]{1,0:T(8,128)S(1)}, f32[984,128]{1,0:T(8,128)S(1)}, u32[]{:S(2)}, u32[]{:S(2)}) collective-permute-start(f32[984,128]{1,0:T(8,128)S(1)} %get-tuple-element.66), channel_id=1, source_target_pairs={{0,1},{1,0},{2,3},{3,2},{4,5},{5,4},{6,7},{7,6},{8,9},{9,8},{10,11... | collective-permute-start | bytes 1511432 | tf_op jit(solution)/shard_map/ppermute | solution.py:662
  3.0 0.7 %collective-permute-start.1 = (f32[984,128]{1,0:T(8,128)S(1)}, f32[984,128]{1,0:T(8,128)S(1)}, u32[]{:S(2)}, u32[]{:S(2)}) collective-permute-start(f32[984,128]{1,0:T(8,128)S(1)} %get-tuple-element.67), channel_id=1, source_target_pairs={{1,2},{2,1},{3,4},{4,3},{5,6},{6,5},{7,8},{8,7},{9,10},{10,9},{11,... | collective-permute-start | bytes 1511432 | tf_op jit(solution)/shard_map/ppermute | solution.py:661
  3.7 1.6 %order.1 = (s32[3,1,512]{2,1,0:T(1,128)S(1)}, f32[3,1,512]{2,1,0:T(1,128)S(1)}, f32[3,1,512]{2,1,0:T(1,128)S(1)}, s32[1,1,512]{2,1,0:T(1,128)S(1)}, f32[1,1,512]...) custom-call(s32[3,1,512]{2,1,0:T(1,128)} %bitcast.7, s32[1,3]{1,0:T(1,128)} %count_at.1, ...), custom_call_target="tpu_custom_call" | custom-call | bytes 6000000 | tf_op jit(solution)/shard_map/order/pallas_call | solution.py:256
  5.3 10.5 %interior.1 = (f32[7040,128]{1,0:T(8,128)S(1)}, f32[7040,128]{1,0:T(8,128)S(1)}, f32[7040,128]{1,0:T(8,128)S(1)}, f32[7040,128]{1,0:T(8,128)S(1)}, f32[7040,128]...) custom-call(f32[8,40,16,128]{3,2,1,0:T(8,128)S(1)} %get-tuple-elemen, ...), custom_call_target="tpu_custom_call" | custom-call | bytes 33000000 | tf_op jit(solution)/shard_map/interior/pallas_call | solution.py:356
  15.8 0.0 collective-permute-done.twin
  15.8 0.0 collective-permute-done.1.other
  15.8 4.5 %bands.1 = (f32[7040,128]{1,0:T(8,128)S(1)}, f32[7040,128]{1,0:T(8,128)S(1)}, f32[7040,128]{1,0:T(8,128)S(1)}, f32[7040,128]{1,0:T(8,128)S(1)}, f32[7040,128]{1,...) custom-call(f32[7040,128]{1,0:T(8,128)S(1)} %get-tuple-element.53.y0, ...), custom_call_target="tpu_custom_call", output_to_operand_aliasing={{0}: (0, {}), {1}: (1, {}), {2}: (2, {}), {3}: (4, {}), {4}... | custom-call | bytes 15000000 | tf_op jit(solution)/shard_map/bands/pallas_call | solution.py:437
  20.3 4.0 %collective-permute-start.2 = (f32[40,128]{1,0:T(8,128)S(1)}, f32[40,128]{1,0:T(8,128)S(1)}, u32[]{:S(2)}, u32[]{:S(2)}) collective-permute-start(f32[40,128]{1,0:T(8,128)S(1)} %get-tuple-element.69.pay), channel_id=1, source_target_pairs={{0,1},{1,0},{2,3},{3,2},{4,5},{5,4},{6,7},{7,6},{8,9},{9,8},{10,11... | collective-permute-start | bytes 61448 | tf_op jit(solution)/shard_map/ppermute | solution.py:669
  24.4 0.7 %collective-permute-start.5 = (f32[40,128]{1,0:T(8,128)S(1)}, f32[40,128]{1,0:T(8,128)S(1)}, u32[]{:S(2)}, u32[]{:S(2)}) collective-permute-start(f32[40,128]{1,0:T(8,128)S(1)} %get-tuple-element.69.pay), channel_id=1, source_target_pairs={{1,2},{2,1},{3,4},{4,3},{5,6},{6,5},{7,8},{8,7},{9,10},{10,9},{11,... | collective-permute-start | bytes 61448 | tf_op jit(solution)/shard_map/ppermute | solution.py:668
  25.0 0.2 collective-permute-done.2.twin
  25.2 2.8 %collective-permute-start.3 = (f32[8,128]{1,0:T(8,128)S(1)}, f32[8,128]{1,0:T(8,128)S(1)}, u32[]{:S(2)}, u32[]{:S(2)}) collective-permute-start(f32[8,128]{1,0:T(8,128)S(1)} %add.3.pay), channel_id=1, source_target_pairs={{0,2},{1,3},{2,0},{3,1},{4,6},{5,7},{6,4},{7,5},{8,10},{9,11},{10,... | collective-permute-start | bytes 12296 | tf_op jit(solution)/shard_map/ppermute | solution.py:648
  28.0 1.5 %adjoint.2.src.f2i = f32[7040,128]{1,0:T(8,128)S(1)} custom-call(f32[7040,128]{1,0:T(8,128)S(1)} %get-tuple-element.83.src.f3i, f32[7040,128]{1,0:T(8,128)S(1)} %get-tuple-element.75.state.y2, f32[7040,128]{1,0:T(8,128)S(1)} %get-tuple-element.76.forcing, f32[176,128]{1,0:T(8,128)S(1)} %get-tuple-element.77.mask), custom_call_target="tpu_custom_call", output_to_operand_aliasing={{}: (2, {})} | custom-call | bytes 6000000 | tf_op jit(solution)/shard_map/adjoint/pallas_call | solution.py:461
  29.6 1.3 %adjoint.3.f1i = f32[7040,128]{1,0:T(8,128)S(1)} custom-call(f32[7040,128]{1,0:T(8,128)S(1)} %adjoint.2.src.f2i, f32[7040,128]{1,0:T(8,128)S(1)} %get-tuple-element.78.state.y1, f32[7040,128]{1,0:T(8,128)S(1)} %get-tuple-element.79.forcing, f32[176,128]{1,0:T(8,128)S(1)} %get-tuple-element.77.mask), custom_call_target="tpu_custom_call", output_to_operand_aliasing={{}: (2, {})} | custom-call | bytes 6000000 | tf_op jit(solution)/shard_map/adjoint/pallas_call | solution.py:461
  30.9 0.0 collective-permute-done.3.twin
  31.0 1.9 %collective-permute-start.4 = (f32[8,128]{1,0:T(8,128)S(1)}, f32[8,128]{1,0:T(8,128)S(1)}, u32[]{:S(2)}, u32[]{:S(2)}) collective-permute-start(f32[8,128]{1,0:T(8,128)S(1)} %add.4.pay), channel_id=1, source_target_pairs={{0,4},{1,5},{2,6},{3,7},{4,0},{5,1},{6,2},{7,3},{8,12},{9,13},{10,... | collective-permute-start | bytes 12296 | tf_op jit(solution)/shard_map/ppermute | solution.py:648
  32.9 0.0 collective-permute-done.5.other
  32.9 4.6 %edge_terms.1 = (f32[7040,128]{1,0:T(8,128)S(1)}, f32[7040,128]{1,0:T(8,128)S(1)}, f32[7040,128]{1,0:T(8,128)S(1)}, f32[5120,128]{1,0:T(8,128)S(1)}) custom-call(f32[7040,128]{1,0:T(8,128)S(1)} %get-tuple-element.68.y0, f32[7040,128]{1,0:T(8,128)S(1)} %get-tuple-element.78.state.y1, ...), custom_call_target="tpu_custom_call", output_to_operand_aliasing={{0}: (3, {}), {1}: (4, {}), {2}: (5, {})} | custom-call | bytes 15000000 | tf_op jit(solution)/shard_map/edge_terms/pallas_call | solution.py:549
  37.5 0.0 collective-permute-done.4.twin
  37.5 2.5 %collective-permute-start.6 = (f32[8,128]{1,0:T(8,128)S(1)}, f32[8,128]{1,0:T(8,128)S(1)}, u32[]{:S(2)}, u32[]{:S(2)}) collective-permute-start(f32[8,128]{1,0:T(8,128)S(1)} %add.5.x), channel_id=1, source_target_pairs={{0,8},{1,9},{2,10},{3,11},{4,12},{5,13},{6,14},{7,15},{8,0},{9,1},... | collective-permute-start | bytes 12296 | tf_op jit(solution)/shard_map/ppermute | solution.py:648
  40.0 3.1 %finish.1 = (f32[5120,128]{1,0:T(8,128)S(1)}, f32[40,16,1024]{2,1,0:T(8,128)}) custom-call(f32[7040,128]{1,0:T(8,128)S(1)} %get-tuple-element.68.y0, f32[7040,128]{1,0:T(8,128)S(1)} %get-tuple-element.86.f1, f32[5120,128]{1,0:T(8,128)S(1)} %get-tuple-element.87.gradi), custom_call_target="tpu_custom_call", output_to_operand_aliasing={{0}: (2, {})} | custom-call | bytes 12000000 | tf_op jit(solution)/shard_map/finish/pallas_call | solution.py:591
  43.2 0.0 collective-permute-done.6.y
  43.2 0.6 %total.1 = f32[1,1]{1,0:T(1,128)} custom-call(f32[8,128]{1,0:T(8,128)S(1)} %add.5.x, f32[8,128]{1,0:T(8,128)S(1)} %collective-permute-done.6.y), custom_call_target="tpu_custom_call" | custom-call | bytes 300000 | tf_op jit(solution)/shard_map/total/pallas_call | solution.py:609
  (3 shorter events, 0.0 us)
Async XLA Ops:
  2.5 13.3 %collective-permute-start = (f32[984,128]{1,0:T(8,128)S(1)}, f32[984,128]{1,0:T(8,128)S(1)}, u32[]{:S(2)}, u32[]{:S(2)}) collective-permute-start(f32[984,128]{1,0:T(8,128)S(1)} %get-tuple-element.66), channel_id=1, source_target_pairs={{0,1},{1,0},{2,3},{3,2},{4,5},{5,4},{6,7},{7,6},{8,9},{9,8},{10,11... | collective-permute-start | bytes 1511432 | tf_op jit(solution)/shard_map/ppermute | solution.py:662
  3.0 12.8 %collective-permute-start.1 = (f32[984,128]{1,0:T(8,128)S(1)}, f32[984,128]{1,0:T(8,128)S(1)}, u32[]{:S(2)}, u32[]{:S(2)}) collective-permute-start(f32[984,128]{1,0:T(8,128)S(1)} %get-tuple-element.67), channel_id=1, source_target_pairs={{1,2},{2,1},{3,4},{4,3},{5,6},{6,5},{7,8},{8,7},{9,10},{10,9},{11,... | collective-permute-start | bytes 1511432 | tf_op jit(solution)/shard_map/ppermute | solution.py:661
  20.3 4.9 %collective-permute-start.2 = (f32[40,128]{1,0:T(8,128)S(1)}, f32[40,128]{1,0:T(8,128)S(1)}, u32[]{:S(2)}, u32[]{:S(2)}) collective-permute-start(f32[40,128]{1,0:T(8,128)S(1)} %get-tuple-element.69.pay), channel_id=1, source_target_pairs={{0,1},{1,0},{2,3},{3,2},{4,5},{5,4},{6,7},{7,6},{8,9},{9,8},{10,11... | collective-permute-start | bytes 61448 | tf_op jit(solution)/shard_map/ppermute | solution.py:669
  24.4 8.5 %collective-permute-start.5 = (f32[40,128]{1,0:T(8,128)S(1)}, f32[40,128]{1,0:T(8,128)S(1)}, u32[]{:S(2)}, u32[]{:S(2)}) collective-permute-start(f32[40,128]{1,0:T(8,128)S(1)} %get-tuple-element.69.pay), channel_id=1, source_target_pairs={{1,2},{2,1},{3,4},{4,3},{5,6},{6,5},{7,8},{8,7},{9,10},{10,9},{11,... | collective-permute-start | bytes 61448 | tf_op jit(solution)/shard_map/ppermute | solution.py:668
  25.2 5.7 %collective-permute-start.3 = (f32[8,128]{1,0:T(8,128)S(1)}, f32[8,128]{1,0:T(8,128)S(1)}, u32[]{:S(2)}, u32[]{:S(2)}) collective-permute-start(f32[8,128]{1,0:T(8,128)S(1)} %add.3.pay), channel_id=1, source_target_pairs={{0,2},{1,3},{2,0},{3,1},{4,6},{5,7},{6,4},{7,5},{8,10},{9,11},{10,... | collective-permute-start | bytes 12296 | tf_op jit(solution)/shard_map/ppermute | solution.py:648
  31.0 6.5 %collective-permute-start.4 = (f32[8,128]{1,0:T(8,128)S(1)}, f32[8,128]{1,0:T(8,128)S(1)}, u32[]{:S(2)}, u32[]{:S(2)}) collective-permute-start(f32[8,128]{1,0:T(8,128)S(1)} %add.4.pay), channel_id=1, source_target_pairs={{0,4},{1,5},{2,6},{3,7},{4,0},{5,1},{6,2},{7,3},{8,12},{9,13},{10,... | collective-permute-start | bytes 12296 | tf_op jit(solution)/shard_map/ppermute | solution.py:648
  37.5 5.7 %collective-permute-start.6 = (f32[8,128]{1,0:T(8,128)S(1)}, f32[8,128]{1,0:T(8,128)S(1)}, u32[]{:S(2)}, u32[]{:S(2)}) collective-permute-start(f32[8,128]{1,0:T(8,128)S(1)} %add.5.x), channel_id=1, source_target_pairs={{0,8},{1,9},{2,10},{3,11},{4,12},{5,13},{6,14},{7,15},{8,0},{9,1},... | collective-permute-start | bytes 12296 | tf_op jit(solution)/shard_map/ppermute | solution.py:648
